TPU v7x, 32 devices: a whole 2x2x4 slice. The times are simulated.
32 devices in a mesh: dp: 4 (over x, core), fsdp: 8 (over z, y).
Axes of the slice: x: 2, y: 2, z: 4, core: 2. Of those that a mesh axis runs over, the one named last changes fastest.
Arguments:
- features: bfloat16 [12288, 512], P(('dp', 'fsdp')), may hold values from -6 to 6
- cotangent: bfloat16 [12288, 512], P(('dp', 'fsdp')), may hold values from -6 to 6
- lengths: int32 [32, 4], P(('dp', 'fsdp')), may hold values from 0 to 384, as said below
- front_up: bfloat16 [512, 2048], P(('dp', 'fsdp')), may hold values from -0.25 to 0.25
- front_down: bfloat16 [2048, 512], P(('dp', 'fsdp')), may hold values from -0.125 to 0.125
- heads_input: bfloat16 [512, 1536], P(('dp', 'fsdp')), may hold values from -0.25 to 0.25
- heads_output: bfloat16 [512, 512], P(('dp', 'fsdp')), may hold values from -3 to 3
- gated_input: bfloat16 [512, 3072], P(('dp', 'fsdp')), may hold values from -0.25 to 0.25
- gated_output: bfloat16 [1536, 512], P(('dp', 'fsdp')), may hold values from -0.15625 to 0.15625
- merge_output: bfloat16 [1024, 512], P(('dp', 'fsdp')), may hold values from -0.1875 to 0.1875
- rear_up: bfloat16 [512, 2048], P(('dp', 'fsdp')), may hold values from -0.25 to 0.25
- rear_down: bfloat16 [2048, 512], P(('dp', 'fsdp')), may hold values from -0.125 to 0.125
- gate_kernel: bfloat16 [31, 1536], P(None, ('dp', 'fsdp')), may hold values from -1 to 1
- merge_kernel: bfloat16 [31, 1024], P(None, ('dp', 'fsdp')), may hold values from -1 to 1
- front_gain: bfloat16 [512], P(('dp', 'fsdp')), may hold values from 0.25 to 1.75
- heads_gain: bfloat16 [512], P(('dp', 'fsdp')), may hold values from 0.25 to 1.75
- gated_gain: bfloat16 [512], P(('dp', 'fsdp')), may hold values from 0.25 to 1.75
- gate_gain: bfloat16 [1536], P(('dp', 'fsdp')), may hold values from 0.25 to 1.75
- rear_gain: bfloat16 [512], P(('dp', 'fsdp')), may hold values from 0.25 to 1.75
- final_gain: bfloat16 [512], P(('dp', 'fsdp')), may hold values from 0.25 to 1.75
Outputs:
- encoded: bfloat16 [12288, 512], P(('dp', 'fsdp'))
- features_grad: bfloat16 [12288, 512], P(('dp', 'fsdp'))
- front_up_grad: float32 [512, 2048], P(('dp', 'fsdp'))
- front_down_grad: float32 [2048, 512], P(('dp', 'fsdp'))
- heads_input_grad: float32 [512, 1536], P(('dp', 'fsdp'))
- heads_output_grad: float32 [512, 512], P(('dp', 'fsdp'))
- gated_input_grad: float32 [512, 3072], P(('dp', 'fsdp'))
- gated_output_grad: float32 [1536, 512], P(('dp', 'fsdp'))
- merge_output_grad: float32 [1024, 512], P(('dp', 'fsdp'))
- rear_up_grad: float32 [512, 2048], P(('dp', 'fsdp'))
- rear_down_grad: float32 [2048, 512], P(('dp', 'fsdp'))
- gate_kernel_grad: float32 [31, 1536], P(None, ('dp', 'fsdp'))
- merge_kernel_grad: float32 [31, 1024], P(None, ('dp', 'fsdp'))
- front_gain_grad: float32 [512], P(('dp', 'fsdp'))
- heads_gain_grad: float32 [512], P(('dp', 'fsdp'))
- gated_gain_grad: float32 [512], P(('dp', 'fsdp'))
- gate_gain_grad: float32 [1536], P(('dp', 'fsdp'))
- rear_gain_grad: float32 [512], P(('dp', 'fsdp'))
- final_gain_grad: float32 [512], P(('dp', 'fsdp'))
- statistics: float32 [7], replicated
Inputs may be any that keep to these rules, and one draw needn't show every extreme that they name: `lengths`: row r holds the frame counts of the utterances of the r-th block, in order from the block's start; zero counts are empty slots; a row sums to at most 384 and to at least 192; in every draw some row is one utterance of 384 frames followed by zeros.
All inputs are finite; a program needn't handle non-finite values.
Results may differ from a plain program's by a relative error of at most 0.018.
Values may be sent and summed in bfloat16 or wider, within the bound.
No kernel may reach another device: no remote copies, remote signals or barrier semaphores. Data moves between devices by JAX's collectives and lax.ppermute only.
A program may use at most 320 MiB of HBM per device.

v0:
```python
import jax
import jax.numpy as jnp
from jax import lax
from jax.sharding import PartitionSpec as P

HEADS = 8


EPSILON = 1e-05
NEGATIVE = -1000000000.0
AXES = ("dp", "fsdp")
LANE = 512


def matmul(left_side, right_side):
    return jnp.dot(left_side, right_side, preferred_element_type=jnp.float32)


def matmul_left_t(left_side, right_side):
    return lax.dot_general(
        left_side, right_side, (((0,), (0,)), ((), ())), preferred_element_type=jnp.float32
    )


def matmul_right_t(left_side, right_side):
    return lax.dot_general(
        left_side, right_side, (((1,), (1,)), ((), ())), preferred_element_type=jnp.float32
    )


def to_low(values):
    return values.astype(jnp.bfloat16)


def pack_rows(shard):
    rows, columns = shard.shape
    if columns == LANE:
        return shard
    pieces = shard.reshape(rows, columns // LANE, LANE).transpose(1, 0, 2)
    return pieces.reshape(rows * columns // LANE, LANE)


def pack_small(parts):
    flat = jnp.concatenate([part.reshape(-1) for part in parts])
    rows = -(-flat.shape[0] // LANE)
    rows = -(-rows // 16) * 16
    return jnp.pad(flat, (0, rows * LANE - flat.shape[0])).reshape(rows, LANE)


def gather_weights(matrices, smaller, count):
    packed = [pack_rows(element) for element in matrices] + [pack_small(smaller)]
    gathered = lax.all_gather(jnp.concatenate(packed), AXES, axis=0)
    weights = []
    start = 0
    for element, piece in zip(matrices, packed):
        rows, columns = element.shape
        window = gathered[:, start : start + piece.shape[0]]
        start += piece.shape[0]
        window = window.reshape(count, columns // LANE, rows, LANE).transpose(0, 2, 1, 3)
        weights.append(window.reshape(count * rows, columns))
    flat = gathered[:, start:].reshape(count, -1)
    start = 0
    for element in smaller:
        size = element.size
        window = flat[:, start : start + size].astype(jnp.float32)
        start += size
        if element.ndim == 2:
            taps, columns = element.shape
            window = window.reshape(count, taps, columns).transpose(1, 0, 2)
            weights.append(window.reshape(taps, count * columns))
        else:
            weights.append(window.reshape(-1))
    return weights


def scatter_gradients(matrices, smaller, count):
    pieces = []
    for element in matrices:
        rows, columns = element.shape
        low = element.astype(jnp.bfloat16).reshape(count, rows // count, columns // LANE, LANE)
        pieces.append(low.transpose(0, 2, 1, 3).reshape(count, -1, LANE))
    flat = []
    for element in smaller:
        if element.ndim == 2:
            taps, columns = element.shape
            flat.append(
                element.reshape(taps, count, columns // count).transpose(1, 0, 2).reshape(count, -1)
            )
        else:
            flat.append(element.reshape(count, -1))
    flat = jnp.concatenate(flat, axis=1).astype(jnp.bfloat16)
    rows = -(-flat.shape[1] // LANE)
    rows = -(-rows // 16) * 16
    flat = jnp.pad(flat, ((0, 0), (0, rows * LANE - flat.shape[1])))
    pieces.append(flat.reshape(count, rows, LANE))
    summed = lax.psum_scatter(
        jnp.concatenate(pieces, axis=1), AXES, scatter_dimension=0, tiled=False
    )
    shards = []
    start = 0
    for element in matrices:
        rows, columns = element.shape
        rows = rows // count
        size = rows * columns // LANE
        window = summed[start : start + size].astype(jnp.float32)
        start += size
        window = window.reshape(columns // LANE, rows, LANE).transpose(1, 0, 2)
        shards.append(window.reshape(rows, columns))
    flat = summed[start:].reshape(-1).astype(jnp.float32)
    start = 0
    for element in smaller:
        size = element.size // count
        window = flat[start : start + size]
        start += size
        if element.ndim == 2:
            window = window.reshape(element.shape[0], -1)
        shards.append(window)
    return tuple(shards)


def norm_forward(values, norm_gain):
    centred = values - jnp.mean(values, axis=-1, keepdims=True)
    variance = jnp.mean(centred * centred, axis=-1, keepdims=True)
    inverse = lax.rsqrt(variance + EPSILON)
    normal = centred * inverse
    return (normal * norm_gain, (normal, inverse))


def norm_backward(upstream, norm_gain, saved_state):
    normal, inverse = saved_state
    gain_grad = jnp.sum(upstream * normal, axis=0)
    scaled = upstream * norm_gain
    mean_scaled = jnp.mean(scaled, axis=-1, keepdims=True)
    mean_cross = jnp.mean(scaled * normal, axis=-1, keepdims=True)
    return (inverse * (scaled - mean_scaled - normal * mean_cross), gain_grad)


def segment_ids(length_row, row_count):
    utterance_ends = jnp.cumsum(length_row)
    position = jnp.arange(row_count, dtype=jnp.int32)
    return jnp.sum((position[None, :] >= utterance_ends[:, None]).astype(jnp.int32), axis=0)


def shifted(values, offset):
    if offset > 0:
        return jnp.concatenate(
            [values[offset:], jnp.zeros((offset,) + values.shape[1:], values.dtype)], axis=0
        )
    if offset < 0:
        return jnp.concatenate(
            [jnp.zeros((-offset,) + values.shape[1:], values.dtype), values[:offset]], axis=0
        )
    return values


def conv_masks(segments, taps):
    half_width = (taps - 1) // 2
    marked = segments + 1
    return [
        (shifted(marked, tap_index - half_width) == marked).astype(jnp.float32)[:, None]
        for tap_index in range(taps)
    ]


def segment_conv(values, kernel, tap_masks):
    half_width = (kernel.shape[0] - 1) // 2
    summed = jnp.zeros_like(values)
    for tap_index in range(kernel.shape[0]):
        summed = (
            summed
            + kernel[tap_index] * shifted(values, tap_index - half_width) * tap_masks[tap_index]
        )
    return summed


def conv_backward(upstream, values, kernel, tap_masks):
    half_width = (kernel.shape[0] - 1) // 2
    summed = jnp.zeros_like(values)
    kernel_rows = []
    for tap_index in range(kernel.shape[0]):
        offset = tap_index - half_width
        masked = upstream * tap_masks[tap_index]
        summed = summed + kernel[tap_index] * shifted(masked, -offset)
        kernel_rows.append(jnp.sum(masked * shifted(values, offset), axis=0))
    return (summed, jnp.stack(kernel_rows))


def ffn_forward(stream, up_weight, down_weight, norm_gain):
    normed, norm_state = norm_forward(stream, norm_gain)
    normed_low = to_low(normed)
    before = matmul(normed_low, up_weight)
    hidden = to_low(jax.nn.silu(before))
    return (0.5 * matmul(hidden, down_weight), (norm_state, normed_low, before, hidden))


def ffn_backward(stream_grad, up_weight, down_weight, norm_gain, saved_state):
    norm_state, normed_low, before, hidden = saved_state
    part_grad = to_low(0.5 * stream_grad)
    down_grad = matmul_left_t(hidden, part_grad)
    hidden_grad = matmul_right_t(part_grad, down_weight)
    before_grad = to_low(jax.vjp(jax.nn.silu, before)[1](hidden_grad)[0])
    up_grad = matmul_left_t(normed_low, before_grad)
    normed_grad = matmul_right_t(before_grad, up_weight)
    input_grad, gain_grad = norm_backward(normed_grad, norm_gain, norm_state)
    return (stream_grad + input_grad, up_grad, down_grad, gain_grad)


def head_scores(packed, allowed, score_scale):
    raw_scores = (
        jnp.einsum("qhd,khd->hqk", packed[:, 0], packed[:, 1], preferred_element_type=jnp.float32)
        * score_scale
    )
    return jnp.where(allowed, raw_scores, NEGATIVE)


def attention_forward(normed_low, packed_weight, output_weight, allowed):
    row_count, feature_width = normed_low.shape
    head_size = feature_width // HEADS
    score_scale = head_size ** (-0.5)
    packed = to_low(matmul(normed_low, packed_weight)).reshape(row_count, 3, HEADS, head_size)
    scores = head_scores(packed, allowed, score_scale)
    largest = jnp.max(scores, axis=-1, keepdims=True)
    exponent = jnp.exp(scores - largest)
    summed = jnp.sum(exponent, axis=-1, keepdims=True)
    probs_low = to_low(exponent / summed)
    log_total = largest + jnp.log(summed)
    mixed_low = to_low(
        jnp.einsum("hqk,khd->qhd", probs_low, packed[:, 2], preferred_element_type=jnp.float32)
    )
    mixed_low = mixed_low.reshape(row_count, feature_width)
    return (matmul(mixed_low, output_weight), (packed, log_total, mixed_low))


def attention_backward(
    attended_grad, normed_low, packed_weight, output_weight, allowed, saved_state
):
    packed, log_total, mixed_low = saved_state
    row_count, feature_width = normed_low.shape
    head_size = feature_width // HEADS
    score_scale = head_size ** (-0.5)
    attended_low = to_low(attended_grad)
    output_grad = matmul_left_t(mixed_low, attended_low)
    mixed_grad = to_low(matmul_right_t(attended_low, output_weight)).reshape(
        row_count, HEADS, head_size
    )
    probs = jnp.exp(head_scores(packed, allowed, score_scale) - log_total)
    probs_low = to_low(probs)
    probs_grad = jnp.einsum(
        "qhd,khd->hqk", mixed_grad, packed[:, 2], preferred_element_type=jnp.float32
    )
    value_grad = jnp.einsum(
        "hqk,qhd->khd", probs_low, mixed_grad, preferred_element_type=jnp.float32
    )
    inner_sum = jnp.sum(probs_grad * probs, axis=-1, keepdims=True)
    score_grad = to_low(probs * (probs_grad - inner_sum))
    query_grad = (
        jnp.einsum("hqk,khd->qhd", score_grad, packed[:, 1], preferred_element_type=jnp.float32)
        * score_scale
    )
    key_grad = (
        jnp.einsum("hqk,qhd->khd", score_grad, packed[:, 0], preferred_element_type=jnp.float32)
        * score_scale
    )
    packed_grad = to_low(
        jnp.stack([query_grad, key_grad, value_grad], axis=1).reshape(row_count, 3 * feature_width)
    )
    packed_weight_grad = matmul_left_t(normed_low, packed_grad)
    normed_grad = matmul_right_t(packed_grad, packed_weight)
    return (normed_grad, packed_weight_grad, output_grad)


def gated_forward(normed_low, input_weight, output_weight, gate_gain, gate_kernel, tap_masks):
    before = matmul(normed_low, input_weight)
    activated = jax.nn.gelu(before)
    half_width = activated.shape[1] // 2
    gate_normed, gate_state = norm_forward(activated[:, half_width:], gate_gain)
    gate_part = segment_conv(gate_normed, gate_kernel, tap_masks)
    product_low = to_low(activated[:, :half_width] * gate_part)
    return (
        matmul(product_low, output_weight),
        (before, gate_normed, gate_state, gate_part, product_low),
    )


def gated_backward(
    gated_grad,
    normed_low,
    input_weight,
    output_weight,
    gate_gain,
    gate_kernel,
    tap_masks,
    saved_state,
):
    before, gate_normed, gate_state, gate_part, product_low = saved_state
    gated_low = to_low(gated_grad)
    output_grad = matmul_left_t(product_low, gated_low)
    product_grad = matmul_right_t(gated_low, output_weight)
    activated, gelu_pull = jax.vjp(jax.nn.gelu, before)
    half_width = activated.shape[1] // 2
    linear_grad = product_grad * gate_part
    part_grad = product_grad * activated[:, :half_width]
    normed_gate_grad, kernel_grad = conv_backward(part_grad, gate_normed, gate_kernel, tap_masks)
    gate_grad, gain_grad = norm_backward(normed_gate_grad, gate_gain, gate_state)
    before_grad = to_low(gelu_pull(jnp.concatenate([linear_grad, gate_grad], axis=1))[0])
    input_grad = matmul_left_t(normed_low, before_grad)
    normed_grad = matmul_right_t(before_grad, input_weight)
    return (normed_grad, input_grad, output_grad, gain_grad, kernel_grad)


def per_device(
    features,
    cotangent,
    lengths,
    front_up,
    front_down,
    heads_input,
    heads_output,
    gated_input,
    gated_output,
    merge_output,
    rear_up,
    rear_down,
    gate_kernel,
    merge_kernel,
    front_gain,
    heads_gain,
    gated_gain,
    gate_gain,
    rear_gain,
    final_gain,
):
    count = lax.axis_size(AXES)
    matrices = (front_up, front_down, heads_input, heads_output, gated_input, gated_output, merge_output, rear_up, rear_down)
    smaller = (gate_kernel, merge_kernel, front_gain, heads_gain, gated_gain, gate_gain, rear_gain, final_gain)
    (
        w_front_up,
        w_front_down,
        w_heads_input,
        w_heads_output,
        w_gated_input,
        w_gated_output,
        w_merge_output,
        w_rear_up,
        w_rear_down,
        w_gate_kernel,
        w_merge_kernel,
        w_front_gain,
        w_heads_gain,
        w_gated_gain,
        w_gate_gain,
        w_rear_gain,
        w_final_gain,
    ) = gather_weights(matrices, smaller, count)
    row_count, feature_width = features.shape
    segments = segment_ids(lengths[0], row_count)
    valid_rows = (segments < lengths.shape[1]).astype(jnp.float32)[:, None]
    tap_masks = conv_masks(segments, w_gate_kernel.shape[0])
    allowed = (segments[:, None] == segments[None, :])[None]
    inputs = features.astype(jnp.float32)
    front_part, front_state = ffn_forward(
        inputs, w_front_up, w_front_down, w_front_gain
    )
    after_front = inputs + front_part
    heads_normed, heads_norm_state = norm_forward(after_front, w_heads_gain)
    heads_low = to_low(heads_normed)
    attended, heads_state = attention_forward(
        heads_low, w_heads_input, w_heads_output, allowed
    )
    gated_normed, gated_norm_state = norm_forward(after_front, w_gated_gain)
    gated_low = to_low(gated_normed)
    gated_out, gated_state = gated_forward(
        gated_low,
        w_gated_input,
        w_gated_output,
        w_gate_gain,
        w_gate_kernel,
        tap_masks,
    )
    joined = jnp.concatenate([attended, gated_out], axis=1)
    merged_low = to_low(joined + segment_conv(joined, w_merge_kernel, tap_masks))
    merge_part = matmul(merged_low, w_merge_output)
    after_merge = after_front + merge_part
    rear_part, rear_state = ffn_forward(
        after_merge, w_rear_up, w_rear_down, w_rear_gain
    )
    after_rear = after_merge + rear_part
    final_normed, final_state = norm_forward(after_rear, w_final_gain)
    encoded = (final_normed * valid_rows).astype(jnp.bfloat16)
    tracked = [inputs, after_front, after_merge, after_rear, front_part, merge_part, rear_part]
    squares = jnp.stack([jnp.sum(element * element * valid_rows) for element in tracked])
    totals = lax.psum((squares, jnp.sum(valid_rows)), AXES)
    statistics = jnp.sqrt(totals[0] / (totals[1] * feature_width))
    upstream = cotangent.astype(jnp.float32) * valid_rows
    rear_stream_grad, final_gain_grad = norm_backward(
        upstream, w_final_gain, final_state
    )
    merge_stream_grad, rear_up_grad, rear_down_grad, rear_gain_grad = ffn_backward(
        rear_stream_grad,
        w_rear_up,
        w_rear_down,
        w_rear_gain,
        rear_state,
    )
    merge_low_grad = to_low(merge_stream_grad)
    merge_output_grad = matmul_left_t(merged_low, merge_low_grad)
    merged_grad = matmul_right_t(merge_low_grad, w_merge_output)
    conv_grad, merge_kernel_grad = conv_backward(
        merged_grad, joined, w_merge_kernel, tap_masks
    )
    joined_grad = merged_grad + conv_grad
    heads_normed_grad, heads_input_grad, heads_output_grad = attention_backward(
        joined_grad[:, :feature_width],
        heads_low,
        w_heads_input,
        w_heads_output,
        allowed,
        heads_state,
    )
    gated_normed_grad, gated_input_grad, gated_output_grad, gate_gain_grad, gate_kernel_grad = (
        gated_backward(
            joined_grad[:, feature_width:],
            gated_low,
            w_gated_input,
            w_gated_output,
            w_gate_gain,
            w_gate_kernel,
            tap_masks,
            gated_state,
        )
    )
    heads_stream, heads_gain_grad = norm_backward(
        heads_normed_grad, w_heads_gain, heads_norm_state
    )
    gated_stream, gated_gain_grad = norm_backward(
        gated_normed_grad, w_gated_gain, gated_norm_state
    )
    front_stream_grad = merge_stream_grad + heads_stream + gated_stream
    inputs_grad, front_up_grad, front_down_grad, front_gain_grad = ffn_backward(
        front_stream_grad,
        w_front_up,
        w_front_down,
        w_front_gain,
        front_state,
    )
    shards = scatter_gradients(
        (front_up_grad, front_down_grad, heads_input_grad, heads_output_grad, gated_input_grad, gated_output_grad, merge_output_grad, rear_up_grad, rear_down_grad),
        (gate_kernel_grad, merge_kernel_grad, front_gain_grad, heads_gain_grad, gated_gain_grad, gate_gain_grad, rear_gain_grad, final_gain_grad),
        count,
    )
    return (encoded, inputs_grad.astype(jnp.bfloat16)) + tuple(shards) + (statistics,)


def solution(mesh):
    rows = P(AXES, None)
    columns = P(None, AXES)
    vector = P(AXES)
    weights = (rows,) * 9 + (columns,) * 2 + (vector,) * 6
    return jax.shard_map(
        per_device,
        mesh=mesh,
        in_specs=(rows, rows, rows) + weights,
        out_specs=(rows, rows) + weights + (P(),),
        check_vma=False,
    )
```

profile of v0, /device:TPU:0, one launch (start us, length us, event | category | flops | bytes accessed | tf_op | source)
XLA Modules:
  0.0 1229.5 jit_solution(9922335577585270984)
XLA Ops:
  25.7 113.6 %all-gather.3.cloned.1.call-done = bf16[16384,512]{1,0:T(8,128)(2,1)} async-done(((bf16[512,512]{1,0:T(8,128)(2,1)}), bf16[16384,512]{1,0:T(8,128)(2,1)}) %all-gather.3.cloned.1.call-update) | async-done | bytes 16777232 | tf_op jit(solution)/shard_map/all_gather | solution.py:52
  159.0 5.9 fusion.135
  184.5 4.3 copy.105
  190.5 4.3 multiply_multiply_fusion.2
  259.3 27.4 %multiply_convert_fusion.3 = (bf16[384,1536]{1,0:T(8,128)(2,1)S(1)}, f32[384,1536]{1,0:T(8,128)}) fusion(f32[384,3072]{1,0:T(8,128)} %copy-done.1, f32[384]{0:T(512)} %get-tuple-element.496, f32[369,1536]{1,0:T(8,128)} %get-tuple-element.303, f32[1536]{0:T(1024)} %mul.2698, f32[384]{0:T(512)} %get-tuple-element.495, f32[370,1536]{1,0:T(8,128)} %get-tuple-element.305, ...), kind=kLoop, calls=%fused_computation.138 | loop fusion | flops 56623104 | bytes 77807616 | tf_op jit(solution)/shard_map/convert_element_type | solution.py:32
  367.7 15.9 %add_convert_fusion.1 = bf16[384,1024]{1,0:T(8,128)(2,1)S(1)} fusion(f32[369,1024]{1,0:T(8,128)} %get-tuple-element.401, f32[370,1024]{1,0:T(8,128)} %get-tuple-element.403, f32[371,1024]{1,0:T(8,128)} %get-tuple-element.405, f32[372,1024]{1,0:T(8,128)} %get-tuple-element.407, f32[373,1024]{1,0:T(8,128)} %get-tuple-element.409, ...), kind=kLoop, calls=%fused_computation.193 | loop fusion | flops 36962304 | bytes 48735232 | tf_op jit(solution)/shard_map/convert_element_type | solution.py:32
  400.5 11.2 multiply_reduce_fusion.66
  411.9 9.8 multiply_reduce_fusion.64
  421.9 6.2 multiply_reduce_fusion.65
  468.8 15.2 %add_convert_fusion = bf16[384,1024]{1,0:T(8,128)(2,1)S(1)} fusion(f32[384,1024]{1,0:T(8,128)S(1)} %get-tuple-element.506, f32[369,1024]{1,0:T(8,128)} %slice.1426, f32[370,1024]{1,0:T(8,128)} %slice.1425, f32[371,1024]{1,0:T(8,128)} %slice.1424, f32[372,1024]{1,0:T(8,128)} %slice.1423, f32[373,1024]{1,0:T(8,128)} %slice.1422, f32[374,1024]{1,0:T(8,128)} %slice.1421, ...), kind=kLoop, calls=%fused_computation.192 | loop fusion | flops 24772608 | bytes 48689152 | tf_op jit(solution)/shard_map/convert.171
  488.0 5.2 multiply_reduce_fusion.2
  494.9 11.6 multiply_reduce_fusion.31
  506.5 7.1 multiply_reduce_fusion.29
  516.2 12.6 %multiply_reduce_fusion.30 = (bf16[1536]{0:T(1024)(128)(2,1)}, f32[384,1536]{1,0:T(8,128)}, bf16[1536]{0:T(1024)(128)(2,1)}, f32[384,1536]{1,0:T(8,128)}, bf16[1...) fusion(f32[371,1536]{1,0:T(8,128)} %get-tuple-element.306, ...), kind=kLoop, calls=%fused_computation.131 | loop fusion | flops 15911424 | bytes 44517888 | tf_op jit(solution)/shard_map/reduce_sum | solution.py:184
  528.9 16.5 %multiply_reduce_fusion.32 = (bf16[1536]{0:T(1024)(128)(2,1)}, f32[384,1536]{1,0:T(8,128)}, bf16[1536]{0:T(1024)(128)(2,1)}, bf16[1536]{0:T(1024)(128)(2,1)}, f3...) fusion(f32[369,1536]{1,0:T(8,128)} %get-tuple-element.302, ...), kind=kLoop, calls=%fused_computation.133 | loop fusion | flops 17091072 | bytes 41951232 | tf_op jit(solution)/shard_map/reduce_sum | solution.py:184
  611.3 21.8 %multiply_reduce_fusion.1 = (bf16[1536]{0:T(1024)(128)(2,1)}, f32[384]{0:T(512)S(1)}, f32[384]{0:T(512)S(1)}, f32[384,1536]{1,0:T(8,128)S(1)}) fusion(f32[384]{0:T(512)S(1)} %copy-done.147, f32[384]{0:T(512)S(1)} %copy-done.141, f32[384,3072]{1,0:T(8,128)S(1)} %bitcast.211, f32[1536]{0:T(1024)S(1)} %copy-done.138, f32[369,1536]{1,0:T(8,128)} %slice.1458, ...), kind=kLoop, calls=%fused_computation.102 | loop fusion | flops 40695552 | bytes 76588032 | tf_op jit(solution)/shard_map/reduce_sum | solution.py:131
  634.8 5.2 fusion.6
  661.2 4.6 reshape.845
  805.0 4.7 reshape.843
  821.0 4.5 reshape.839
  829.1 5.6 reshape.841
  853.7 4.6 stack.303
  858.3 46.8 %all-reduce.150 = (f32[7]{0:T(128)S(1)}, f32[]{:T(128)}) all-reduce(f32[7]{0:T(128)S(1)} %stack.303, f32[]{:T(128)} %fusion.125), channel_id=1, replica_groups=mesh['dp'=4,'fsdp'=8] {'dp','fsdp'}, use_global_device_ids=true, to_apply=%region_103.104 | all-reduce | flops 8 | bytes 64 | tf_op jit(solution)/shard_map/psum | solution.py:392
  907.4 302.9 %reduce-scatter.2.cloned.1.call-done = bf16[1,512,512]{2,1,0:T(8,128)(2,1)} async-done(((bf16[32,512,512]{2,1,0:T(8,128)(2,1)}), bf16[1,512,512]{2,1,0:T(8,128)(2,1)}) %reduce-scatter.2.cloned.1.call-update) | async-done | bytes 524304 | tf_op jit(solution)/shard_map/reduce_scatter | solution.py:96
  (1088 shorter events, 543.6 us)
Async XLA Ops:
  7.2 132.1 %all-gather.3.cloned.1.call-start = ((), (), s32[]{:S(2)}) async-start(), calls=%async_computation.2 | async-start | bytes 17301504 | tf_op jit(solution)/shard_map/all_gather | solution.py:52
  21.6 1188.7 %reduce-scatter.2.cloned.1.call-start = ((), (), s32[]{:S(2)}) async-start(), calls=%async_computation.1 | async-start | bytes 17301504 | tf_op jit(solution)/shard_map/reduce_scatter | solution.py:96
  22.1 149.1 %copy-start.144 = (f32[384]{0:T(512)}, f32[384]{0:T(512)S(1)}, u32[]{:S(2)}) copy-start(f32[384]{0:T(512)S(1)} %broadcast_multiply_fusion.77) | copy-start | bytes 4612
  22.4 148.8 %copy-start.170 = (f32[384]{0:T(512)}, f32[384]{0:T(512)S(1)}, u32[]{:S(2)}) copy-start(f32[384]{0:T(512)S(1)} %add_rsqrt_fusion.4) | copy-start | bytes 4612
  24.9 150.0 %copy-start.298 = (f32[384]{0:T(512)}, f32[384]{0:T(512)S(1)}, u32[]{:S(2)}) copy-start(f32[384]{0:T(512)S(1)} %get-tuple-element.452) | copy-start | bytes 4612
  184.4 74.8 %copy-start.137 = (f32[1536]{0:T(1024)}, f32[1536]{0:T(1024)S(1)}, u32[]{:S(2)}) copy-start(f32[1536]{0:T(1024)S(1)} %reshape.869) | copy-start | bytes 18436
  195.0 64.2 %copy-start.140 = (f32[384]{0:T(512)}, f32[384]{0:T(512)S(1)}, u32[]{:S(2)}) copy-start(f32[384]{0:T(512)S(1)} %broadcast_multiply_fusion.63) | copy-start | bytes 4612
  197.0 62.3 %copy-start.146 = (f32[384]{0:T(512)}, f32[384]{0:T(512)S(1)}, u32[]{:S(2)}) copy-start(f32[384]{0:T(512)S(1)} %add_rsqrt_fusion.2) | copy-start | bytes 4612
  223.1 36.1 %copy-start.2 = (f32[382,1536]{1,0:T(8,128)}, f32[382,1536]{1,0:T(8,128)S(1)}, u32[]{:S(2)}) copy-start(f32[382,1536]{1,0:T(8,128)S(1)} %get-tuple-element.328) | copy-start | bytes 7041028
  234.1 19.5 %copy-start.178 = (f32[32,48]{1,0:T(8,128)S(1)}, f32[32,48]{1,0:T(8,128)}, u32[]{:S(2)}) copy-start(f32[32,48]{1,0:T(8,128)} %get-tuple-element.88) | copy-start | bytes 18436
  234.1 20.2 %copy-start.177 = (f32[32,48]{1,0:T(8,128)S(1)}, f32[32,48]{1,0:T(8,128)}, u32[]{:S(2)}) copy-start(f32[32,48]{1,0:T(8,128)} %get-tuple-element.89) | copy-start | bytes 18436
  234.1 20.8 %copy-start.176 = (f32[32,48]{1,0:T(8,128)S(1)}, f32[32,48]{1,0:T(8,128)}, u32[]{:S(2)}) copy-start(f32[32,48]{1,0:T(8,128)} %get-tuple-element.90) | copy-start | bytes 18436
  234.2 21.5 %copy-start.175 = (f32[32,48]{1,0:T(8,128)S(1)}, f32[32,48]{1,0:T(8,128)}, u32[]{:S(2)}) copy-start(f32[32,48]{1,0:T(8,128)} %get-tuple-element.91) | copy-start | bytes 18436
  234.2 22.2 %copy-start.174 = (f32[32,48]{1,0:T(8,128)S(1)}, f32[32,48]{1,0:T(8,128)}, u32[]{:S(2)}) copy-start(f32[32,48]{1,0:T(8,128)} %get-tuple-element.92) | copy-start | bytes 18436
  234.2 22.8 %copy-start.173 = (f32[32,48]{1,0:T(8,128)S(1)}, f32[32,48]{1,0:T(8,128)}, u32[]{:S(2)}) copy-start(f32[32,48]{1,0:T(8,128)} %get-tuple-element.93) | copy-start | bytes 18436
  259.3 27.4 %copy-start.100 = (bf16[32,48,512]{2,1,0:T(8,128)(2,1)S(1)}, bf16[32,48,512]{2,1,0:T(8,128)(2,1)}, u32[]{:S(2)}) copy-start(bf16[32,48,512]{2,1,0:T(8,128)(2,1)} %get-tuple-element.245) | copy-start | bytes 4718596
  305.0 61.5 %copy-start.20 = (f32[383,1024]{1,0:T(8,128)}, f32[383,1024]{1,0:T(8,128)S(1)}, u32[]{:S(2)}) copy-start(f32[383,1024]{1,0:T(8,128)S(1)} %get-tuple-element.399) | copy-start | bytes 4706308
  315.2 45.9 %copy-start.172 = (f32[32,32]{1,0:T(8,128)S(1)}, f32[32,32]{1,0:T(8,128)}, u32[]{:S(2)}) copy-start(f32[32,32]{1,0:T(8,128)} %get-tuple-element.62) | copy-start | bytes 12292
  464.4 23.4 %slice-start.2 = ((s8[4718592]{0:T(1024)(128)(4,1)}), s8[4194304]{0:T(1024)(128)(4,1)S(1)}, s32[]{:S(2)}) async-start(s8[4718592]{0:T(1024)(128)(4,1)} %bitcast.208), calls=%async_computation.5 | async-start | bytes 8388608
  852.4 53.9 %copy-start.305 = (f32[384]{0:T(512)S(1)}, f32[384]{0:T(512)}, u32[]{:S(2)}) copy-start(f32[384]{0:T(512)} %get-tuple-element.32) | copy-start | bytes 4612
  852.4 53.9 %copy-start.304 = (f32[384]{0:T(512)S(1)}, f32[384]{0:T(512)}, u32[]{:S(2)}) copy-start(f32[384]{0:T(512)} %get-tuple-element.35) | copy-start | bytes 4612
  852.4 53.9 %copy-start.120 = (f32[384,512]{1,0:T(8,128)S(1)}, f32[384,512]{1,0:T(8,128)}, u32[]{:S(2)}) copy-start(f32[384,512]{1,0:T(8,128)} %copy-done.119) | copy-start | bytes 2359300
  852.4 53.9 %copy-start.135 = (f32[384,512]{1,0:T(8,128)S(1)}, f32[384,512]{1,0:T(8,128)}, u32[]{:S(2)}) copy-start(f32[384,512]{1,0:T(8,128)} %get-tuple-element.511) | copy-start | bytes 2359300
  852.4 53.9 %copy-start.297 = (f32[512]{0:T(512)S(1)}, f32[512]{0:T(512)}, u32[]{:S(2)}) copy-start(f32[512]{0:T(512)} %copy-done.295) | copy-start | bytes 6148
  (291 other events, 1736.6 us)
Sparse Core Ops, SparseCore 0:
  21.7 117.5 all-gather.2
  852.6 357.6 reduce-scatter.1
where the time goes:
time: 1240 us; the launch traced here: 1230 us
  local copies, waits for them, and re-layouts  471 us (38%)
  waiting for transfers between devices  417 us (34%)
  other arithmetic  203 us (16%)
  matrix products  73.1 us (6%)
  blocking collectives  46.8 us (4%)
  between operations  18.3 us (1%)
    reduce_scatter x1, waiting for transfers between devices, scatter_gradients(): lax.psum_scatter(jnp.concatenate(pieces, axis=1), AXES, scatter_dimension...  303 us
    all_gather x1, waiting for transfers between devices, gather_weights(): gathered = lax.all_gather(jnp.concatenate(packed), AXES, axis=0)  114 us
    unnamed x713, local copies, waits for them, and re-layouts  108 us
    another operation x64, local copies, waits for them, and re-layouts, conv_backward(): return (summed, jnp.stack(kernel_rows))  84.5 us
    reduce_sum x7, other arithmetic, conv_backward(): kernel_rows.append(jnp.sum(masked * shifted(values, offset), axis=0))  66.2 us
    slice x46, local copies, waits for them, and re-layouts, shifted(): values[:offset]  62.9 us
    mul x62, local copies, waits for them, and re-layouts, segment_conv(): kernel[tap_index] * shifted(values, tap_index - half_width)  62.7 us
    convert_element_type x5, other arithmetic, to_low(): return values.astype(jnp.bfloat16)  49.6 us
  transfers between devices with their start and end apart: 2, of which 2 were waited for; matrix products, arithmetic and copies ran while one was open for 1% of the time, Pallas kernels for 0%

commit v1 on v0

v1 whole, which is shorter than its diff:
```python
import functools

import jax
import jax.numpy as jnp
from jax import lax
from jax.experimental import pallas as pl
from jax.experimental.pallas import tpu as pltpu
from jax.sharding import Mesh, PartitionSpec as P

HEADS = 8
EPSILON = 1e-05
NEGATIVE = -1000000000.0
TILE = 8
GAP = 16
CHAN = 128
WIDTH = 512
BLOCKS = 32
F32 = jnp.float32
LOW = jnp.bfloat16


def dot(left, right):
    return jnp.dot(left, right, preferred_element_type=F32)


def dot_tn(left, right):
    return lax.dot_general(left, right, (((0,), (0,)), ((), ())), preferred_element_type=F32)


def dot_nt(left, right):
    return lax.dot_general(left, right, (((1,), (1,)), ((), ())), preferred_element_type=F32)


def normalize(values):
    centred = values - jnp.mean(values, axis=-1, keepdims=True)
    variance = jnp.mean(centred * centred, axis=-1, keepdims=True)
    inverse = lax.rsqrt(variance + EPSILON)
    return centred * inverse, inverse


def normalize_back(upstream, gain, normal, inverse):
    scaled = upstream * gain
    mean_scaled = jnp.mean(scaled, axis=-1, keepdims=True)
    mean_cross = jnp.mean(scaled * normal, axis=-1, keepdims=True)
    return inverse * (scaled - mean_scaled - normal * mean_cross)


def row_sum(values):
    return jnp.sum(values, axis=0, keepdims=True)


GELU_A = 0.7978845608028654
GELU_B = 0.044715


def gelu(v):
    return 0.5 * v * (1.0 + jnp.tanh(GELU_A * (v + GELU_B * v * v * v)))


def gelu_pair(v):
    square = v * v
    bend = jnp.tanh(GELU_A * (v + GELU_B * square * v))
    value = 0.5 * v * (1.0 + bend)
    slope = 0.5 * (1.0 + bend) + 0.5 * v * (1.0 - bend * bend) * (
        GELU_A * (1.0 + 3.0 * GELU_B * square)
    )
    return value, slope


def silu(v):
    return v * jax.nn.sigmoid(v)


def store_halves(value, send, keep, mine, rows, start):
    parts = value.astype(LOW).reshape(2, 2, 8, rows, WIDTH)

    @pl.when(mine == 0)
    def _():
        keep[:, :, pl.ds(start, rows), :] = parts[:, 0]
        send[:, :, pl.ds(start, rows), :] = parts[:, 1]

    @pl.when(mine == 1)
    def _():
        keep[:, :, pl.ds(start, rows), :] = parts[:, 1]
        send[:, :, pl.ds(start, rows), :] = parts[:, 0]


def join_rows(first, second, mine):
    low = jnp.where(mine == 0, first, second)
    high = jnp.where(mine == 0, second, first)
    return jnp.stack([low, high], axis=1).reshape(-1, WIDTH)


def pick_rows(first, second, flag):
    return jnp.where(flag, first, second).reshape(-1, WIDTH)


def visits(info, segments, body):
    for s in range(segments):
        begin, end = info[1 + s], info[1 + segments + s]

        def visit(i, _, s=s, begin=begin, end=end):
            row = i * TILE + lax.broadcasted_iota(jnp.int32, (TILE, CHAN), 0)
            inside = jnp.logical_and(row >= begin, row < end)
            body(s, pl.multiple_of(i * TILE, TILE), inside)
            return 0

        lax.fori_loop(begin // TILE, (end + TILE - 1) // TILE, visit, 0)


def spread(source, padded, info, segments, blocks):
    padded[...] = jnp.zeros_like(padded)

    def body(s, base, inside):
        for c in range(blocks):
            value = source[pl.ds(base, TILE), c * CHAN : (c + 1) * CHAN]
            padded[c, pl.ds(base + GAP * (s + 1), TILE), :] = jnp.where(inside, value, 0.0)

    visits(info, segments, body)


def unspread(padded, target, info, segments, blocks):
    def body(s, base, inside):
        for c in range(blocks):
            lanes = slice(c * CHAN, (c + 1) * CHAN)
            value = padded[c, pl.ds(base + GAP * (s + 1), TILE), :]
            target[pl.ds(base, TILE), lanes] = jnp.where(
                inside, value, target[pl.ds(base, TILE), lanes]
            )

    visits(info, segments, body)


def conv_rows(padded, kernel, out, blocks, row_block, taps, flip):
    half = (taps - 1) // 2
    steps = (padded.shape[1] - 2 * GAP) // row_block

    def body(step, _):
        c = step // steps
        base = (step % steps) * row_block + GAP
        lanes = pl.ds(pl.multiple_of(c * CHAN, CHAN), CHAN)
        total = jnp.zeros((row_block, CHAN), F32)
        for j in range(taps):
            shift = half - j if flip else j - half
            total += kernel[pl.ds(j, 1), lanes] * padded[c, pl.ds(base + shift, row_block), :]
        out[c, pl.ds(pl.multiple_of(base, TILE), row_block), :] = total
        return 0

    lax.fori_loop(0, blocks * steps, body, 0)


def conv_taps(padded_grad, padded, out, blocks, row_block, taps):
    half = (taps - 1) // 2
    steps = (padded.shape[1] - 2 * GAP) // row_block
    tiles = row_block // TILE

    def block(c, _):
        lanes = pl.ds(pl.multiple_of(c * CHAN, CHAN), CHAN)

        def body(step, sums):
            base = pl.multiple_of(step * row_block + GAP, TILE)
            grad = padded_grad[c, pl.ds(base, row_block), :]
            new = []
            for j in range(taps):
                term = grad * padded[c, pl.ds(base + j - half, row_block), :]
                new.append(sums[j] + jnp.sum(term.reshape(tiles, TILE, CHAN), axis=0))
            return tuple(new)

        zero = jnp.zeros((TILE, CHAN), F32)
        sums = lax.fori_loop(0, steps, body, (zero,) * taps)
        for j in range(taps):
            out[pl.ds(j, 1), lanes] = row_sum(sums[j])
        return 0

    lax.fori_loop(0, blocks, block, 0)


def front_forward_kernel(
    info, x_ref, gain, valid, up, up_two, down, down_two, out, before_out, stat, low, total
):
    h = pl.program_id(0)
    mine = info[0]
    up_value = join_rows(up[...], up_two[...], mine)
    down_value = pick_rows(down[...], down_two[...], h % 2 == mine)

    @pl.when(h == 0)
    def _():
        normal, _ = normalize(x_ref[...].astype(F32))
        low[...] = (normal * gain[...]).astype(LOW)
        total[...] = jnp.zeros_like(total)

    before = dot(low[...], up_value)
    before_out[...] = before
    total[...] += dot(silu(before).astype(LOW), down_value)

    @pl.when(h == pl.num_programs(0) - 1)
    def _():
        x = x_ref[...].astype(F32)
        part = 0.5 * total[...]
        after = x + part
        out[...] = after
        v = valid[...]
        stat[0:1, :] = row_sum(x * x * v)
        stat[1:2, :] = row_sum(after * after * v)
        stat[2:3, :] = row_sum(part * part * v)
        stat[3:, :] = jnp.zeros((5, WIDTH), F32)


def head_masks(segs_col, segs_row):
    allowed = segs_col == segs_row
    lane = lax.broadcasted_iota(jnp.int32, (1, CHAN), 1)
    return allowed, (lane < CHAN // 2, lane >= CHAN // 2)


def head_probs(query, key, allowed, scale):
    scores = jnp.where(allowed, dot_nt(query, key) * scale, NEGATIVE)
    exponent = jnp.exp(scores - jnp.max(scores, axis=-1, keepdims=True))
    return exponent / jnp.sum(exponent, axis=-1, keepdims=True)


def heads_forward_kernel(
    info, x_ref, gain, segs_col, segs_row, w_in, w_in_two, w_out, w_out_two,
    attended, packed, mixed,
):
    mine = info[0]
    scale = (WIDTH // HEADS) ** -0.5
    normal, _ = normalize(x_ref[...])
    low = (normal * gain[...]).astype(LOW)
    for q in range(3):
        rows = slice(16 * q, 16 * (q + 1))
        weight = join_rows(w_in[:, :, rows, :], w_in_two[:, :, rows, :], mine)
        packed[:, WIDTH * q : WIDTH * (q + 1)] = dot(low, weight).astype(LOW)
    allowed, halves = head_masks(segs_col[...], segs_row[...])

    def pair(p, _):
        lanes = [
            pl.ds(pl.multiple_of(WIDTH * q + CHAN * p, CHAN), CHAN) for q in range(3)
        ]
        query, key, value = (packed[:, lane] for lane in lanes)
        parts = []
        for half in halves:
            probs = head_probs(jnp.where(half, query, 0), key, allowed, scale)
            parts.append(dot(probs.astype(LOW), value))
        mixed[:, lanes[0]] = jnp.where(halves[0], parts[0], parts[1]).astype(LOW)
        return 0

    lax.fori_loop(0, HEADS // 2, pair, 0)
    attended[...] = dot(mixed[...], join_rows(w_out[...], w_out_two[...], mine))


def heads_backward_kernel(
    info, grad, x_ref, gain, segs_col, segs_row, packed, mixed, w_in, w_in_two, w_out, w_out_two,
    stream, gain_grad, in_send, in_keep, out_send, out_keep, mixed_grad, packed_grad, low,
):
    scale = (WIDTH // HEADS) ** -0.5
    mine = info[0]
    attended_low = grad[...].astype(LOW)
    store_halves(dot_tn(mixed[...], attended_low), out_send, out_keep, mine, 16, 0)
    mixed_grad[...] = dot_nt(attended_low, join_rows(w_out[...], w_out_two[...], mine)).astype(LOW)
    normal, inverse = normalize(x_ref[...])
    low[...] = (normal * gain[...]).astype(LOW)
    allowed, halves = head_masks(segs_col[...], segs_row[...])

    def pair(p, _):
        lanes = [
            pl.ds(pl.multiple_of(WIDTH * q + CHAN * p, CHAN), CHAN) for q in range(3)
        ]
        query, key, value = (packed[:, lane] for lane in lanes)
        upstream = mixed_grad[:, lanes[0]]
        parts = []
        for half in halves:
            probs = head_probs(jnp.where(half, query, 0), key, allowed, scale)
            probs_grad = dot_nt(jnp.where(half, upstream, 0), value)
            value_grad = dot_tn(probs.astype(LOW), upstream)
            inner = jnp.sum(probs_grad * probs, axis=-1, keepdims=True)
            score_grad = (probs * (probs_grad - inner)).astype(LOW)
            query_grad = dot(score_grad, key) * scale
            key_grad = dot_tn(score_grad, query) * scale
            parts.append((query_grad, key_grad, value_grad))
        for q in range(3):
            packed_grad[:, lanes[q]] = jnp.where(halves[0], parts[0][q], parts[1][q]).astype(LOW)
        return 0

    lax.fori_loop(0, HEADS // 2, pair, 0)
    total = jnp.zeros(x_ref.shape, F32)
    for q in range(3):
        rows = slice(16 * q, 16 * (q + 1))
        weight = join_rows(w_in[:, :, rows, :], w_in_two[:, :, rows, :], mine)
        piece = packed_grad[:, WIDTH * q : WIDTH * (q + 1)]
        store_halves(dot_tn(low[...], piece), in_send, in_keep, mine, 16, 16 * q)
        total += dot_nt(piece, weight)
    gain_grad[...] = row_sum(total * normal)
    stream[...] = normalize_back(total, gain[...], normal, inverse)


def gated_forward_kernel(
    info, x_ref, gain, gate_gain, taps_ref, w_in, w_in_two, w_out, w_out_two,
    gated, before_out, normal_out, inverse_out, part_out, product,
    low, act, padded, conv, *, segments, row_block, taps,
):
    j = pl.program_id(0)
    thirds = WIDTH * 3

    @pl.when(j == 0)
    def _():
        normal, _ = normalize(x_ref[...])
        low[...] = (normal * gain[...]).astype(LOW)

    before = dot(low[...], join_rows(w_in[...], w_in_two[...], info[0]))
    before_out[...] = before
    value = gelu(before)

    @pl.when(j < 3)
    def _():
        act[:, pl.ds(pl.multiple_of(j * WIDTH, WIDTH), WIDTH)] = value

    @pl.when(j == 2)
    def _():
        normal, inverse = normalize(act[...])
        normal_out[...] = normal
        inverse_out[...] = inverse
        act[...] = normal * gate_gain[...]
        blocks = thirds // CHAN
        spread(act, padded, info, segments, blocks)
        conv_rows(padded, taps_ref, conv, blocks, row_block, taps, False)
        unspread(conv, part_out, info, segments, blocks)

    @pl.when(j >= 3)
    def _():
        lanes = pl.ds(pl.multiple_of((j - 3) * WIDTH, WIDTH), WIDTH)
        product[:, lanes] = (value * part_out[:, lanes]).astype(LOW)

    @pl.when(j == 5)
    def _():
        gated[...] = dot(product[...], join_rows(w_out[...], w_out_two[...], info[0]))


def gated_backward_kernel(
    info, grad, x_ref, gain, gate_gain, taps_ref, before, normal_ref, inverse_ref, part, product,
    w_in, w_in_two, w_out, w_out_two,
    stream, gain_grad, gate_gain_grad, taps_grad, in_send, in_keep, out_send, out_keep,
    low, product_grad, padded, padded_grad, conv, total, *, segments, row_block, taps,
):
    j = pl.program_id(0)
    mine = info[0]
    thirds = WIDTH * 3
    blocks = thirds // CHAN

    @pl.when(j == 0)
    def _():
        normal, _ = normalize(x_ref[...])
        low[...] = (normal * gain[...]).astype(LOW)
        total[...] = jnp.zeros_like(total)
        gated_low = grad[...].astype(LOW)
        store_halves(dot_tn(product[...], gated_low), out_send, out_keep, mine, 48, 0)
        product_grad[...] = dot_nt(gated_low, join_rows(w_out[...], w_out_two[...], mine))

    value, slope = gelu_pair(before[...])
    weight = join_rows(w_in[...], w_in_two[...], mine)

    def finish(before_grad, column):
        store_halves(
            dot_tn(low[...], before_grad), in_send, in_keep, mine, 16,
            pl.multiple_of(column * 16, 16),
        )
        total[...] += dot_nt(before_grad, weight)

    @pl.when(j < 3)
    def _():
        lanes = pl.ds(pl.multiple_of(j * WIDTH, WIDTH), WIDTH)
        upstream = product_grad[:, lanes]
        product_grad[:, lanes] = upstream * value
        finish((upstream * part[:, lanes] * slope).astype(LOW), j)

    @pl.when(j == 2)
    def _():
        spread(product_grad, padded_grad, info, segments, blocks)
        product_grad[...] = normal_ref[...] * gate_gain[...]
        spread(product_grad, padded, info, segments, blocks)
        conv_taps(padded_grad, padded, taps_grad, blocks, row_block, taps)
        conv_rows(padded_grad, taps_ref, conv, blocks, row_block, taps, True)
        unspread(conv, product_grad, info, segments, blocks)
        upstream = product_grad[...]
        normal = normal_ref[...]
        gate_gain_grad[...] = row_sum(upstream * normal)
        product_grad[...] = normalize_back(upstream, gate_gain[...], normal, inverse_ref[...])

    @pl.when(j >= 3)
    def _():
        lanes = pl.ds(pl.multiple_of((j - 3) * WIDTH, WIDTH), WIDTH)
        finish((product_grad[:, lanes] * slope).astype(LOW), j)

    @pl.when(j == 5)
    def _():
        normal, inverse = normalize(x_ref[...])
        gain_grad[...] = row_sum(total[...] * normal)
        stream[...] = normalize_back(total[...], gain[...], normal, inverse)


def merge_forward_kernel(
    info, x_ref, attended, gated, taps_ref, valid, weight, weight_two,
    out, merged_low, stat, joined, padded, conv, *, segments, row_block, taps,
):
    blocks = 2 * WIDTH // CHAN
    joined[:, :WIDTH] = attended[...]
    joined[:, WIDTH:] = gated[...]
    spread(joined, padded, info, segments, blocks)
    conv_rows(padded, taps_ref, conv, blocks, row_block, taps, False)
    for c in range(blocks):
        conv[c] += padded[c]
    unspread(conv, joined, info, segments, blocks)
    merged_low[...] = joined[...].astype(LOW)
    part = dot(merged_low[...], join_rows(weight[...], weight_two[...], info[0]))
    after = x_ref[...] + part
    out[...] = after
    v = valid[...]
    stat[0:1, :] = row_sum(after * after * v)
    stat[1:2, :] = row_sum(part * part * v)
    stat[2:, :] = jnp.zeros((6, WIDTH), F32)


def merge_backward_kernel(
    info, grad, attended, gated, merged_low, taps_ref, weight, weight_two,
    attended_grad, gated_grad, taps_grad, send, keep,
    joined, padded, padded_grad, conv, *, segments, row_block, taps,
):
    blocks = 2 * WIDTH // CHAN
    low = grad[...].astype(LOW)
    store_halves(dot_tn(merged_low[...], low), send, keep, info[0], 32, 0)
    joined[:, :WIDTH] = attended[...]
    joined[:, WIDTH:] = gated[...]
    spread(joined, padded, info, segments, blocks)
    joined[...] = dot_nt(low, join_rows(weight[...], weight_two[...], info[0]))
    spread(joined, padded_grad, info, segments, blocks)
    conv_taps(padded_grad, padded, taps_grad, blocks, row_block, taps)
    conv_rows(padded_grad, taps_ref, conv, blocks, row_block, taps, True)
    for c in range(blocks):
        conv[c] += padded_grad[c]
    unspread(conv, joined, info, segments, blocks)
    attended_grad[...] = joined[:, :WIDTH]
    gated_grad[...] = joined[:, WIDTH:]


def ffn_backward_step(h, mine, low, before, part_grad, up, down, sends, total):
    up_send, up_keep, down_send, down_keep = sends
    gate = jax.nn.sigmoid(before)
    hidden = (before * gate).astype(LOW)
    part_low = part_grad[...]
    hidden_grad = dot_nt(part_low, down)
    before_grad = (hidden_grad * (gate * (1.0 + before * (1.0 - gate)))).astype(LOW)
    down_grad = dot_tn(hidden, part_low).astype(LOW).reshape(8, 64, WIDTH)

    @pl.when(h % 2 == mine)
    def _():
        down_keep[h // 2] = down_grad

    @pl.when(h % 2 != mine)
    def _():
        down_send[h // 2] = down_grad

    store_halves(
        dot_tn(low[...], before_grad), up_send, up_keep, mine, 16, pl.multiple_of(h * 16, 16)
    )
    total[...] += dot_nt(before_grad, up)


def rear_kernel(
    info, x_ref, gain, final_gain, valid, cotangent, up, up_two, down, down_two,
    encoded, stream, gain_grad, final_gain_grad, stat,
    up_send, up_keep, down_send, down_keep,
    low, before, part_grad, stream_grad, total,
):
    step = pl.program_id(0)
    h = jnp.where(step < 4, step, 7 - step)
    up_value = join_rows(up[...], up_two[...], info[0])
    down_value = pick_rows(down[...], down_two[...], h % 2 == info[0])

    @pl.when(step == 0)
    def _():
        normal, _ = normalize(x_ref[...])
        low[...] = (normal * gain[...]).astype(LOW)
        total[...] = jnp.zeros_like(total)

    @pl.when(step < 4)
    def _():
        value = dot(low[...], up_value)
        before[step] = value
        total[...] += dot(silu(value).astype(LOW), down_value)

    @pl.when(step == 3)
    def _():
        part = 0.5 * total[...]
        after = x_ref[...] + part
        v = valid[...]
        stat[0:1, :] = row_sum(after * after * v)
        stat[1:2, :] = row_sum(part * part * v)
        stat[2:, :] = jnp.zeros((6, WIDTH), F32)
        normal, inverse = normalize(after)
        encoded[...] = (normal * final_gain[...] * v).astype(LOW)
        upstream = cotangent[...].astype(F32) * v
        final_gain_grad[...] = row_sum(upstream * normal)
        grad = normalize_back(upstream, final_gain[...], normal, inverse)
        stream_grad[...] = grad
        part_grad[...] = (0.5 * grad).astype(LOW)
        total[...] = jnp.zeros_like(total)

    @pl.when(step >= 4)
    def _():
        ffn_backward_step(
            h, info[0], low, before[h], part_grad, up_value, down_value,
            (up_send, up_keep, down_send, down_keep), total,
        )

    @pl.when(step == 7)
    def _():
        normal, inverse = normalize(x_ref[...])
        gain_grad[...] = row_sum(total[...] * normal)
        stream[...] = stream_grad[...] + normalize_back(total[...], gain[...], normal, inverse)


def front_backward_kernel(
    info, grad, heads_stream, gated_stream, x_ref, gain, before, up, up_two, down, down_two,
    x_grad, gain_send, gain_keep, up_send, up_keep, down_send, down_keep,
    low, part_grad, stream_grad, total,
):
    h = pl.program_id(0)

    @pl.when(h == 0)
    def _():
        normal, _ = normalize(x_ref[...].astype(F32))
        low[...] = (normal * gain[...]).astype(LOW)
        stream_sum = grad[...] + heads_stream[...] + gated_stream[...]
        stream_grad[...] = stream_sum
        part_grad[...] = (0.5 * stream_sum).astype(LOW)
        total[...] = jnp.zeros_like(total)

    ffn_backward_step(
        h, info[0], low, before[...], part_grad,
        join_rows(up[...], up_two[...], info[0]),
        pick_rows(down[...], down_two[...], h % 2 == info[0]),
        (up_send, up_keep, down_send, down_keep), total,
    )

    @pl.when(h == 3)
    def _():
        normal, inverse = normalize(x_ref[...].astype(F32))
        gain_grad = row_sum(total[...] * normal).astype(LOW)
        gain_send[...] = jnp.broadcast_to(gain_grad.reshape(1, 1, 1, WIDTH), gain_send.shape)
        gain_keep[...] = gain_send[...]
        x_grad[...] = (
            stream_grad[...] + normalize_back(total[...], gain[...], normal, inverse)
        ).astype(LOW)


def whole(shape):
    return pl.BlockSpec(shape, lambda *_: (0,) * len(shape))


def call(kernel, grid, inputs, outputs, scratch, info, flops):
    in_specs = [
        whole(array.shape) if block is None else pl.BlockSpec(block, index)
        for array, block, index in inputs
    ]
    out_specs = [
        whole(shape) if block is None else pl.BlockSpec(block, index)
        for shape, _, block, index in outputs
    ]
    arrays = [array for array, _, _ in inputs]
    shapes = [jax.ShapeDtypeStruct(shape, kind) for shape, kind, _, _ in outputs]
    moved = sum(array.size * array.dtype.itemsize for array in arrays)
    moved = sum(shape.size * shape.dtype.itemsize for shape in shapes) + min(moved, 1 << 24)
    return pl.pallas_call(
        kernel,
        grid_spec=pltpu.PrefetchScalarGridSpec(
            num_scalar_prefetch=1,
            grid=grid,
            in_specs=in_specs,
            out_specs=out_specs,
            scratch_shapes=scratch,
        ),
        out_shape=shapes,
        compiler_params=pltpu.CompilerParams(vmem_limit_bytes=56 * 1024 * 1024),
        cost_estimate=pl.CostEstimate(flops=flops, bytes_accessed=moved, transcendentals=0),
    )(info, *arrays)


def segment_table(lengths, mine, row_count):
    ends = jnp.cumsum(lengths)
    position = jnp.arange(row_count, dtype=jnp.int32)
    segments = jnp.sum((position[None, :] >= ends[:, None]).astype(jnp.int32), axis=0)
    zero = jnp.zeros((1,), jnp.int32)
    last = jnp.full((1,), row_count, jnp.int32)
    info = jnp.concatenate([jnp.full((1,), mine, jnp.int32), zero, ends, ends, last])
    return segments, info.astype(jnp.int32)


def layer(features, cotangent, lengths, mine, front, middle, rear, smaller, taps):
    gate_taps, merge_taps, front_gain, heads_gain, gated_gain, gate_gain, rear_gain, final_gain = (
        element if element.ndim == 2 else element.reshape(1, -1) for element in smaller
    )
    tokens = features.shape[0]
    count = lengths.shape[0]
    segments = count + 1
    seg_ids, info = segment_table(lengths, mine, tokens)
    segs_col, segs_row = seg_ids[:, None], seg_ids[None, :]
    valid = (segs_col < count).astype(F32)
    stream = (tokens, WIDTH)
    thirds, double, hidden = 3 * WIDTH, 2 * WIDTH, 4 * WIDTH
    spread_rows = tokens + GAP * (segments + 1)
    row_block = (spread_rows - 2 * GAP) // 4
    tokens_low = pltpu.VMEM(stream, LOW)
    tokens_f32 = pltpu.VMEM(stream, F32)
    stat = ((8, WIDTH), F32, None, None)
    vector = ((1, WIDTH), F32, None, None)
    flop = 2 * tokens * WIDTH * WIDTH

    def all_of(*arrays):
        return [(array, None, None) for array in arrays]

    def halves(rows):
        return [((2, 8, rows, WIDTH), LOW, None, None)] * 2

    def columns(pair, rows, start, index):
        block = (2, 8, rows, WIDTH), lambda *i: (0, 0, start // rows + index(*i), 0)
        return [(array, *block) for array in pair]

    def lines(pair, index):
        block = (1, 8, 64, WIDTH), lambda *i: (index(*i) // 2, 0, 1, 0)
        return [(array, *block) for array in pair]

    def first(*_):
        return 0

    def step(h, _):
        return h

    front_blocks = columns(front, 16, 0, step) + lines(front, step)
    after_front, front_before, front_stat = call(
        front_forward_kernel,
        (4,),
        all_of(features, front_gain, valid) + front_blocks,
        [
            (stream, F32, None, None),
            ((tokens, hidden), F32, (tokens, WIDTH), lambda h, _: (0, h)),
            stat,
        ],
        [tokens_low, tokens_f32],
        info,
        8 * flop,
    )
    heads_blocks = columns(middle, 48, 144, first) + columns(middle, 16, 192, first)
    attended, packed, mixed = call(
        heads_forward_kernel,
        (1,),
        all_of(after_front, heads_gain, segs_col, segs_row)
        + heads_blocks,
        [
            (stream, F32, None, None),
            ((tokens, thirds), LOW, None, None),
            (stream, LOW, None, None),
        ],
        [],
        info,
        6 * flop,
    )
    gated_out = columns(middle, 48, 96, first)
    padded = pltpu.VMEM((thirds // CHAN, spread_rows, CHAN), F32)
    gated, gated_before, gate_normal, gate_inverse, gate_part, product = call(
        functools.partial(gated_forward_kernel, segments=segments, row_block=row_block, taps=taps),
        (6,),
        all_of(after_front, gated_gain, gate_gain, gate_taps)
        + columns(middle, 16, 0, lambda j, _: (j + 3) % 6)
        + gated_out,
        [
            (stream, F32, None, None),
            ((tokens, 6 * WIDTH), F32, (tokens, WIDTH), lambda j, _: (0, (j + 3) % 6)),
            ((tokens, thirds), F32, None, None),
            ((tokens, 1), F32, None, None),
            ((tokens, thirds), F32, None, None),
            ((tokens, thirds), LOW, None, None),
        ],
        [tokens_low, pltpu.VMEM((tokens, thirds), F32), padded, padded],
        info,
        18 * flop,
    )
    merge_block = columns(rear, 32, 128, first)
    joined = pltpu.VMEM((tokens, double), F32)
    padded_two = pltpu.VMEM((double // CHAN, spread_rows, CHAN), F32)
    after_merge, merged_low, merge_stat = call(
        functools.partial(merge_forward_kernel, segments=segments, row_block=row_block, taps=taps),
        (1,),
        all_of(after_front, attended, gated, merge_taps, valid) + merge_block,
        [(stream, F32, None, None), ((tokens, double), LOW, None, None), stat],
        [joined, padded_two, padded_two],
        info,
        8 * flop,
    )

    def bounce(i, _):
        return jnp.where(i < 4, i, 7 - i)

    encoded, merge_grad, rear_gain_grad, final_gain_grad, rear_stat, *rear_halves = call(
        rear_kernel,
        (8,),
        all_of(after_merge, rear_gain, final_gain, valid, cotangent)
        + columns(rear, 16, 0, bounce)
        + lines(rear, bounce),
        [(stream, LOW, None, None), (stream, F32, None, None), vector, vector, stat]
        + halves(64)
        + halves(64),
        [tokens_low, pltpu.VMEM((4, tokens, WIDTH), F32), tokens_low, tokens_f32, tokens_f32],
        info,
        26 * flop,
    )
    attended_grad, gated_grad, merge_taps_grad, *merge_halves = call(
        functools.partial(merge_backward_kernel, segments=segments, row_block=row_block, taps=taps),
        (1,),
        all_of(merge_grad, attended, gated, merged_low, merge_taps) + merge_block,
        [(stream, F32, None, None), (stream, F32, None, None), ((taps + 1, double), F32, None, None)]
        + halves(32),
        [joined, padded_two, padded_two, padded_two],
        info,
        16 * flop,
    )
    heads_stream, heads_gain_grad, *heads_halves = call(
        heads_backward_kernel,
        (1,),
        all_of(attended_grad, after_front, heads_gain, segs_col, segs_row, packed, mixed)
        + heads_blocks,
        [(stream, F32, None, None), vector] + halves(48) + halves(16),
        [tokens_low, pltpu.VMEM((tokens, thirds), LOW), tokens_low],
        info,
        16 * flop,
    )
    gated_stream, gated_gain_grad, gate_gain_grad, gate_taps_grad, *gated_halves = call(
        functools.partial(gated_backward_kernel, segments=segments, row_block=row_block, taps=taps),
        (6,),
        all_of(gated_grad, after_front, gated_gain, gate_gain, gate_taps)
        + [(gated_before, (tokens, WIDTH), lambda j, _: (0, j))]
        + all_of(gate_normal, gate_inverse, gate_part, product)
        + columns(middle, 16, 0, step)
        + gated_out,
        [
            (stream, F32, None, None),
            vector,
            ((1, thirds), F32, None, None),
            ((taps + 1, thirds), F32, None, None),
        ]
        + halves(96)
        + halves(48),
        [tokens_low, pltpu.VMEM((tokens, thirds), F32), padded, padded, padded, tokens_f32],
        info,
        36 * flop,
    )
    features_grad, *front_halves = call(
        front_backward_kernel,
        (4,),
        all_of(merge_grad, heads_stream, gated_stream, features, front_gain)
        + [(front_before, (tokens, WIDTH), lambda h, _: (0, h))]
        + front_blocks,
        [(stream, LOW, None, None)] + halves(16) + halves(64) + halves(64),
        [tokens_low, tokens_low, tokens_f32, tokens_f32],
        info,
        16 * flop,
    )
    small_grads = (
        gate_taps_grad, merge_taps_grad, heads_gain_grad, gated_gain_grad, rear_gain_grad,
        final_gain_grad, gate_gain_grad,
    )
    stats = (front_stat, merge_stat, rear_stat)
    weight_halves = (front_halves, heads_halves, gated_halves, merge_halves, rear_halves)
    return encoded, features_grad, info, stats, weight_halves, small_grads


SMALL = 16


def ring(size, shift):
    return [(i, (i + shift) % size) for i in range(size)]


def local_call(kernel, inputs, outputs, scratch, info, grid=(1,), specs=None):
    in_specs, out_specs = specs if specs else (None, None)
    whole_out = [whole(shape) for shape, _ in outputs]
    return pl.pallas_call(
        kernel,
        grid_spec=pltpu.PrefetchScalarGridSpec(
            num_scalar_prefetch=1,
            grid=grid,
            in_specs=in_specs if in_specs else [whole(array.shape) for array in inputs],
            out_specs=out_specs if out_specs else whole_out,
            scratch_shapes=scratch,
        ),
        out_shape=[jax.ShapeDtypeStruct(shape, kind) for shape, kind in outputs],
        compiler_params=pltpu.CompilerParams(vmem_limit_bytes=40 * 1024 * 1024),
        cost_estimate=pl.CostEstimate(
            flops=0,
            bytes_accessed=2 * sum(array.size * array.dtype.itemsize for array in inputs),
            transcendentals=0,
        ),
    )(info, *inputs)


def pack_kernel(
    info, front_up, front_down, heads_in, heads_out, gated_in, gated_out, merge_out, rear_up,
    rear_down, gate_taps, merge_taps, gains, front, middle, rear,
):
    def put(target, start, source):
        rows, width = source.shape
        for q in range(width // WIDTH):
            target[start + rows * q : start + rows * (q + 1), :] = source[
                :, WIDTH * q : WIDTH * (q + 1)
            ]

    put(front, 0, front_up)
    put(front, 64, front_down)
    put(middle, 0, gated_in)
    put(middle, 96, gated_out)
    put(middle, 144, heads_in)
    put(middle, 192, heads_out)
    put(rear, 0, rear_up)
    put(rear, 64, rear_down)
    put(rear, 128, merge_out)
    gate = gate_taps[...].astype(F32)
    merge = merge_taps[...].astype(F32)
    last = lax.broadcasted_iota(jnp.int32, (SMALL, CHAN), 0) == SMALL - 1
    quads = [
        gate[:SMALL],
        jnp.where(last, gains[...].astype(F32), gate[SMALL:]),
        merge[:SMALL],
        merge[SMALL:],
    ]
    for q in range(4):
        front[128 : 128 + SMALL, CHAN * q : CHAN * (q + 1)] = quads[q].astype(LOW)


def place_line_kernel(info, *refs):
    pieces, out, sem = refs[:4], refs[4], refs[5]
    copies = [
        pltpu.make_async_copy(piece, out.at[info[i]], sem.at[i])
        for i, piece in enumerate(pieces)
    ]
    for copy in copies:
        copy.start()
    for copy in copies:
        copy.wait()


def place_plane_kernel(info, *refs):
    pieces, out, sem = refs[:4], refs[4], refs[5]
    copies = [
        pltpu.make_async_copy(piece, out.at[info[4 + 2 * i], :, info[5 + 2 * i]], sem.at[i])
        for i, piece in enumerate(pieces)
    ]
    for copy in copies:
        copy.start()
    for copy in copies:
        copy.wait()


def anywhere(count):
    return [pl.BlockSpec(memory_space=pl.ANY)] * count


def gather_chunk(shard, spots):
    rows = shard.shape[0]
    line = [shard] + [lax.ppermute(shard, "z", ring(4, d)) for d in (1, 2, 3)]
    (line,) = local_call(
        place_line_kernel,
        line,
        [((4, rows, WIDTH), LOW)],
        [pltpu.SemaphoreType.DMA((4,))],
        spots,
        specs=(anywhere(4), anywhere(1)),
    )
    plane = [line] + [
        lax.ppermute(line, ("x", "y"), [(i, i ^ d) for i in range(4)]) for d in (1, 2, 3)
    ]
    (mine,) = local_call(
        place_plane_kernel,
        plane,
        [((2, 4, 2, rows, WIDTH), LOW)],
        [pltpu.SemaphoreType.DMA((4,))],
        spots,
        specs=(anywhere(4), anywhere(1)),
    )
    mine = mine.reshape(2, 8, rows, WIDTH)
    return mine, lax.ppermute(mine, "k", ring(2, 1))


def unpack_kernel(info, first, second, gate_taps, merge_taps, gains, gate_gain):
    mine = info[0]
    lane = lax.broadcasted_iota(jnp.int32, (SMALL, CHAN), 1)
    lane_row = lane[:1]
    gate_gain[...] = jnp.zeros_like(gate_gain)
    gains[...] = jnp.zeros_like(gains)

    def put(target, rows, value, start, size, lanes):
        block, offset = start // CHAN, start % CHAN
        inside = jnp.logical_and(lanes >= offset, lanes < offset + size)
        window = slice(CHAN * block, CHAN * (block + 1))
        target[rows, window] = jnp.where(inside, value, target[rows, window])
        spill = offset + size - CHAN
        if spill > 0:
            window = slice(CHAN * (block + 1), CHAN * (block + 2))
            target[rows, window] = jnp.where(lanes < spill, value, target[rows, window])

    for i in range(BLOCKS):
        x, core, rest = i // 16, (i // 8) % 2, i % 8
        value = jnp.where(mine == core, first[x, rest], second[x, rest]).astype(F32)
        quads = [value[:, CHAN * q : CHAN * (q + 1)] for q in range(4)]
        start = 48 * i
        for half in range(2):
            rows = slice(SMALL * half, SMALL * (half + 1))
            rolled = pltpu.roll(quads[half], start % CHAN, 1)
            put(gate_taps, rows, rolled, start, 48, lane)
            rolled = pltpu.roll(quads[2 + half], (32 * i) % CHAN, 1)
            put(merge_taps, rows, rolled, 32 * i, 32, lane)
        line = quads[1][SMALL - 1 :]
        for g in range(5):
            rolled = pltpu.roll(line, (16 * i - 16 * g) % CHAN, 1)
            put(gains, slice(g, g + 1), rolled, 16 * i, 16, lane_row)
        rolled = pltpu.roll(line, (48 * i - 80) % CHAN, 1)
        put(gate_gain, slice(0, 1), rolled, 48 * i, 48, lane_row)


def pack_small_kernel(
    info, gate_taps, merge_taps, heads_gain, gated_gain, rear_gain, final_gain, gate_gain,
    front_stat, merge_stat, rear_stat,
    send_high, keep_high, send_low, keep_low, *, count_at,
):
    mine = info[0]
    lane = lax.broadcasted_iota(jnp.int32, (SMALL, CHAN), 1)
    lane_row = lane[:1]
    last = lax.broadcasted_iota(jnp.int32, (SMALL, CHAN), 0) == SMALL - 1
    stats = [
        front_stat[0:1, :], front_stat[1:2, :], merge_stat[0:1, :], rear_stat[0:1, :],
        front_stat[2:3, :], merge_stat[1:2, :], rear_stat[1:2, :],
    ]
    stat_line = jnp.where(lane_row == 7, info[count_at].astype(F32), 0.0)
    for i, stat in enumerate(stats):
        stat_line = jnp.where(lane_row == i, jnp.sum(stat, axis=1, keepdims=True), stat_line)

    def take(source, rows, start, size, lanes):
        block, offset = start // CHAN, start % CHAN
        value = pltpu.roll(source[rows, CHAN * block : CHAN * (block + 1)], (-offset) % CHAN, 1)
        if offset + size > CHAN:
            other = source[rows, CHAN * (block + 1) : CHAN * (block + 2)]
            value = jnp.where(lanes < CHAN - offset, value, pltpu.roll(other, (-offset) % CHAN, 1))
        return value

    for i in range(BLOCKS):
        x, core, rest = i // 16, (i // 8) % 2, i % 8
        halves = [slice(0, SMALL), slice(SMALL, 2 * SMALL)]
        quads = [take(gate_taps, rows, 48 * i, 48, lane) for rows in halves]
        quads += [take(merge_taps, rows, 32 * i, 32, lane) for rows in halves]
        line = pltpu.roll(take(gate_gain, slice(0, 1), 48 * i, 48, lane_row), 80, 1)
        for g, gain in enumerate((heads_gain, gated_gain, rear_gain, final_gain)):
            start = 16 * (g + 1)
            value = pltpu.roll(take(gain, slice(0, 1), 16 * i, 16, lane_row), start, 1)
            inside = jnp.logical_and(lane_row >= start, lane_row < start + 16)
            line = jnp.where(inside, value, line)
        quads[1] = jnp.where(last, line, quads[1])
        quads[3] = jnp.where(last, stat_line, quads[3])
        for q in range(4):
            lanes = slice(CHAN * q, CHAN * (q + 1))
            high = quads[q].astype(LOW)
            rest_low = (quads[q] - high.astype(F32)).astype(LOW)

            @pl.when(mine == core)
            def _():
                keep_high[x, rest, :, lanes] = high
                keep_low[x, rest, :, lanes] = rest_low

            @pl.when(mine != core)
            def _():
                send_high[x, rest, :, lanes] = high
                send_low[x, rest, :, lanes] = rest_low


def split_store(target, index, start, rows, total, paired):
    high = total.astype(LOW)
    target[index, start : start + rows, :] = high
    if paired:
        target[index, start + rows : start + 2 * rows, :] = (total - high.astype(F32)).astype(LOW)


def core_sum_kernel(info, *refs, sizes):
    outs = refs[-4:]
    inputs = refs[:-4]
    half = len(inputs) // 2
    keeps, gots = inputs[:half], inputs[half:]
    x, y = info[4], info[5]
    for d in range(4):
        xi = lax.rem(x + d // 2, 2)
        yi = lax.rem(y + d % 2, 2)
        start = 0
        at = 0
        for rows, paired in sizes:
            total = keeps[at][xi, 0, yi].astype(F32) + gots[at][xi, 0, yi].astype(F32)
            at += 1
            if paired:
                total += keeps[at][xi, 0, yi].astype(F32) + gots[at][xi, 0, yi].astype(F32)
                at += 1
            split_store(outs[d], 0, start, rows, total, paired)
            start += rows * (2 if paired else 1)


def windows(sizes):
    start = 0
    for rows, paired in sizes:
        yield start, rows, paired
        start += rows * (2 if paired else 1)


def plane_sum_kernel(info, *refs, sizes):
    pieces, outs = refs[:4], refs[4:]
    z = info[0]
    for e in range(4):
        zi = lax.rem(z + e, 4)
        for start, rows, paired in windows(sizes):
            span = slice(start, start + rows)
            total = sum(piece[zi, span, :].astype(F32) for piece in pieces)
            if paired:
                span = slice(start + rows, start + 2 * rows)
                total += sum(piece[zi, span, :].astype(F32) for piece in pieces)
            if e == 0:
                outs[0][start : start + rows, :] = total
            else:
                high = total.astype(LOW)
                outs[e][start : start + rows, :] = high
                if paired:
                    rest = (total - high.astype(F32)).astype(LOW)
                    outs[e][start + rows : start + 2 * rows, :] = rest


def line_sum_kernel(info, keep, one, two, three, *outs, sizes, shapes):
    at = 0
    for (start, rows, paired), shape in zip(windows(sizes), shapes):
        span = slice(start, start + rows)
        total = keep[span, :]
        for piece in (one, two, three):
            total += piece[span, :].astype(F32)
            if paired:
                total += piece[start + rows : start + 2 * rows, :].astype(F32)
        if paired:
            quads = [total[:, CHAN * q : CHAN * (q + 1)] for q in range(4)]
            outs[at][0:SMALL, :] = quads[0][:, :48]
            outs[at][SMALL : 2 * SMALL - 1, :] = quads[1][: SMALL - 1, :48]
            outs[at + 1][0:SMALL, :] = quads[2][:, :32]
            outs[at + 1][SMALL : 2 * SMALL - 1, :] = quads[3][: SMALL - 1, :32]
            outs[at + 2][...] = quads[1][SMALL - 1 :, :]
            outs[at + 3][...] = quads[3][SMALL - 1 :, :]
            at += 4
        elif shape is None:
            owner = info[12]
            block = total[0:1, :]
            base = (owner // 8) * CHAN
            line = jnp.zeros((1, CHAN), F32)
            for b in range(WIDTH // CHAN):
                line = jnp.where(
                    base == b * CHAN, block[:, CHAN * b : CHAN * (b + 1)], line
                )
            lane = lax.broadcasted_iota(jnp.int32, (16, CHAN), 1)
            row = lax.broadcasted_iota(jnp.int32, (16, CHAN), 0)
            chosen = jnp.where(lane == row + 16 * lax.rem(owner, 8), line, 0.0)
            outs[at][...] = jnp.broadcast_to(
                jnp.sum(chosen, axis=1, keepdims=True), (16, CHAN)
            )
            at += 1
        else:
            height, width = shape
            for q in range(width // WIDTH):
                outs[at][:, WIDTH * q : WIDTH * (q + 1)] = total[height * q : height * (q + 1), :]
            at += 1


def scatter_chunk(pairs, sizes, shapes, spots):
    got = [lax.ppermute(send, "k", ring(2, 1)) for send, _ in pairs]
    keep = [own for _, own in pairs]
    inputs = [array.reshape(2, 4, 2, array.shape[2], WIDTH) for array in keep + got]
    total = sum(array.shape[3] for array in inputs) // 2
    in_specs = [
        pl.BlockSpec((2, 1, 2, array.shape[3], WIDTH), lambda i, _: (0, i, 0, 0, 0))
        for array in inputs
    ]
    out_specs = [pl.BlockSpec((1, total, WIDTH), lambda i, _: (i, 0, 0))] * 4
    own, *rest = local_call(
        functools.partial(core_sum_kernel, sizes=sizes),
        inputs,
        [((4, total, WIDTH), LOW)] * 4,
        [],
        spots,
        grid=(4,),
        specs=(in_specs, out_specs),
    )
    rest = [
        lax.ppermute(array, ("x", "y"), [(i, i ^ d) for i in range(4)])
        for d, array in zip((1, 2, 3), rest)
    ]
    own, *rest = local_call(
        functools.partial(plane_sum_kernel, sizes=sizes),
        [own] + rest,
        [((total, WIDTH), F32)] + [((total, WIDTH), LOW)] * 3,
        [],
        spots,
    )
    rest = [lax.ppermute(array, "z", ring(4, d)) for d, array in zip((1, 2, 3), rest)]
    outputs = []
    for (_, paired), shape in zip(sizes, shapes):
        if paired:
            outputs += [((31, 48), F32), ((31, 32), F32), ((1, CHAN), F32), ((1, CHAN), F32)]
        elif shape is None:
            outputs.append(((16, CHAN), F32))
        else:
            outputs.append((shape, F32))
    return local_call(
        functools.partial(line_sum_kernel, sizes=sizes, shapes=shapes),
        [own] + rest,
        outputs,
        [],
        spots,
    )


def grid_device(
    features, cotangent, lengths, front_up, front_down, heads_input, heads_output, gated_input,
    gated_output, merge_output, rear_up, rear_down, gate_kernel, merge_kernel, front_gain,
    heads_gain, gated_gain, gate_gain, rear_gain, final_gain,
):
    x, k, z, y = (lax.axis_index(name) for name in ("x", "k", "z", "y"))
    places = [z, z + 3, z + 2, z + 1]
    places = [lax.rem(place, 4) for place in places]
    for dx, dy in ((0, 0), (0, 1), (1, 0), (1, 1)):
        places += [lax.rem(x + dx, 2), lax.rem(y + dy, 2)]
    places.append(((x * 2 + k) * 4 + z) * 2 + y)
    spots = jnp.stack([place.astype(jnp.int32) for place in places])
    mine = k.astype(jnp.int32)
    taps = gate_kernel.shape[0]

    def tall(element):
        return jnp.pad(element, ((0, 1), (0, CHAN - element.shape[1])))

    gains = jnp.concatenate([front_gain, heads_gain, gated_gain, rear_gain, final_gain, gate_gain])
    front, middle, rear = local_call(
        pack_kernel,
        [
            front_up, front_down, heads_input, heads_output, gated_input, gated_output,
            merge_output, rear_up, rear_down, tall(gate_kernel), tall(merge_kernel),
            gains.reshape(1, -1),
        ],
        [((144, WIDTH), LOW), ((208, WIDTH), LOW), ((160, WIDTH), LOW)],
        [],
        spots,
    )
    front = gather_chunk(front, spots)
    middle = gather_chunk(middle, spots)
    rear = gather_chunk(rear, spots)
    small_specs = [pl.BlockSpec((2, 8, SMALL, WIDTH), lambda *_: (0, 0, 8, 0))] * 2
    small_shapes = [((32, 3 * WIDTH), F32), ((32, 2 * WIDTH), F32), ((8, WIDTH), F32), ((1, 3 * WIDTH), F32)]
    gate_taps, merge_taps, gains, gate_full = local_call(
        unpack_kernel,
        list(front),
        small_shapes,
        [],
        mine.reshape(1),
        specs=(small_specs, [whole(shape) for shape, _ in small_shapes]),
    )
    lines = [gains[g : g + 1] for g in range(5)]
    smaller = (gate_taps, merge_taps, lines[0], lines[1], lines[2], gate_full, lines[3], lines[4])
    encoded, features_grad, info, stats, weight_halves, small_grads = layer(
        features, cotangent, lengths[0], mine, front, middle, rear, smaller, taps
    )
    front_halves, heads_halves, gated_halves, merge_halves, rear_halves = weight_halves
    count_at = 1 + 2 * lengths.shape[1]
    small_high_low = local_call(
        functools.partial(pack_small_kernel, count_at=count_at),
        list(small_grads) + list(stats),
        [((2, 8, SMALL, WIDTH), LOW)] * 4,
        [],
        info,
    )

    def by_two(arrays):
        return [tuple(arrays[i : i + 2]) for i in range(0, len(arrays), 2)]

    rear_up_grad, rear_down_grad, merge_output_grad = scatter_chunk(
        by_two(rear_halves) + by_two(merge_halves),
        ((64, False), (64, False), (32, False)),
        (rear_up.shape, rear_down.shape, merge_output.shape),
        spots,
    )
    (
        heads_input_grad, heads_output_grad, gated_input_grad, gated_output_grad,
        gate_kernel_grad, merge_kernel_grad, gain_line, stat_line,
    ) = scatter_chunk(
        by_two(heads_halves) + by_two(gated_halves) + by_two(small_high_low),
        ((48, False), (16, False), (96, False), (48, False), (16, True)),
        (heads_input.shape, heads_output.shape, gated_input.shape, gated_output.shape, None),
        spots,
    )
    front_gain_grad, front_up_grad, front_down_grad = scatter_chunk(
        by_two(front_halves),
        ((16, False), (64, False), (64, False)),
        (None, front_up.shape, front_down.shape),
        spots,
    )
    line = gain_line[0]
    statistics = jnp.sqrt(stat_line[0, :7] / (stat_line[0, 7] * features.shape[1]))
    return (
        encoded, features_grad, front_up_grad, front_down_grad, heads_input_grad,
        heads_output_grad, gated_input_grad, gated_output_grad, merge_output_grad, rear_up_grad,
        rear_down_grad, gate_kernel_grad, merge_kernel_grad, front_gain_grad[:, 0], line[16:32],
        line[32:48], line[80:128], line[48:64], line[64:80], statistics,
    )


def pack_rows(shard):
    rows, columns = shard.shape
    pieces = shard.reshape(rows, columns // WIDTH, WIDTH).transpose(1, 0, 2)
    return pieces.reshape(rows * columns // WIDTH, WIDTH)


def pad_lines(flat):
    rows = -(-flat.shape[-1] // (WIDTH * 16)) * 16
    spare = [(0, 0)] * (flat.ndim - 1) + [(0, rows * WIDTH - flat.shape[-1])]
    return jnp.pad(flat, spare).reshape(flat.shape[:-1] + (rows, WIDTH))


def to_owners(weight):
    rows, columns = weight.shape
    pieces = weight.reshape(BLOCKS, rows // BLOCKS, columns // WIDTH, WIDTH)
    pieces = pieces.transpose(0, 2, 1, 3).reshape(2, 2, 8, -1, WIDTH)
    return pieces[:, 0], pieces[:, 1]


def from_owners(halves, rows, columns):
    send, keep = halves
    pieces = jnp.stack([keep, send], axis=1)
    pieces = pieces.reshape(BLOCKS, columns // WIDTH, rows // BLOCKS, WIDTH)
    return pieces.transpose(0, 2, 1, 3).reshape(rows, columns)


def any_device(features, cotangent, lengths, *shards, axes):
    count = lax.axis_size(axes)
    matrices, smaller = shards[:9], shards[9:]
    packed = [pack_rows(element) for element in matrices]
    packed.append(pad_lines(jnp.concatenate([element.reshape(-1) for element in smaller])))
    gathered = lax.all_gather(jnp.concatenate(packed), axes, axis=0)
    weights = []
    start = 0
    for element, piece in zip(matrices, packed):
        rows, columns = element.shape
        window = gathered[:, start : start + piece.shape[0]]
        start += piece.shape[0]
        window = window.reshape(count, columns // WIDTH, rows, WIDTH).transpose(0, 2, 1, 3)
        weights.append(to_owners(window.reshape(count * rows, columns)))
    flat = gathered[:, start:].reshape(count, -1).astype(F32)
    lines = []
    start = 0
    for element in smaller:
        window = flat[:, start : start + element.size]
        start += element.size
        if element.ndim == 2:
            window = window.reshape((count,) + element.shape).transpose(1, 0, 2)
            window = window.reshape(element.shape[0], -1)
            lines.append(jnp.pad(window, ((0, 1), (0, 0))))
        else:
            lines.append(window.reshape(1, -1))
    up, down, h_in, h_out, g_in, g_out, m_out, r_up, r_down = weights

    def chunk(*members):
        return tuple(jnp.concatenate([member[i] for member in members], axis=2) for i in (0, 1))

    encoded, features_grad, info, stats, halves, small_grads = layer(
        features, cotangent, lengths[0], jnp.int32(0), chunk(up, down),
        chunk(g_in, g_out, h_in, h_out), chunk(r_up, r_down, m_out), lines, smaller[0].shape[0],
    )
    front, heads, gated, merge, rear = halves
    front_gain = front[1][0, 0, 0].astype(F32)
    ordered = (front[2:4], front[4:6], heads[:2], heads[2:], gated[:2], gated[2:], merge, rear[:2], rear[2:])
    pieces = []
    for element, halves in zip(matrices, ordered):
        rows, columns = element.shape
        full = from_owners(halves, rows * count, columns)
        full = full.reshape(count, rows, columns // WIDTH, WIDTH).transpose(0, 2, 1, 3)
        pieces.append(full.reshape(count, -1, WIDTH))
    gate_taps, merge_taps, heads_gain, gated_gain, rear_gain, final_gain, gate_gain = small_grads
    small_full = (gate_taps, merge_taps, front_gain, heads_gain, gated_gain, gate_gain, rear_gain, final_gain)
    flat = []
    for element, full in zip(smaller, small_full):
        if element.ndim == 2:
            full = full[: element.shape[0]].reshape(element.shape[0], count, -1).transpose(1, 0, 2)
        flat.append(full.reshape(count, -1))
    pieces.append(pad_lines(jnp.concatenate(flat, axis=1).astype(LOW)))
    summed = lax.psum_scatter(jnp.concatenate(pieces, axis=1), axes, scatter_dimension=0)
    outputs = []
    start = 0
    for element, piece in zip(matrices, pieces):
        rows, columns = element.shape
        window = summed[start : start + piece.shape[1]].astype(F32)
        start += piece.shape[1]
        window = window.reshape(columns // WIDTH, rows, WIDTH).transpose(1, 0, 2)
        outputs.append(window.reshape(rows, columns))
    flat = summed[start:].reshape(-1).astype(F32)
    start = 0
    for element in smaller:
        outputs.append(flat[start : start + element.size].reshape(element.shape))
        start += element.size
    front_stat, merge_stat, rear_stat = stats
    squares = jnp.stack(
        [
            front_stat[0], front_stat[1], merge_stat[0], rear_stat[0], front_stat[2],
            merge_stat[1], rear_stat[1],
        ]
    )
    totals = lax.psum(
        jnp.append(jnp.sum(squares, axis=1), jnp.sum(lengths).astype(F32)), axes
    )
    statistics = jnp.sqrt(totals[:7] / (totals[7] * features.shape[1]))
    return (encoded, features_grad) + tuple(outputs) + (statistics,)


def solution(mesh):
    body = grid_device
    axes = ("x", "k", "z", "y")
    if mesh.devices.shape == (4, 8):
        mesh = Mesh(mesh.devices.reshape(2, 2, 4, 2), axes)
    else:
        axes = tuple(mesh.axis_names)
        body = functools.partial(any_device, axes=axes)
    rows, columns, vector = P(axes, None), P(None, axes), P(axes)
    weights = (rows,) * 9 + (columns,) * 2 + (vector,) * 6
    return jax.shard_map(
        body,
        mesh=mesh,
        in_specs=(rows, rows, rows) + weights,
        out_specs=(rows, rows) + weights + (P(),),
        check_vma=False,
    )
```

time: 1240 us -> 471 us (0.38)
  local copies, waits for them, and re-layouts: 471 us -> 22.7 us
  waiting for transfers between devices: 417 us -> 196 us
  other arithmetic: 203 us -> 1.59 us
  Pallas kernels: 0 us -> 182 us
  matrix products: 73.1 us -> 0 us
  starting transfers between devices: 0.08 us -> 57 us
  blocking collectives: 46.8 us -> 0 us
  between operations: 18.3 us -> 2.32 us
    reduce_scatter x1 -> x0, waiting for transfers between devices: 303 us -> none  [scatter_gradients(): lax.psum_scatter(jnp.concatenate(pieces, axis=1), AXES, scatter_dimension...]
    ppermute x0 -> x51, waiting for transfers between devices: none -> 196 us  [the longest x9 83.5 us: scatter_chunk(): lax.ppermute(array, ('x', 'y'), [(i, i ^ d) for i in range(4)])]
    pallas_call x0 -> x27, Pallas kernels: none -> 182 us  [the longest x9 153 us: call(): pl.pallas_call(kernel, grid_spec=pltpu.PrefetchScalarGridSpec(num_scalar_...]
    slice x90 -> x5, local copies, waits for them, and re-layouts: 133 us -> 2.99 us  [the longest x1 0.62 us: grid_device(): front_gain_grad[:, 0]]
    all_gather x1 -> x0, waiting for transfers between devices: 114 us -> none  [gather_weights(): gathered = lax.all_gather(jnp.concatenate(packed), AXES, axis=0)]
    unnamed x713 -> x78, local copies, waits for them, and re-layouts: 108 us -> 12.2 us
    reduce_sum x19 -> x1, other arithmetic: 93.3 us -> 0.09 us  [segment_table(): jnp.sum((position[None, :] >= ends[:, None]).astype(jnp.int32), axis=0)]
    another operation x65 -> x1, local copies, waits for them, and re-layouts: 89.1 us -> 0.09 us  [grid_device(): spots = jnp.stack([place.astype(jnp.int32) for place in places])]
  transfers between devices with their start and end apart: 2 -> 51, of which waited for: 2 -> 22; matrix products, arithmetic and copies ran while one was open for 1% -> 1% of each run, Pallas kernels for 0% -> 14%
where the time goes in v1:
time: 471 us; the launch traced here: 462 us
  waiting for transfers between devices  196 us (42%)
  Pallas kernels  182 us (39%)
  starting transfers between devices  57 us (12%)
  local copies, waits for them, and re-layouts  22.7 us (5%)
    pallas_call x9, Pallas kernels, call(): pl.pallas_call(kernel, grid_spec=pltpu.PrefetchScalarGridSpec(num_scalar_...  153 us
    ppermute x9, waiting for transfers between devices, scatter_chunk(): lax.ppermute(array, ('x', 'y'), [(i, i ^ d) for i in range(4)])  83.5 us
    ppermute x9, waiting for transfers between devices, gather_chunk(): line = [shard] + [lax.ppermute(shard, 'z', ring(4, d)) for d in (1, 2, 3)]  43.8 us
    ppermute x9, waiting for transfers between devices, gather_chunk(): lax.ppermute(line, ('x', 'y'), [(i, i ^ d) for i in range(4)])  42.1 us
    pallas_call x18, Pallas kernels, local_call(): pl.pallas_call(kernel, grid_spec=pltpu.PrefetchScalarGridSpec(num_scalar_...  29.4 us
    ppermute x9, waiting for transfers between devices, scatter_chunk(): lax.ppermute(array, 'z', ring(4, d))  25.3 us
    ppermute x9, starting transfers between devices, gather_chunk(): line = [shard] + [lax.ppermute(shard, 'z', ring(4, d)) for d in (1, 2, 3)]  17.6 us
    ppermute x9, starting transfers between devices, scatter_chunk(): lax.ppermute(array, 'z', ring(4, d))  13.2 us
  transfers between devices with their start and end apart: 51, of which 22 were waited for; matrix products, arithmetic and copies ran while one was open for 1% of the time, Pallas kernels for 14%

profile of v1, /device:TPU:0, one launch (start us, length us, event | category | flops | bytes accessed | tf_op | source)
XLA Modules:
  0.0 461.7 jit_solution(12567483022674788809)
XLA Ops:
  25.0 12.4 %collective-permute-done.8.refs_2_ = bf16[208,512]{1,0:T(8,128)(2,1)S(1)} collective-permute-done((bf16[208,512]{1,0:T(8,128)(2,1)S(1)}, bf16[208,512]{1,0:T(8,128)(2,1)S(1)}, u32[]{:S(2)}, u32[]{:S(2)}) %collective-permute-start.8) | collective-permute-done | bytes 213024 | tf_op jit(solution)/shard_map/ppermute | solution.py:867
  48.9 5.8 %collective-permute-start = (bf16[144,512]{1,0:T(8,128)(2,1)S(1)}, bf16[144,512]{1,0:T(8,128)(2,1)S(1)}, u32[]{:S(2)}, u32[]{:S(2)}) collective-permute-start(bf16[144,512]{1,0:T(8,128)(2,1)S(1)} %get-tuple-element.119.refs_0_), channel_id=1, source_target_pairs={{0,2},{2,4},{4,6},{6,0},{1,3},{3,5},{5,7},{7,1},{8,10},{10,12},{12... | collective-permute-start | bytes 442376 | tf_op jit(solution)/shard_map/ppermute | solution.py:867
  62.0 18.3 %collective-permute-done.11.refs_2_ = bf16[4,208,512]{2,1,0:T(8,128)(2,1)S(1)} collective-permute-done((bf16[4,208,512]{2,1,0:T(8,128)(2,1)S(1)}, bf16[4,208,512]{2,1,0:T(8,128)(2,1)S(1)}, u32[]{:S(2)}, u32[]{:S(2)}) %collective-permute-start.11) | collective-permute-done | bytes 852000 | tf_op jit(solution)/shard_map/ppermute | solution.py:877
  82.7 6.3 %collective-permute-done.16.refs_3_ = bf16[160,512]{1,0:T(8,128)(2,1)S(1)} collective-permute-done((bf16[160,512]{1,0:T(8,128)(2,1)S(1)}, bf16[160,512]{1,0:T(8,128)(2,1)S(1)}, u32[]{:S(2)}, u32[]{:S(2)}) %collective-permute-start.16) | collective-permute-done | bytes 163872 | tf_op jit(solution)/shard_map/ppermute | solution.py:867
  91.8 7.2 %collective-permute-done.15.refs_2_ = bf16[160,512]{1,0:T(8,128)(2,1)S(1)} collective-permute-done((bf16[160,512]{1,0:T(8,128)(2,1)S(1)}, bf16[160,512]{1,0:T(8,128)(2,1)S(1)}, u32[]{:S(2)}, u32[]{:S(2)}) %collective-permute-start.15) | collective-permute-done | bytes 163872 | tf_op jit(solution)/shard_map/ppermute | solution.py:867
  99.0 7.1 %collective-permute-done.14.refs_1_ = bf16[160,512]{1,0:T(8,128)(2,1)S(1)} collective-permute-done((bf16[160,512]{1,0:T(8,128)(2,1)S(1)}, bf16[160,512]{1,0:T(8,128)(2,1)S(1)}, u32[]{:S(2)}, u32[]{:S(2)}) %collective-permute-start.14) | collective-permute-done | bytes 163872 | tf_op jit(solution)/shard_map/ppermute | solution.py:867
  113.2 13.0 %collective-permute-done.19.refs_3_ = bf16[4,160,512]{2,1,0:T(8,128)(2,1)S(1)} collective-permute-done((bf16[4,160,512]{2,1,0:T(8,128)(2,1)S(1)}, bf16[4,160,512]{2,1,0:T(8,128)(2,1)S(1)}, u32[]{:S(2)}, u32[]{:S(2)}) %collective-permute-start.19) | collective-permute-done | bytes 655392 | tf_op jit(solution)/shard_map/ppermute | solution.py:877
  126.2 9.8 %collective-permute-done.18.refs_2_ = bf16[4,160,512]{2,1,0:T(8,128)(2,1)S(1)} collective-permute-done((bf16[4,160,512]{2,1,0:T(8,128)(2,1)S(1)}, bf16[4,160,512]{2,1,0:T(8,128)(2,1)S(1)}, u32[]{:S(2)}, u32[]{:S(2)}) %collective-permute-start.18) | collective-permute-done | bytes 655392 | tf_op jit(solution)/shard_map/ppermute | solution.py:877
  145.3 8.0 %shard_map.351 = (f32[384,512]{1,0:T(8,128)}, f32[384,2048]{1,0:T(8,128)}, f32[8,512]{1,0:T(8,128)}) custom-call(s32[11]{0:T(128)} %concatenate.6.info, bf16[384,512]{1,0:T(8,128)(2,1)} %x_ref.3, f32[1,512]{1,0:T(1,128)} %get-tuple-element.222.gain, f32[384,1]{1,0:T(8,128)} %compare_convert_fusion.valid, bf16[2,8,144,512]{3,2,1,0:T(8,128)(2,1)} %bitcast.13.first.up.down, ...), custom_call_target="tpu_custom_call" | custom-call | flops 1610612736 | bytes 13782528 | tf_op jit(solution)/shard_map/pallas_call | solution.py:572
  153.3 9.0 %shard_map.354 = (f32[384,512]{1,0:T(8,128)}, bf16[384,1536]{1,0:T(8,128)(2,1)}, bf16[384,512]{1,0:T(8,128)(2,1)}) custom-call(s32[11]{0:T(128)} %concatenate.6.info, f32[384,512]{1,0:T(8,128)} %get-tuple-element.121.x_ref, f32[1,512]{1,0:T(1,128)} %get-tuple-element.221.gain, s32[384,1]{1,0:T(8,128)} %reduce_sum.13.segs_col, ...), custom_call_target="tpu_custom_call" | custom-call | flops 1207959552 | bytes 16782336 | tf_op jit(solution)/shard_map/pallas_call | solution.py:572
  162.3 20.7 %shard_map.355 = (f32[384,512]{1,0:T(8,128)}, f32[384,3072]{1,0:T(8,128)}, f32[384,1536]{1,0:T(8,128)}, f32[384,1]{1,0:T(8,128)}, f32[384,1536]{1,0:T(8,128)}, /*index=5*/bf16[384,1536]{1,0:T(8,128)(2,1)}) custom-call(s32[11]{0:T(128)} %concatenate.6.info, f32[384,512]{1,0:T(8,128)} %get-tuple-element.121.x_ref, f32[1,512]{1,0:T(1,128)} %get-tuple-element.220.gain, ...), custom_call_target="tpu_custom_call" | custom-call | flops 3623878656 | bytes 26027520 | tf_op jit(solution)/shard_map/pallas_call | solution.py:572
  183.0 10.3 %shard_map.358 = (f32[384,512]{1,0:T(8,128)}, bf16[384,1024]{1,0:T(8,128)(2,1)}, f32[8,512]{1,0:T(8,128)}) custom-call(s32[11]{0:T(128)} %concatenate.6.info, f32[384,512]{1,0:T(8,128)} %get-tuple-element.121.x_ref, f32[384,512]{1,0:T(8,128)} %get-tuple-element.123.attended, f32[384,512]{1,0:T(8,128)} %get-tuple-element.126.gated, f32[32,1024]{1,0:T(8,128)} %copy-done.13, ...), custom_call_target="tpu_custom_call" | custom-call | flops 1610612736 | bytes 9324032 | tf_op jit(solution)/shard_map/pallas_call | solution.py:572
  193.3 18.1 %shard_map.359 = (bf16[384,512]{1,0:T(8,128)(2,1)}, f32[384,512]{1,0:T(8,128)}, f32[1,512]{1,0:T(1,128)}, f32[1,512]{1,0:T(1,128)}, f32[8,512]{1,0:T(8,128)}, /*...) custom-call(s32[11]{0:T(128)} %concatenate.6.info, ...), custom_call_target="tpu_custom_call" | custom-call | flops 5234491392 | bytes 17065472 | tf_op jit(solution)/shard_map/pallas_call | solution.py:572
  211.4 17.3 %shard_map.360 = (f32[384,512]{1,0:T(8,128)}, f32[384,512]{1,0:T(8,128)}, f32[32,1024]{1,0:T(8,128)}, bf16[2,8,32,512]{3,2,1,0:T(8,128)(2,1)}, bf16[2,8,32,512]{3,2,1,0:T(8,128)(2,1)}) custom-call(s32[11]{0:T(128)} %concatenate.6.info, f32[384,512]{1,0:T(8,128)} %get-tuple-element.131.grad, f32[384,512]{1,0:T(8,128)} %get-tuple-element.123.attended, ...), custom_call_target="tpu_custom_call" | custom-call | flops 3221225472 | bytes 11272192 | tf_op jit(solution)/shard_map/pallas_call | solution.py:572
  228.7 14.8 %shard_map.361 = (f32[384,512]{1,0:T(8,128)}, f32[1,512]{1,0:T(1,128)}, bf16[2,8,48,512]{3,2,1,0:T(8,128)(2,1)}, bf16[2,8,48,512]{3,2,1,0:T(8,128)(2,1)}, bf16[2...) custom-call(s32[11]{0:T(128)} %concatenate.6.info, f32[384,512]{1,0:T(8,128)} %get-tuple-element.133.grad, ...), custom_call_target="tpu_custom_call" | custom-call | flops 3221225472 | bytes 19662848 | tf_op jit(solution)/shard_map/pallas_call | solution.py:572
  243.5 40.5 %shard_map.362 = (f32[384,512]{1,0:T(8,128)}, f32[1,512]{1,0:T(1,128)}, f32[1,1536]{1,0:T(1,128)}, f32[32,1536]{1,0:T(8,128)}, bf16[2,8,96,512]{3,2,1,0:T(8,128)...) custom-call(s32[11]{0:T(128)} %concatenate.6.info, ...), custom_call_target="tpu_custom_call" | custom-call | flops 7247757312 | bytes 22487040 | tf_op jit(solution)/shard_map/pallas_call | solution.py:572
  284.2 14.1 %shard_map.363 = (bf16[384,512]{1,0:T(8,128)(2,1)}, bf16[2,8,16,512]{3,2,1,0:T(8,128)(2,1)}, bf16[2,8,16,512]{3,2,1,0:T(8,128)(2,1)}, bf16[2,8,64,512]{3,2,1,0:T...) custom-call(s32[11]{0:T(128)} %concatenate.6.info, ...), custom_call_target="tpu_custom_call" | custom-call | flops 3221225472 | bytes 20449280 | tf_op jit(solution)/shard_map/pallas_call | solution.py:572
  323.7 7.1 %collective-permute-done.24.refs_1_ = bf16[4,144,512]{2,1,0:T(8,128)(2,1)S(1)} collective-permute-done((bf16[4,144,512]{2,1,0:T(8,128)(2,1)S(1)}, bf16[4,144,512]{2,1,0:T(8,128)(2,1)S(1)}, u32[]{:S(2)}, u32[]{:S(2)}) %collective-permute-start.24) | collective-permute-done | bytes 589856 | tf_op jit(solution)/shard_map/ppermute | solution.py:1098
  333.0 11.1 %collective-permute-done.26.refs_3_ = bf16[4,144,512]{2,1,0:T(8,128)(2,1)S(1)} collective-permute-done((bf16[4,144,512]{2,1,0:T(8,128)(2,1)S(1)}, bf16[4,144,512]{2,1,0:T(8,128)(2,1)S(1)}, u32[]{:S(2)}, u32[]{:S(2)}) %collective-permute-start.26) | collective-permute-done | bytes 589856 | tf_op jit(solution)/shard_map/ppermute | solution.py:1098
  345.7 11.0 %collective-permute-done.45.refs_1_ = bf16[4,160,512]{2,1,0:T(8,128)(2,1)S(1)} collective-permute-done((bf16[4,160,512]{2,1,0:T(8,128)(2,1)S(1)}, bf16[4,160,512]{2,1,0:T(8,128)(2,1)S(1)}, u32[]{:S(2)}, u32[]{:S(2)}) %collective-permute-start.45) | collective-permute-done | bytes 655392 | tf_op jit(solution)/shard_map/ppermute | solution.py:1098
  359.0 40.4 %collective-permute-done.46.refs_2_ = bf16[4,160,512]{2,1,0:T(8,128)(2,1)S(1)} collective-permute-done((bf16[4,160,512]{2,1,0:T(8,128)(2,1)S(1)}, bf16[4,160,512]{2,1,0:T(8,128)(2,1)S(1)}, u32[]{:S(2)}, u32[]{:S(2)}) %collective-permute-start.46) | collective-permute-done | bytes 655392 | tf_op jit(solution)/shard_map/ppermute | solution.py:1098
  399.4 13.9 %collective-permute-done.47.refs_3_ = bf16[4,160,512]{2,1,0:T(8,128)(2,1)S(1)} collective-permute-done((bf16[4,160,512]{2,1,0:T(8,128)(2,1)S(1)}, bf16[4,160,512]{2,1,0:T(8,128)(2,1)S(1)}, u32[]{:S(2)}, u32[]{:S(2)}) %collective-permute-start.47) | collective-permute-done | bytes 655392 | tf_op jit(solution)/shard_map/ppermute | solution.py:1098
  420.4 12.5 %collective-permute-done.28.two = bf16[144,512]{1,0:T(8,128)(2,1)S(1)} collective-permute-done((bf16[144,512]{1,0:T(8,128)(2,1)S(1)}, bf16[144,512]{1,0:T(8,128)(2,1)S(1)}, u32[]{:S(2)}, u32[]{:S(2)}) %collective-permute-start.28) | collective-permute-done | bytes 147488 | tf_op jit(solution)/shard_map/ppermute | solution.py:1108
  442.9 12.8 %collective-permute-done.49.two = bf16[160,512]{1,0:T(8,128)(2,1)S(1)} collective-permute-done((bf16[160,512]{1,0:T(8,128)(2,1)S(1)}, bf16[160,512]{1,0:T(8,128)(2,1)S(1)}, u32[]{:S(2)}, u32[]{:S(2)}) %collective-permute-start.49) | collective-permute-done | bytes 163872 | tf_op jit(solution)/shard_map/ppermute | solution.py:1108
  (199 shorter events, 117.9 us)
Async XLA Ops:
  39.1 22.9 %collective-permute-start.12 = (bf16[4,208,512]{2,1,0:T(8,128)(2,1)S(1)}, bf16[4,208,512]{2,1,0:T(8,128)(2,1)S(1)}, u32[]{:S(2)}, u32[]{:S(2)}) collective-permute-start(bf16[4,208,512]{2,1,0:T(8,128)(2,1)S(1)} %shard_map.352.refs_0_), channel_id=1, source_target_pairs={{0,17},{1,16},{16,1},{17,0},{2,19},{3,18},{18,3},{19,2},{4,21},{5,... | collective-permute-start | bytes 2555912 | tf_op jit(solution)/shard_map/ppermute | solution.py:877
  41.6 38.7 %collective-permute-start.11 = (bf16[4,208,512]{2,1,0:T(8,128)(2,1)S(1)}, bf16[4,208,512]{2,1,0:T(8,128)(2,1)S(1)}, u32[]{:S(2)}, u32[]{:S(2)}) collective-permute-start(bf16[4,208,512]{2,1,0:T(8,128)(2,1)S(1)} %shard_map.352.refs_0_), channel_id=1, source_target_pairs={{0,16},{1,17},{16,0},{17,1},{2,18},{3,19},{18,2},{19,3},{4,20},{5,... | collective-permute-start | bytes 2555912 | tf_op jit(solution)/shard_map/ppermute | solution.py:877
  42.1 38.2 %collective-permute-start.10 = (bf16[4,208,512]{2,1,0:T(8,128)(2,1)S(1)}, bf16[4,208,512]{2,1,0:T(8,128)(2,1)S(1)}, u32[]{:S(2)}, u32[]{:S(2)}) collective-permute-start(bf16[4,208,512]{2,1,0:T(8,128)(2,1)S(1)} %shard_map.352.refs_0_), channel_id=1, source_target_pairs={{0,1},{1,0},{16,17},{17,16},{2,3},{3,2},{18,19},{19,18},{4,5},{5,4... | collective-permute-start | bytes 2555912 | tf_op jit(solution)/shard_map/ppermute | solution.py:877
  58.8 50.5 %collective-permute-start.5 = (bf16[4,144,512]{2,1,0:T(8,128)(2,1)S(1)}, bf16[4,144,512]{2,1,0:T(8,128)(2,1)S(1)}, u32[]{:S(2)}, u32[]{:S(2)}) collective-permute-start(bf16[4,144,512]{2,1,0:T(8,128)(2,1)S(1)} %shard_map.348.refs_0_), channel_id=1, source_target_pairs={{0,17},{1,16},{16,1},{17,0},{2,19},{3,18},{18,3},{19,2},{4,21},{5,... | collective-permute-start | bytes 1769480 | tf_op jit(solution)/shard_map/ppermute | solution.py:877
  61.3 48.5 %collective-permute-start.4 = (bf16[4,144,512]{2,1,0:T(8,128)(2,1)S(1)}, bf16[4,144,512]{2,1,0:T(8,128)(2,1)S(1)}, u32[]{:S(2)}, u32[]{:S(2)}) collective-permute-start(bf16[4,144,512]{2,1,0:T(8,128)(2,1)S(1)} %shard_map.348.refs_0_), channel_id=1, source_target_pairs={{0,16},{1,17},{16,0},{17,1},{2,18},{3,19},{18,2},{19,3},{4,20},{5,... | collective-permute-start | bytes 1769480 | tf_op jit(solution)/shard_map/ppermute | solution.py:877
  81.2 72.0 %collective-permute-start.13 = (bf16[2,8,208,512]{3,2,1,0:T(8,128)(2,1)S(1)}, bf16[2,8,208,512]{3,2,1,0:T(8,128)(2,1)}, u32[]{:S(2)}, u32[]{:S(2)}) collective-permute-start(bf16[2,8,208,512]{3,2,1,0:T(8,128)(2,1)S(1)} %bitcast.53), channel_id=1, source_target_pairs={{0,8},{8,0},{1,9},{9,1},{2,10},{10,2},{3,11},{11,3},{4,12},{12,4},... | collective-permute-start | bytes 10223624 | tf_op jit(solution)/shard_map/ppermute | solution.py:888
  81.3 29.8 %collective-permute-start.3 = (bf16[4,144,512]{2,1,0:T(8,128)(2,1)S(1)}, bf16[4,144,512]{2,1,0:T(8,128)(2,1)S(1)}, u32[]{:S(2)}, u32[]{:S(2)}) collective-permute-start(bf16[4,144,512]{2,1,0:T(8,128)(2,1)S(1)} %shard_map.348.refs_0_), channel_id=1, source_target_pairs={{0,1},{1,0},{16,17},{17,16},{2,3},{3,2},{18,19},{19,18},{4,5},{5,4... | collective-permute-start | bytes 1769480 | tf_op jit(solution)/shard_map/ppermute | solution.py:877
  109.2 26.8 %collective-permute-start.18 = (bf16[4,160,512]{2,1,0:T(8,128)(2,1)S(1)}, bf16[4,160,512]{2,1,0:T(8,128)(2,1)S(1)}, u32[]{:S(2)}, u32[]{:S(2)}) collective-permute-start(bf16[4,160,512]{2,1,0:T(8,128)(2,1)S(1)} %shard_map.356.refs_0_), channel_id=1, source_target_pairs={{0,16},{1,17},{16,0},{17,1},{2,18},{3,19},{18,2},{19,3},{4,20},{5,... | collective-permute-start | bytes 1966088 | tf_op jit(solution)/shard_map/ppermute | solution.py:877
  109.7 27.0 %collective-permute-start.17 = (bf16[4,160,512]{2,1,0:T(8,128)(2,1)S(1)}, bf16[4,160,512]{2,1,0:T(8,128)(2,1)S(1)}, u32[]{:S(2)}, u32[]{:S(2)}) collective-permute-start(bf16[4,160,512]{2,1,0:T(8,128)(2,1)S(1)} %shard_map.356.refs_0_), channel_id=1, source_target_pairs={{0,1},{1,0},{16,17},{17,16},{2,3},{3,2},{18,19},{19,18},{4,5},{5,4... | collective-permute-start | bytes 1966088 | tf_op jit(solution)/shard_map/ppermute | solution.py:877
  113.1 28.9 %collective-permute-start.6 = (bf16[2,8,144,512]{3,2,1,0:T(8,128)(2,1)}, bf16[2,8,144,512]{3,2,1,0:T(8,128)(2,1)}, u32[]{:S(2)}, u32[]{:S(2)}) collective-permute-start(bf16[2,8,144,512]{3,2,1,0:T(8,128)(2,1)} %bitcast.13.first.up.down), channel_id=1, source_target_pairs={{0,8},{8,0},{1,9},{9,1},{2,10},{10,2},{3,11},{11,3},{4,12},{12,4},... | collective-permute-start | bytes 7077896 | tf_op jit(solution)/shard_map/ppermute | solution.py:888
  138.8 44.2 %collective-permute-start.20 = (bf16[2,8,160,512]{3,2,1,0:T(8,128)(2,1)}, bf16[2,8,160,512]{3,2,1,0:T(8,128)(2,1)}, u32[]{:S(2)}, u32[]{:S(2)}) collective-permute-start(bf16[2,8,160,512]{3,2,1,0:T(8,128)(2,1)} %bitcast.15.weight.up.down), channel_id=1, source_target_pairs={{0,8},{8,0},{1,9},{9,1},{2,10},{10,2},{3,11},{11,3},{4,12},{12,4},... | collective-permute-start | bytes 7864328 | tf_op jit(solution)/shard_map/ppermute | solution.py:888
  317.7 39.0 %collective-permute-start.45 = (bf16[4,160,512]{2,1,0:T(8,128)(2,1)S(1)}, bf16[4,160,512]{2,1,0:T(8,128)(2,1)S(1)}, u32[]{:S(2)}, u32[]{:S(2)}) collective-permute-start(bf16[4,160,512]{2,1,0:T(8,128)(2,1)S(1)} %get-tuple-element.203), channel_id=1, source_target_pairs={{0,1},{1,0},{16,17},{17,16},{2,3},{3,2},{18,19},{19,18},{4,5},{5,4... | collective-permute-start | bytes 1966088 | tf_op jit(solution)/shard_map/ppermute | solution.py:1098
  319.2 25.0 %collective-permute-start.26 = (bf16[4,144,512]{2,1,0:T(8,128)(2,1)S(1)}, bf16[4,144,512]{2,1,0:T(8,128)(2,1)S(1)}, u32[]{:S(2)}, u32[]{:S(2)}) collective-permute-start(bf16[4,144,512]{2,1,0:T(8,128)(2,1)S(1)} %get-tuple-element.155), channel_id=1, source_target_pairs={{0,17},{1,16},{16,1},{17,0},{2,19},{3,18},{18,3},{19,2},{4,21},{5,... | collective-permute-start | bytes 1769480 | tf_op jit(solution)/shard_map/ppermute | solution.py:1098
  322.0 92.2 %collective-permute-start.36 = (bf16[4,240,512]{2,1,0:T(8,128)(2,1)S(1)}, bf16[4,240,512]{2,1,0:T(8,128)(2,1)S(1)}, u32[]{:S(2)}, u32[]{:S(2)}) collective-permute-start(bf16[4,240,512]{2,1,0:T(8,128)(2,1)S(1)} %get-tuple-element.185), channel_id=1, source_target_pairs={{0,1},{1,0},{16,17},{17,16},{2,3},{3,2},{18,19},{19,18},{4,5},{5,4... | collective-permute-start | bytes 2949128 | tf_op jit(solution)/shard_map/ppermute | solution.py:1098
  330.7 84.5 %collective-permute-start.37 = (bf16[4,240,512]{2,1,0:T(8,128)(2,1)S(1)}, bf16[4,240,512]{2,1,0:T(8,128)(2,1)S(1)}, u32[]{:S(2)}, u32[]{:S(2)}) collective-permute-start(bf16[4,240,512]{2,1,0:T(8,128)(2,1)S(1)} %get-tuple-element.186), channel_id=1, source_target_pairs={{0,16},{1,17},{16,0},{17,1},{2,18},{3,19},{18,2},{19,3},{4,20},{5,... | collective-permute-start | bytes 2949128 | tf_op jit(solution)/shard_map/ppermute | solution.py:1098
  332.3 85.8 %collective-permute-start.38 = (bf16[4,240,512]{2,1,0:T(8,128)(2,1)S(1)}, bf16[4,240,512]{2,1,0:T(8,128)(2,1)S(1)}, u32[]{:S(2)}, u32[]{:S(2)}) collective-permute-start(bf16[4,240,512]{2,1,0:T(8,128)(2,1)S(1)} %get-tuple-element.187), channel_id=1, source_target_pairs={{0,17},{1,16},{16,1},{17,0},{2,19},{3,18},{18,3},{19,2},{4,21},{5,... | collective-permute-start | bytes 2949128 | tf_op jit(solution)/shard_map/ppermute | solution.py:1098
  344.2 55.2 %collective-permute-start.46 = (bf16[4,160,512]{2,1,0:T(8,128)(2,1)S(1)}, bf16[4,160,512]{2,1,0:T(8,128)(2,1)S(1)}, u32[]{:S(2)}, u32[]{:S(2)}) collective-permute-start(bf16[4,160,512]{2,1,0:T(8,128)(2,1)S(1)} %get-tuple-element.204), channel_id=1, source_target_pairs={{0,16},{1,17},{16,0},{17,1},{2,18},{3,19},{18,2},{19,3},{4,20},{5,... | collective-permute-start | bytes 1966088 | tf_op jit(solution)/shard_map/ppermute | solution.py:1098
  356.7 56.7 %collective-permute-start.47 = (bf16[4,160,512]{2,1,0:T(8,128)(2,1)S(1)}, bf16[4,160,512]{2,1,0:T(8,128)(2,1)S(1)}, u32[]{:S(2)}, u32[]{:S(2)}) collective-permute-start(bf16[4,160,512]{2,1,0:T(8,128)(2,1)S(1)} %get-tuple-element.205), channel_id=1, source_target_pairs={{0,17},{1,16},{16,1},{17,0},{2,19},{3,18},{18,3},{19,2},{4,21},{5,... | collective-permute-start | bytes 1966088 | tf_op jit(solution)/shard_map/ppermute | solution.py:1098
  399.4 19.8 %collective-permute-start.27 = (bf16[144,512]{1,0:T(8,128)(2,1)S(1)}, bf16[144,512]{1,0:T(8,128)(2,1)S(1)}, u32[]{:S(2)}, u32[]{:S(2)}) collective-permute-start(bf16[144,512]{1,0:T(8,128)(2,1)S(1)} %get-tuple-element.157), channel_id=1, source_target_pairs={{0,2},{2,4},{4,6},{6,0},{1,3},{3,5},{5,7},{7,1},{8,10},{10,12},{12... | collective-permute-start | bytes 442376 | tf_op jit(solution)/shard_map/ppermute | solution.py:1108
  414.2 23.4 %collective-permute-start.48 = (bf16[160,512]{1,0:T(8,128)(2,1)S(1)}, bf16[160,512]{1,0:T(8,128)(2,1)S(1)}, u32[]{:S(2)}, u32[]{:S(2)}) collective-permute-start(bf16[160,512]{1,0:T(8,128)(2,1)S(1)} %get-tuple-element.207), channel_id=1, source_target_pairs={{0,2},{2,4},{4,6},{6,0},{1,3},{3,5},{5,7},{7,1},{8,10},{10,12},{12... | collective-permute-start | bytes 491528 | tf_op jit(solution)/shard_map/ppermute | solution.py:1108
  419.1 37.8 %collective-permute-start.39 = (bf16[240,512]{1,0:T(8,128)(2,1)S(1)}, bf16[240,512]{1,0:T(8,128)(2,1)S(1)}, u32[]{:S(2)}, u32[]{:S(2)}) collective-permute-start(bf16[240,512]{1,0:T(8,128)(2,1)S(1)} %get-tuple-element.189), channel_id=1, source_target_pairs={{0,2},{2,4},{4,6},{6,0},{1,3},{3,5},{5,7},{7,1},{8,10},{10,12},{12... | collective-permute-start | bytes 737288 | tf_op jit(solution)/shard_map/ppermute | solution.py:1108
  419.2 37.8 %collective-permute-start.40 = (bf16[240,512]{1,0:T(8,128)(2,1)S(1)}, bf16[240,512]{1,0:T(8,128)(2,1)S(1)}, u32[]{:S(2)}, u32[]{:S(2)}) collective-permute-start(bf16[240,512]{1,0:T(8,128)(2,1)S(1)} %get-tuple-element.190), channel_id=1, source_target_pairs={{0,4},{2,6},{4,0},{6,2},{1,5},{3,7},{5,1},{7,3},{8,12},{10,14},{12... | collective-permute-start | bytes 737288 | tf_op jit(solution)/shard_map/ppermute | solution.py:1108
  432.9 24.1 %collective-permute-start.41 = (bf16[240,512]{1,0:T(8,128)(2,1)S(1)}, bf16[240,512]{1,0:T(8,128)(2,1)S(1)}, u32[]{:S(2)}, u32[]{:S(2)}) collective-permute-start(bf16[240,512]{1,0:T(8,128)(2,1)S(1)} %get-tuple-element.191), channel_id=1, source_target_pairs={{0,6},{2,0},{4,2},{6,4},{1,7},{3,1},{5,3},{7,5},{8,14},{10,8},{12,... | collective-permute-start | bytes 737288 | tf_op jit(solution)/shard_map/ppermute | solution.py:1108
  432.9 22.8 %collective-permute-start.49 = (bf16[160,512]{1,0:T(8,128)(2,1)S(1)}, bf16[160,512]{1,0:T(8,128)(2,1)S(1)}, u32[]{:S(2)}, u32[]{:S(2)}) collective-permute-start(bf16[160,512]{1,0:T(8,128)(2,1)S(1)} %get-tuple-element.208), channel_id=1, source_target_pairs={{0,4},{2,6},{4,0},{6,2},{1,5},{3,7},{5,1},{7,3},{8,12},{10,14},{12... | collective-permute-start | bytes 491528 | tf_op jit(solution)/shard_map/ppermute | solution.py:1108
  (66 other events, 646.9 us)

commit v2 on v1

v2 whole, which is shorter than its diff:
```python
import functools

import jax
import jax.numpy as jnp
from jax import lax
from jax.experimental import pallas as pl
from jax.experimental.pallas import tpu as pltpu
from jax.sharding import Mesh, PartitionSpec as P

HEADS = 8
EPSILON = 1e-05
NEGATIVE = -1000000000.0
TILE = 8
GAP = 16
CHAN = 128
WIDTH = 512
BLOCKS = 32
F32 = jnp.float32
LOW = jnp.bfloat16


def dot(left, right):
    return jnp.dot(left, right, preferred_element_type=F32)


def dot_tn(left, right):
    return lax.dot_general(left, right, (((0,), (0,)), ((), ())), preferred_element_type=F32)


def dot_nt(left, right):
    return lax.dot_general(left, right, (((1,), (1,)), ((), ())), preferred_element_type=F32)


def normalize(values):
    centred = values - jnp.mean(values, axis=-1, keepdims=True)
    variance = jnp.mean(centred * centred, axis=-1, keepdims=True)
    inverse = lax.rsqrt(variance + EPSILON)
    return centred * inverse, inverse


def normalize_back(upstream, gain, normal, inverse):
    scaled = upstream * gain
    mean_scaled = jnp.mean(scaled, axis=-1, keepdims=True)
    mean_cross = jnp.mean(scaled * normal, axis=-1, keepdims=True)
    return inverse * (scaled - mean_scaled - normal * mean_cross)


def row_sum(values):
    return jnp.sum(values, axis=0, keepdims=True)


GELU_A = 0.7978845608028654
GELU_B = 0.044715


def gelu(v):
    return 0.5 * v * (1.0 + jnp.tanh(GELU_A * (v + GELU_B * v * v * v)))


def gelu_pair(v):
    square = v * v
    bend = jnp.tanh(GELU_A * (v + GELU_B * square * v))
    value = 0.5 * v * (1.0 + bend)
    slope = 0.5 * (1.0 + bend) + 0.5 * v * (1.0 - bend * bend) * (
        GELU_A * (1.0 + 3.0 * GELU_B * square)
    )
    return value, slope


def silu(v):
    return v * jax.nn.sigmoid(v)


def store_halves(value, send, keep, mine, rows, start):
    parts = value.astype(LOW).reshape(2, 2, 8, rows, WIDTH)

    @pl.when(mine == 0)
    def _():
        keep[:, :, pl.ds(start, rows), :] = parts[:, 0]
        send[:, :, pl.ds(start, rows), :] = parts[:, 1]

    @pl.when(mine == 1)
    def _():
        keep[:, :, pl.ds(start, rows), :] = parts[:, 1]
        send[:, :, pl.ds(start, rows), :] = parts[:, 0]


def join_rows(first, second, mine):
    cores = jnp.where(mine == 0, first, second), jnp.where(mine == 0, second, first)
    return jnp.concatenate(
        [core[2 * x + y, z] for x in (0, 1) for core in cores for z in range(4) for y in (0, 1)]
    )


def pick_rows(first, second, flag):
    chosen = jnp.where(flag, first, second)
    return jnp.concatenate([chosen[y, z] for z in range(4) for y in (0, 1)])


def visits(info, segments, body):
    for s in range(segments):
        begin, end = info[1 + s], info[1 + segments + s]

        def visit(i, _, s=s, begin=begin, end=end):
            row = i * TILE + lax.broadcasted_iota(jnp.int32, (TILE, CHAN), 0)
            inside = jnp.logical_and(row >= begin, row < end)
            body(s, pl.multiple_of(i * TILE, TILE), inside)
            return 0

        lax.fori_loop(begin // TILE, (end + TILE - 1) // TILE, visit, 0)


def spread(source, padded, info, segments, blocks):
    padded[...] = jnp.zeros_like(padded)

    def body(s, base, inside):
        for c in range(blocks):
            value = source[pl.ds(base, TILE), c * CHAN : (c + 1) * CHAN]
            padded[c, pl.ds(base + GAP * (s + 1), TILE), :] = jnp.where(inside, value, 0.0)

    visits(info, segments, body)


def unspread(padded, target, info, segments, blocks):
    def body(s, base, inside):
        for c in range(blocks):
            lanes = slice(c * CHAN, (c + 1) * CHAN)
            value = padded[c, pl.ds(base + GAP * (s + 1), TILE), :]
            target[pl.ds(base, TILE), lanes] = jnp.where(
                inside, value, target[pl.ds(base, TILE), lanes]
            )

    visits(info, segments, body)


def conv_rows(padded, kernel, out, blocks, row_block, taps, flip):
    half = (taps - 1) // 2
    steps = (padded.shape[1] - 2 * GAP) // row_block

    def body(step, _):
        c = step // steps
        base = (step % steps) * row_block + GAP
        lanes = pl.ds(pl.multiple_of(c * CHAN, CHAN), CHAN)
        total = jnp.zeros((row_block, CHAN), F32)
        for j in range(taps):
            shift = half - j if flip else j - half
            total += kernel[pl.ds(j, 1), lanes] * padded[c, pl.ds(base + shift, row_block), :]
        out[c, pl.ds(pl.multiple_of(base, TILE), row_block), :] = total
        return 0

    lax.fori_loop(0, blocks * steps, body, 0)


def conv_taps(padded_grad, padded, out, blocks, row_block, taps):
    half = (taps - 1) // 2
    steps = (padded.shape[1] - 2 * GAP) // row_block
    tiles = row_block // TILE

    def block(c, _):
        lanes = pl.ds(pl.multiple_of(c * CHAN, CHAN), CHAN)

        def body(step, sums):
            base = pl.multiple_of(step * row_block + GAP, TILE)
            grad = padded_grad[c, pl.ds(base, row_block), :]
            new = []
            for j in range(taps):
                term = grad * padded[c, pl.ds(base + j - half, row_block), :]
                new.append(sums[j] + jnp.sum(term.reshape(tiles, TILE, CHAN), axis=0))
            return tuple(new)

        zero = jnp.zeros((TILE, CHAN), F32)
        sums = lax.fori_loop(0, steps, body, (zero,) * taps)
        for j in range(taps):
            out[pl.ds(j, 1), lanes] = row_sum(sums[j])
        return 0

    lax.fori_loop(0, blocks, block, 0)


def front_forward_kernel(
    info, x_ref, gain, valid, up, up_two, down, down_two, out, before_out, stat, low, total
):
    h = pl.program_id(0)
    mine = info[0]
    up_value = join_rows(up[...], up_two[...], mine)
    down_value = pick_rows(down[...], down_two[...], h % 2 == mine)

    @pl.when(h == 0)
    def _():
        normal, _ = normalize(x_ref[...].astype(F32))
        low[...] = (normal * gain[...]).astype(LOW)
        total[...] = jnp.zeros_like(total)

    before = dot(low[...], up_value)
    before_out[...] = before
    total[...] += dot(silu(before).astype(LOW), down_value)

    @pl.when(h == pl.num_programs(0) - 1)
    def _():
        x = x_ref[...].astype(F32)
        part = 0.5 * total[...]
        after = x + part
        out[...] = after
        v = valid[...]
        stat[0:1, :] = row_sum(x * x * v)
        stat[1:2, :] = row_sum(after * after * v)
        stat[2:3, :] = row_sum(part * part * v)
        stat[3:, :] = jnp.zeros((5, WIDTH), F32)


def head_masks(segs_col, segs_row):
    allowed = segs_col == segs_row
    lane = lax.broadcasted_iota(jnp.int32, (1, CHAN), 1)
    return allowed, (lane < CHAN // 2, lane >= CHAN // 2)


def head_probs(query, key, allowed, scale):
    scores = jnp.where(allowed, dot_nt(query, key) * scale, NEGATIVE)
    exponent = jnp.exp(scores - jnp.max(scores, axis=-1, keepdims=True))
    return exponent / jnp.sum(exponent, axis=-1, keepdims=True)


def heads_forward_kernel(
    info, x_ref, gain, segs_col, segs_row, w_in, w_in_two, w_out, w_out_two,
    attended, packed, mixed,
):
    mine = info[0]
    scale = (WIDTH // HEADS) ** -0.5
    normal, _ = normalize(x_ref[...])
    low = (normal * gain[...]).astype(LOW)
    for q in range(3):
        rows = slice(16 * q, 16 * (q + 1))
        weight = join_rows(w_in[:, :, rows, :], w_in_two[:, :, rows, :], mine)
        packed[:, WIDTH * q : WIDTH * (q + 1)] = dot(low, weight).astype(LOW)
    allowed, halves = head_masks(segs_col[...], segs_row[...])

    def pair(p, _):
        lanes = [
            pl.ds(pl.multiple_of(WIDTH * q + CHAN * p, CHAN), CHAN) for q in range(3)
        ]
        query, key, value = (packed[:, lane] for lane in lanes)
        parts = []
        for half in halves:
            probs = head_probs(jnp.where(half, query, 0), key, allowed, scale)
            parts.append(dot(probs.astype(LOW), value))
        mixed[:, lanes[0]] = jnp.where(halves[0], parts[0], parts[1]).astype(LOW)
        return 0

    lax.fori_loop(0, HEADS // 2, pair, 0)
    attended[...] = dot(mixed[...], join_rows(w_out[...], w_out_two[...], mine))


def heads_backward_kernel(
    info, grad, x_ref, gain, segs_col, segs_row, packed, mixed, w_in, w_in_two, w_out, w_out_two,
    stream, gain_grad, send, keep, mixed_grad, packed_grad, low,
):
    scale = (WIDTH // HEADS) ** -0.5
    mine = info[0]
    attended_low = grad[...].astype(LOW)
    store_halves(dot_tn(mixed[...], attended_low), send, keep, mine, 16, 48)
    mixed_grad[...] = dot_nt(attended_low, join_rows(w_out[...], w_out_two[...], mine)).astype(LOW)
    normal, inverse = normalize(x_ref[...])
    low[...] = (normal * gain[...]).astype(LOW)
    allowed, halves = head_masks(segs_col[...], segs_row[...])

    def pair(p, _):
        lanes = [
            pl.ds(pl.multiple_of(WIDTH * q + CHAN * p, CHAN), CHAN) for q in range(3)
        ]
        query, key, value = (packed[:, lane] for lane in lanes)
        upstream = mixed_grad[:, lanes[0]]
        parts = []
        for half in halves:
            probs = head_probs(jnp.where(half, query, 0), key, allowed, scale)
            probs_grad = dot_nt(jnp.where(half, upstream, 0), value)
            value_grad = dot_tn(probs.astype(LOW), upstream)
            inner = jnp.sum(probs_grad * probs, axis=-1, keepdims=True)
            score_grad = (probs * (probs_grad - inner)).astype(LOW)
            query_grad = dot(score_grad, key) * scale
            key_grad = dot_tn(score_grad, query) * scale
            parts.append((query_grad, key_grad, value_grad))
        for q in range(3):
            packed_grad[:, lanes[q]] = jnp.where(halves[0], parts[0][q], parts[1][q]).astype(LOW)
        return 0

    lax.fori_loop(0, HEADS // 2, pair, 0)
    total = jnp.zeros(x_ref.shape, F32)
    for q in range(3):
        rows = slice(16 * q, 16 * (q + 1))
        weight = join_rows(w_in[:, :, rows, :], w_in_two[:, :, rows, :], mine)
        piece = packed_grad[:, WIDTH * q : WIDTH * (q + 1)]
        store_halves(dot_tn(low[...], piece), send, keep, mine, 16, 16 * q)
        total += dot_nt(piece, weight)
    gain_grad[...] = row_sum(total * normal)
    stream[...] = normalize_back(total, gain[...], normal, inverse)


def gated_forward_kernel(
    info, x_ref, gain, gate_gain, taps_ref, w_in, w_in_two, w_out, w_out_two,
    gated, before_out, normal_out, inverse_out, part_out, product,
    low, act, padded, conv, *, segments, row_block, taps,
):
    j = pl.program_id(0)
    thirds = WIDTH * 3

    @pl.when(j == 0)
    def _():
        normal, _ = normalize(x_ref[...])
        low[...] = (normal * gain[...]).astype(LOW)

    before = dot(low[...], join_rows(w_in[...], w_in_two[...], info[0]))
    before_out[...] = before
    value = gelu(before)

    @pl.when(j < 3)
    def _():
        act[:, pl.ds(pl.multiple_of(j * WIDTH, WIDTH), WIDTH)] = value

    @pl.when(j == 2)
    def _():
        normal, inverse = normalize(act[...])
        normal_out[...] = normal
        inverse_out[...] = inverse
        act[...] = normal * gate_gain[...]
        blocks = thirds // CHAN
        spread(act, padded, info, segments, blocks)
        conv_rows(padded, taps_ref, conv, blocks, row_block, taps, False)
        unspread(conv, part_out, info, segments, blocks)

    @pl.when(j >= 3)
    def _():
        lanes = pl.ds(pl.multiple_of((j - 3) * WIDTH, WIDTH), WIDTH)
        product[:, lanes] = (value * part_out[:, lanes]).astype(LOW)

    @pl.when(j == 5)
    def _():
        gated[...] = dot(product[...], join_rows(w_out[...], w_out_two[...], info[0]))


def gated_linear_kernel(
    info, grad, x_ref, gain, before, part, product, w_in, w_in_two, w_out, w_out_two,
    part_grad, total_out, send, keep, low, product_grad, gated_low,
):
    j = pl.program_id(0)
    mine = info[0]

    @pl.when(j == 0)
    def _():
        normal, _ = normalize(x_ref[...])
        low[...] = (normal * gain[...]).astype(LOW)
        total_out[...] = jnp.zeros_like(total_out)
        gated_low[...] = grad[...].astype(LOW)
        store_halves(dot_tn(product[...], gated_low[...]), send, keep, mine, 48, 48)
        product_grad[...] = dot_nt(gated_low[...], join_rows(w_out[...], w_out_two[...], mine))

    value, slope = gelu_pair(before[...])
    lanes = pl.ds(pl.multiple_of(j * WIDTH, WIDTH), WIDTH)
    upstream = product_grad[:, lanes]
    part_grad[...] = upstream * value
    before_grad = (upstream * part[...] * slope).astype(LOW)
    store_halves(
        dot_tn(low[...], before_grad), send, keep, mine, 16, pl.multiple_of(j * 16, 16)
    )
    total_out[...] += dot_nt(before_grad, join_rows(w_in[...], w_in_two[...], mine))


def gated_conv_kernel(
    info, part_grad, normal_ref, inverse_ref, gate_gain, taps_ref,
    gate_grad, gate_gain_grad, taps_grad, padded, padded_grad, conv, work,
    *, segments, row_block, taps,
):
    blocks = 3 * WIDTH // CHAN
    spread(part_grad, padded_grad, info, segments, blocks)
    work[...] = normal_ref[...] * gate_gain[...]
    spread(work, padded, info, segments, blocks)
    conv_taps(padded_grad, padded, taps_grad, blocks, row_block, taps)
    conv_rows(padded_grad, taps_ref, conv, blocks, row_block, taps, True)
    unspread(conv, work, info, segments, blocks)
    upstream = work[...]
    normal = normal_ref[...]
    gate_gain_grad[...] = row_sum(upstream * normal)
    gate_grad[...] = normalize_back(upstream, gate_gain[...], normal, inverse_ref[...])


def gated_gate_kernel(
    info, gate_grad, x_ref, gain, before, total_in, w_in, w_in_two,
    stream, gain_grad, send, keep, low, total,
):
    j = pl.program_id(0)
    mine = info[0]

    @pl.when(j == 0)
    def _():
        normal, _ = normalize(x_ref[...])
        low[...] = (normal * gain[...]).astype(LOW)
        total[...] = total_in[...]

    _, slope = gelu_pair(before[...])
    before_grad = (gate_grad[...] * slope).astype(LOW)
    store_halves(
        dot_tn(low[...], before_grad), send, keep, mine, 16, pl.multiple_of(j * 16, 16)
    )
    total[...] += dot_nt(before_grad, join_rows(w_in[...], w_in_two[...], mine))

    @pl.when(j == 2)
    def _():
        normal, inverse = normalize(x_ref[...])
        gain_grad[...] = row_sum(total[...] * normal)
        stream[...] = normalize_back(total[...], gain[...], normal, inverse)


def merge_forward_kernel(
    info, x_ref, attended, gated, taps_ref, valid, weight, weight_two,
    out, merged_low, stat, joined, padded, conv, *, segments, row_block, taps,
):
    blocks = 2 * WIDTH // CHAN
    joined[:, :WIDTH] = attended[...]
    joined[:, WIDTH:] = gated[...]
    spread(joined, padded, info, segments, blocks)
    conv_rows(padded, taps_ref, conv, blocks, row_block, taps, False)
    for c in range(blocks):
        conv[c] += padded[c]
    unspread(conv, joined, info, segments, blocks)
    merged_low[...] = joined[...].astype(LOW)
    part = dot(merged_low[...], join_rows(weight[...], weight_two[...], info[0]))
    after = x_ref[...] + part
    out[...] = after
    v = valid[...]
    stat[0:1, :] = row_sum(after * after * v)
    stat[1:2, :] = row_sum(part * part * v)
    stat[2:, :] = jnp.zeros((6, WIDTH), F32)


def merge_backward_kernel(
    info, grad, attended, gated, merged_low, taps_ref, weight, weight_two,
    attended_grad, gated_grad, taps_grad, send, keep,
    joined, padded, padded_grad, conv, *, segments, row_block, taps,
):
    blocks = 2 * WIDTH // CHAN
    low = grad[...].astype(LOW)
    store_halves(dot_tn(merged_low[...], low), send, keep, info[0], 32, 0)
    joined[:, :WIDTH] = attended[...]
    joined[:, WIDTH:] = gated[...]
    spread(joined, padded, info, segments, blocks)
    joined[...] = dot_nt(low, join_rows(weight[...], weight_two[...], info[0]))
    spread(joined, padded_grad, info, segments, blocks)
    conv_taps(padded_grad, padded, taps_grad, blocks, row_block, taps)
    conv_rows(padded_grad, taps_ref, conv, blocks, row_block, taps, True)
    for c in range(blocks):
        conv[c] += padded_grad[c]
    unspread(conv, joined, info, segments, blocks)
    attended_grad[...] = joined[:, :WIDTH]
    gated_grad[...] = joined[:, WIDTH:]


def hidden_back(h, mine, before, part_low, down, send, keep, start):
    gate = jax.nn.sigmoid(before)
    hidden = (before * gate).astype(LOW)
    hidden_grad = dot_nt(part_low, down)
    before_grad = (hidden_grad * (gate * (1.0 + before * (1.0 - gate)))).astype(LOW)
    down_grad = dot_tn(hidden, part_low).astype(LOW).reshape(8, 64, WIDTH)

    @pl.when(h % 2 == mine)
    def _():
        keep[h // 2, :, start : start + 64, :] = down_grad

    @pl.when(h % 2 != mine)
    def _():
        send[h // 2, :, start : start + 64, :] = down_grad

    return before_grad


def rear_kernel(
    info, x_ref, gain, final_gain, valid, cotangent, up, up_two, down, down_two,
    encoded, stream, gain_grad, final_gain_grad, stat,
    send, keep, low, before, part_grad, stream_grad, total,
):
    step = pl.program_id(0)
    h = jnp.where(step < 4, step, 7 - step)
    up_value = join_rows(up[...], up_two[...], info[0])
    down_value = pick_rows(down[...], down_two[...], h % 2 == info[0])

    @pl.when(step == 0)
    def _():
        normal, _ = normalize(x_ref[...])
        low[...] = (normal * gain[...]).astype(LOW)
        total[...] = jnp.zeros_like(total)

    @pl.when(step < 4)
    def _():
        value = dot(low[...], up_value)
        before[step] = value
        total[...] += dot(silu(value).astype(LOW), down_value)

    @pl.when(step == 3)
    def _():
        part = 0.5 * total[...]
        after = x_ref[...] + part
        v = valid[...]
        stat[0:1, :] = row_sum(after * after * v)
        stat[1:2, :] = row_sum(part * part * v)
        stat[2:, :] = jnp.zeros((6, WIDTH), F32)
        normal, inverse = normalize(after)
        encoded[...] = (normal * final_gain[...] * v).astype(LOW)
        upstream = cotangent[...].astype(F32) * v
        final_gain_grad[...] = row_sum(upstream * normal)
        grad = normalize_back(upstream, final_gain[...], normal, inverse)
        stream_grad[...] = grad
        part_grad[...] = (0.5 * grad).astype(LOW)
        total[...] = jnp.zeros_like(total)

    @pl.when(step >= 4)
    def _():
        before_grad = hidden_back(
            h, info[0], before[h], part_grad[...], down_value, send, keep, 64
        )
        store_halves(
            dot_tn(low[...], before_grad), send, keep, info[0], 16, pl.multiple_of(h * 16, 16)
        )
        total[...] += dot_nt(before_grad, up_value)

    @pl.when(step == 7)
    def _():
        normal, inverse = normalize(x_ref[...])
        gain_grad[...] = row_sum(total[...] * normal)
        stream[...] = stream_grad[...] + normalize_back(total[...], gain[...], normal, inverse)


def front_hidden_kernel(
    info, grad, heads_stream, gated_stream, before, down, down_two,
    stream_out, before_grad, send, keep, part_grad,
):
    h = pl.program_id(0)

    @pl.when(h == 0)
    def _():
        stream_sum = grad[...] + heads_stream[...] + gated_stream[...]
        stream_out[...] = stream_sum
        part_grad[...] = (0.5 * stream_sum).astype(LOW)

    down_value = pick_rows(down[...], down_two[...], h % 2 == info[0])
    before_grad[...] = hidden_back(
        h, info[0], before[...], part_grad[...], down_value, send, keep, 0
    )


def front_input_kernel(
    info, stream_grad, before_grad, x_ref, gain, up, up_two,
    x_grad, send, keep, low, total,
):
    h = pl.program_id(0)

    @pl.when(h == 0)
    def _():
        normal, _ = normalize(x_ref[...].astype(F32))
        low[...] = (normal * gain[...]).astype(LOW)
        total[...] = jnp.zeros_like(total)

    store_halves(
        dot_tn(low[...], before_grad[...]), send, keep, info[0], 16, pl.multiple_of(h * 16, 16)
    )
    total[...] += dot_nt(before_grad[...], join_rows(up[...], up_two[...], info[0]))

    @pl.when(h == 3)
    def _():
        normal, inverse = normalize(x_ref[...].astype(F32))
        gain_grad = row_sum(total[...] * normal).astype(LOW)
        gain_rows = jnp.broadcast_to(gain_grad.reshape(1, 1, 1, WIDTH), (2, 8, 16, WIDTH))
        send[:, :, 64:80, :] = gain_rows
        keep[:, :, 64:80, :] = gain_rows
        x_grad[...] = (
            stream_grad[...] + normalize_back(total[...], gain[...], normal, inverse)
        ).astype(LOW)


def whole(shape):
    return pl.BlockSpec(shape, lambda *_: (0,) * len(shape))


def call(kernel, grid, inputs, outputs, scratch, info, flops=0, after=()):
    in_specs = [
        whole(array.shape) if block is None else pl.BlockSpec(block, index)
        for array, block, index in inputs
    ]
    out_specs = [
        whole(shape) if block is None else pl.BlockSpec(block, index)
        for shape, _, block, index in outputs
    ]
    arrays = [array for array, _, _ in inputs]
    shapes = [jax.ShapeDtypeStruct(shape, kind) for shape, kind, _, _ in outputs]
    moved = sum(array.size * array.dtype.itemsize for array in arrays)
    moved = sum(shape.size * shape.dtype.itemsize for shape in shapes) + min(moved, 1 << 24)
    skipped = len(after)
    name = getattr(kernel, "func", kernel).__name__

    def body(info_ref, *refs):
        kernel(info_ref, *refs[skipped:])

    return pl.pallas_call(
        body,
        grid_spec=pltpu.PrefetchScalarGridSpec(
            num_scalar_prefetch=1,
            grid=grid,
            in_specs=[pl.BlockSpec(memory_space=pl.ANY)] * skipped + in_specs,
            out_specs=out_specs,
            scratch_shapes=scratch,
        ),
        out_shape=shapes,
        name=name,
        compiler_params=pltpu.CompilerParams(vmem_limit_bytes=56 * 1024 * 1024),
        cost_estimate=pl.CostEstimate(flops=flops, bytes_accessed=moved, transcendentals=0),
    )(info, *after, *arrays)


def segment_table(lengths, mine, row_count):
    ends = jnp.cumsum(lengths)
    position = jnp.arange(row_count, dtype=jnp.int32)
    segments = jnp.sum((position[None, :] >= ends[:, None]).astype(jnp.int32), axis=0)
    zero = jnp.zeros((1,), jnp.int32)
    last = jnp.full((1,), row_count, jnp.int32)
    info = jnp.concatenate([jnp.full((1,), mine, jnp.int32), zero, ends, ends, last])
    return segments, info.astype(jnp.int32)


def all_of(*arrays):
    return [(array, None, None) for array in arrays]


def plain(*shapes_and_types):
    return [(shape, kind, None, None) for shape, kind in shapes_and_types]


def halves(rows):
    return plain(((2, 8, rows, WIDTH), LOW)) * 2


def columns(pair, rows, start, index):
    block = (4, 4, rows, WIDTH), lambda *i: (0, 0, start // rows + index(*i), 0)
    return [(array, *block) for array in pair]


def lines(pair, index):
    block = (2, 4, 64, WIDTH), lambda *i: (index(*i) // 2, 0, 1, 0)
    return [(array, *block) for array in pair]


def first(*_):
    return 0


def step(h, _):
    return h


class Layer:
    def __init__(self, features, cotangent, lengths, mine, taps):
        self.features, self.cotangent, self.taps = features, cotangent, taps
        self.tokens = features.shape[0]
        self.count = lengths.shape[0]
        self.segments = self.count + 1
        seg_ids, self.info = segment_table(lengths, mine, self.tokens)
        self.segs_col, self.segs_row = seg_ids[:, None], seg_ids[None, :]
        self.valid = (self.segs_col < self.count).astype(F32)
        self.stream = ((self.tokens, WIDTH), F32)
        self.low = pltpu.VMEM((self.tokens, WIDTH), LOW)
        self.wide = pltpu.VMEM((self.tokens, WIDTH), F32)
        self.spread_rows = self.tokens + GAP * (self.segments + 1)
        self.conv = dict(
            segments=self.segments, row_block=(self.spread_rows - 2 * GAP) // 4, taps=taps
        )
        self.stat = ((8, WIDTH), F32)
        self.vector = ((1, WIDTH), F32)
        self.flop = 2 * self.tokens * WIDTH * WIDTH

    def set_small(self, smaller):
        (
            self.gate_taps, self.merge_taps, self.front_gain, self.heads_gain, self.gated_gain,
            self.gate_gain, self.rear_gain, self.final_gain,
        ) = smaller

    def padded(self, width):
        return pltpu.VMEM((width // CHAN, self.spread_rows, CHAN), F32)

    def tall(self, width, kind=F32):
        return ((self.tokens, width), kind)

    def by_column(self, array, start=0):
        return [(array, (self.tokens, WIDTH), lambda j, _: (0, j + start))]

    def front_forward(self, front, after=()):
        self.front = front
        self.after_front, self.front_before, self.front_stat = call(
            front_forward_kernel,
            (4,),
            all_of(self.features, self.front_gain, self.valid)
            + columns(front, 16, 0, step)
            + lines(front, step),
            plain(self.stream)
            + [(*self.tall(4 * WIDTH), (self.tokens, WIDTH), lambda h, _: (0, h))]
            + plain(self.stat),
            [self.low, self.wide],
            self.info,
            8 * self.flop,
            after,
        )
        return self.front_stat

    def heads_forward(self, heads, after=()):
        self.heads = columns(heads, 48, 144, first) + columns(heads, 16, 192, first)
        self.attended, self.packed, self.mixed = call(
            heads_forward_kernel,
            (1,),
            all_of(self.after_front, self.heads_gain, self.segs_col, self.segs_row) + self.heads,
            plain(self.stream, self.tall(3 * WIDTH, LOW), self.tall(WIDTH, LOW)),
            [],
            self.info,
            16 * self.flop,
            after,
        )
        return self.mixed

    def gated_forward(self, gated, after=()):
        self.gated_weights = gated
        (
            self.gated, self.gated_before, self.gate_normal, self.gate_inverse, self.gate_part,
            self.product,
        ) = call(
            functools.partial(gated_forward_kernel, **self.conv),
            (6,),
            all_of(self.after_front, self.gated_gain, self.gate_gain, self.gate_taps)
            + columns(gated, 16, 0, lambda j, _: (j + 3) % 6)
            + columns(gated, 48, 96, first),
            plain(self.stream)
            + [(*self.tall(6 * WIDTH), (self.tokens, WIDTH), lambda j, _: (0, (j + 3) % 6))]
            + plain(
                self.tall(3 * WIDTH), self.tall(1), self.tall(3 * WIDTH), self.tall(3 * WIDTH, LOW)
            ),
            [self.low, pltpu.VMEM((self.tokens, 3 * WIDTH), F32)] + [self.padded(3 * WIDTH)] * 2,
            self.info,
            36 * self.flop,
            after,
        )
        return self.gate_inverse

    def merge_forward(self, rear, after=()):
        self.rear = rear
        self.merge_weight = columns(rear, 32, 128, first)
        self.after_merge, self.merged_low, self.merge_stat = call(
            functools.partial(merge_forward_kernel, **self.conv),
            (1,),
            all_of(self.after_front, self.attended, self.gated, self.merge_taps, self.valid)
            + self.merge_weight,
            plain(self.stream, self.tall(2 * WIDTH, LOW), self.stat),
            [pltpu.VMEM((self.tokens, 2 * WIDTH), F32)] + [self.padded(2 * WIDTH)] * 2,
            self.info,
            18 * self.flop,
            after,
        )
        return self.merge_stat

    def rear_both(self, after=()):
        def bounce(i, _):
            return jnp.where(i < 4, i, 7 - i)

        (
            self.encoded, self.merge_grad, self.rear_gain_grad, self.final_gain_grad,
            self.rear_stat, *pair,
        ) = call(
            rear_kernel,
            (8,),
            all_of(self.after_merge, self.rear_gain, self.final_gain, self.valid, self.cotangent)
            + columns(self.rear, 16, 0, bounce)
            + lines(self.rear, bounce),
            plain(self.tall(WIDTH, LOW), self.stream, self.vector, self.vector, self.stat)
            + halves(128),
            [self.low, pltpu.VMEM((4, self.tokens, WIDTH), F32), self.low, self.wide, self.wide],
            self.info,
            32 * self.flop,
            after,
        )
        return pair

    def merge_backward(self, after=()):
        self.attended_grad, self.gated_grad, self.merge_taps_grad, *pair = call(
            functools.partial(merge_backward_kernel, **self.conv),
            (1,),
            all_of(
                self.merge_grad, self.attended, self.gated, self.merged_low, self.merge_taps
            )
            + self.merge_weight,
            plain(self.stream, self.stream, ((self.taps + 1, 2 * WIDTH), F32)) + halves(32),
            [pltpu.VMEM((self.tokens, 2 * WIDTH), F32)] + [self.padded(2 * WIDTH)] * 3,
            self.info,
            30 * self.flop,
            after,
        )
        return pair

    def heads_backward(self, after=()):
        self.heads_stream, self.heads_gain_grad, *pair = call(
            heads_backward_kernel,
            (1,),
            all_of(
                self.attended_grad, self.after_front, self.heads_gain, self.segs_col,
                self.segs_row, self.packed, self.mixed,
            )
            + self.heads,
            plain(self.stream, self.vector) + halves(64),
            [self.low, pltpu.VMEM((self.tokens, 3 * WIDTH), LOW), self.low],
            self.info,
            26 * self.flop,
            after,
        )
        return pair

    def gated_linear(self, after=()):
        self.part_grad, self.gated_total, *pair = call(
            gated_linear_kernel,
            (3,),
            all_of(self.gated_grad, self.after_front, self.gated_gain)
            + self.by_column(self.gated_before)
            + self.by_column(self.gate_part)
            + all_of(self.product)
            + columns(self.gated_weights, 16, 0, step)
            + columns(self.gated_weights, 48, 96, first),
            [(*self.tall(3 * WIDTH), (self.tokens, WIDTH), lambda j, _: (0, j))]
            + plain(self.stream)
            + halves(96),
            [self.low, pltpu.VMEM((self.tokens, 3 * WIDTH), F32), self.low],
            self.info,
            14 * self.flop,
            after,
        )
        return pair

    def gated_conv(self, after=()):
        self.gate_grad, self.gate_gain_grad, self.gate_taps_grad = call(
            functools.partial(gated_conv_kernel, **self.conv),
            (1,),
            all_of(
                self.part_grad, self.gate_normal, self.gate_inverse, self.gate_gain,
                self.gate_taps,
            ),
            plain(
                self.tall(3 * WIDTH), ((1, 3 * WIDTH), F32), ((self.taps + 1, 3 * WIDTH), F32)
            ),
            [self.padded(3 * WIDTH)] * 3 + [pltpu.VMEM((self.tokens, 3 * WIDTH), F32)],
            self.info,
            36 * self.flop,
            after,
        )
        return self.gate_gain_grad

    def gated_gate(self, after=()):
        self.gated_stream, self.gated_gain_grad, *pair = call(
            gated_gate_kernel,
            (3,),
            self.by_column(self.gate_grad)
            + all_of(self.after_front, self.gated_gain)
            + self.by_column(self.gated_before, 3)
            + all_of(self.gated_total)
            + columns(self.gated_weights, 16, 0, lambda j, _: j + 3),
            plain(self.stream, self.vector) + halves(48),
            [self.low, self.wide],
            self.info,
            12 * self.flop,
            after,
        )
        return pair

    def front_hidden(self, after=()):
        self.front_grad, self.front_before_grad, *pair = call(
            front_hidden_kernel,
            (4,),
            all_of(self.merge_grad, self.heads_stream, self.gated_stream)
            + self.by_column(self.front_before)
            + lines(self.front, step),
            plain(self.stream)
            + [(*self.tall(4 * WIDTH, LOW), (self.tokens, WIDTH), lambda h, _: (0, h))]
            + halves(64),
            [self.low],
            self.info,
            12 * self.flop,
            after,
        )
        return pair

    def front_input(self, after=()):
        self.features_grad, *pair = call(
            front_input_kernel,
            (4,),
            all_of(self.front_grad)
            + self.by_column(self.front_before_grad)
            + all_of(self.features, self.front_gain)
            + columns(self.front, 16, 0, step),
            plain(self.tall(WIDTH, LOW)) + halves(80),
            [self.low, self.wide],
            self.info,
            12 * self.flop,
            after,
        )
        return pair

    def small_grads(self):
        return (
            self.gate_taps_grad, self.merge_taps_grad, self.heads_gain_grad,
            self.gated_gain_grad, self.rear_gain_grad, self.final_gain_grad, self.gate_gain_grad,
        )

    def stats(self):
        return self.front_stat, self.merge_stat, self.rear_stat


SMALL = 16
STATS = 8


def ring(size, shift):
    return [(i, (i + shift) % size) for i in range(size)]


def pack_kernel(
    info, front_up, front_down, heads_in, heads_out, gated_in, gated_out, merge_out, rear_up,
    rear_down, gate_taps, merge_taps, front_gain, heads_gain, gated_gain, rear_gain, final_gain,
    gate_gain, front, middle, rear, small,
):
    def put(target, start, source):
        rows, width = source.shape
        for q in range(width // WIDTH):
            target[start + rows * q : start + rows * (q + 1), :] = source[
                :, WIDTH * q : WIDTH * (q + 1)
            ]

    put(front, 0, front_up)
    put(front, 64, front_down)
    put(middle, 0, gated_in)
    put(middle, 96, gated_out)
    put(middle, 144, heads_in)
    put(middle, 192, heads_out)
    put(rear, 0, rear_up)
    put(rear, 64, rear_down)
    put(rear, 128, merge_out)
    small[...] = jnp.zeros_like(small)
    for q, source in ((0, gate_taps), (2, merge_taps)):
        value = source[...].astype(F32)
        taps, width = value.shape
        small[0:SMALL, CHAN * q : CHAN * q + width] = value[:SMALL]
        small[0 : taps - SMALL, CHAN * (q + 1) : CHAN * (q + 1) + width] = value[SMALL:]
    start = CHAN
    for source in (front_gain, heads_gain, gated_gain, rear_gain, final_gain, gate_gain):
        width = source.shape[1]
        small[SMALL - 1 :, start : start + width] = source[...].astype(F32)
        start += width
    front[128 : 128 + SMALL, :] = small[...].astype(LOW)


def copy_all(copies):
    for copy in copies:
        copy.start()
    for copy in copies:
        copy.wait()


def place_line_kernel(info, *refs):
    pieces, out, sem = refs[:4], refs[4], refs[5]
    copy_all(
        [
            pltpu.make_async_copy(piece, out.at[chip, info[i]], sem.at[chip, i])
            for chip in range(4)
            for i, piece in enumerate(pieces)
        ]
    )


def place(kernel, pieces, rows, spots, after=()):
    skipped = len(after)

    def body(info, *refs):
        kernel(info, *refs[skipped:])

    anywhere = pl.BlockSpec(memory_space=pl.ANY)
    return pl.pallas_call(
        body,
        grid_spec=pltpu.PrefetchScalarGridSpec(
            num_scalar_prefetch=1,
            grid=(1,),
            in_specs=[anywhere] * skipped + [whole(piece.shape) for piece in pieces],
            out_specs=anywhere,
            scratch_shapes=[pltpu.SemaphoreType.DMA((4, 4))],
        ),
        out_shape=jax.ShapeDtypeStruct((4, 4, rows, WIDTH), LOW),
        name=kernel.__name__,
        cost_estimate=pl.CostEstimate(
            flops=0, bytes_accessed=32 * rows * WIDTH * 2, transcendentals=0
        ),
    )(spots, *after, *pieces)


def line_sends(array):
    return [lax.ppermute(array, "z", ring(4, d)) for d in (1, 2, 3)]


def plane_exchange(array):
    return lax.all_to_all(array, ("x", "y"), 0, 0, tiled=True)


def core_swap(array):
    return lax.ppermute(array, "k", ring(2, 1))


def tie(array, *others):
    return lax.optimization_barrier((array, others))[0]


def unpack_kernel(info, first, second, gate_taps, merge_taps, gains, gate_gain):
    mine = info[0]
    lane = lax.broadcasted_iota(jnp.int32, (SMALL, CHAN), 1)
    lane_row = lane[:1]
    gate_gain[...] = jnp.zeros_like(gate_gain)
    gains[...] = jnp.zeros_like(gains)

    def put(target, rows, value, start, size, lanes):
        block, offset = start // CHAN, start % CHAN
        inside = jnp.logical_and(lanes >= offset, lanes < offset + size)
        window = slice(CHAN * block, CHAN * (block + 1))
        target[rows, window] = jnp.where(inside, value, target[rows, window])
        spill = offset + size - CHAN
        if spill > 0:
            window = slice(CHAN * (block + 1), CHAN * (block + 2))
            target[rows, window] = jnp.where(lanes < spill, value, target[rows, window])

    for i in range(BLOCKS):
        x, core, rest = i // 16, (i // 8) % 2, i % 8
        chip, z = 2 * x + rest % 2, rest // 2
        value = jnp.where(mine == core, first[chip, z], second[chip, z]).astype(F32)
        quads = [value[:, CHAN * q : CHAN * (q + 1)] for q in range(4)]
        start = 48 * i
        for half in range(2):
            rows = slice(SMALL * half, SMALL * (half + 1))
            rolled = pltpu.roll(quads[half], start % CHAN, 1)
            put(gate_taps, rows, rolled, start, 48, lane)
            rolled = pltpu.roll(quads[2 + half], (32 * i) % CHAN, 1)
            put(merge_taps, rows, rolled, 32 * i, 32, lane)
        line = quads[1][SMALL - 1 :]
        for g in range(5):
            rolled = pltpu.roll(line, (16 * i - 16 * g) % CHAN, 1)
            put(gains, slice(g, g + 1), rolled, 16 * i, 16, lane_row)
        rolled = pltpu.roll(line, (48 * i - 80) % CHAN, 1)
        put(gate_gain, slice(0, 1), rolled, 48 * i, 48, lane_row)


def pack_small_kernel(
    info, gate_taps, merge_taps, heads_gain, gated_gain, rear_gain, final_gain, gate_gain,
    front_stat, merge_stat, rear_stat, send, keep, *, count_at,
):
    mine = info[0]
    lane = lax.broadcasted_iota(jnp.int32, (SMALL, CHAN), 1)
    lane_row = lane[:1]
    last = lax.broadcasted_iota(jnp.int32, (SMALL, CHAN), 0) == SMALL - 1
    stats = [
        front_stat[0:1, :], front_stat[1:2, :], merge_stat[0:1, :], rear_stat[0:1, :],
        front_stat[2:3, :], merge_stat[1:2, :], rear_stat[1:2, :],
    ]
    stat_line = jnp.where(lane_row == 7, info[count_at].astype(F32), 0.0)
    for i, stat in enumerate(stats):
        stat_line = jnp.where(lane_row == i, jnp.sum(stat, axis=1, keepdims=True), stat_line)
    rest = stat_line - stat_line.astype(LOW).astype(F32)
    stat_line += pltpu.roll(rest, STATS, 1)

    def take(source, rows, start, size, lanes):
        block, offset = start // CHAN, start % CHAN
        value = source[rows, CHAN * block : CHAN * (block + 1)]
        if offset:
            value = pltpu.roll(value, CHAN - offset, 1)
        if offset + size > CHAN:
            other = source[rows, CHAN * (block + 1) : CHAN * (block + 2)]
            value = jnp.where(lanes < CHAN - offset, value, pltpu.roll(other, CHAN - offset, 1))
        return value

    def quads_of(i):
        halves = [slice(0, SMALL), slice(SMALL, 2 * SMALL)]
        quads = [take(gate_taps, rows, 48 * i, 48, lane) for rows in halves]
        quads += [take(merge_taps, rows, 32 * i, 32, lane) for rows in halves]
        line = pltpu.roll(take(gate_gain, slice(0, 1), 48 * i, 48, lane_row), 80, 1)
        for g, gain in enumerate((heads_gain, gated_gain, rear_gain, final_gain)):
            start = 16 * (g + 1)
            block = gain[:, CHAN * (i // 8) : CHAN * (i // 8 + 1)]
            value = pltpu.roll(block, (start - 16 * i) % CHAN, 1)
            inside = jnp.logical_and(lane_row >= start, lane_row < start + 16)
            line = jnp.where(inside, value, line)
        quads[1] = jnp.where(last, line, quads[1])
        quads[3] = jnp.where(last, stat_line, quads[3])
        return quads

    for i in [*range(8), *range(16, 24)]:
        x, spot = i // 16, i % 8
        pairs = zip(quads_of(i), quads_of(i + 8))
        for q, (low, high) in enumerate(pairs):
            lanes = slice(CHAN * q, CHAN * (q + 1))
            keep[x, spot, :, lanes] = jnp.where(mine == 0, low, high).astype(LOW)
            send[x, spot, :, lanes] = jnp.where(mine == 0, high, low).astype(LOW)


def round_small(total):
    quad = total[:, 3 * CHAN :]
    lane = lax.broadcasted_iota(jnp.int32, quad.shape, 1)
    row = lax.broadcasted_iota(jnp.int32, quad.shape, 0)
    stat = jnp.logical_and(row == SMALL - 1, lane < STATS)
    rest = jnp.where(stat, quad - quad.astype(LOW).astype(F32), 0.0)
    quad = quad + pltpu.roll(rest, STATS, 1)
    return jnp.concatenate([total[:, : 3 * CHAN], quad], axis=1).astype(LOW)


def core_sum_kernel(info, *refs, sizes):
    inputs, out = refs[:-1], refs[-1]
    half = len(inputs) // 2
    keeps, gots = inputs[:half], inputs[half:]
    for chip in range(4):
        x, y = chip // 2, chip % 2
        start = 0
        for keep, got, (rows, small) in zip(keeps, gots, sizes):
            if small:
                total = keep[x, 0, y].astype(F32) + got[x, 0, y].astype(F32)
                out[chip, 0, start : start + rows, :] = round_small(total)
            else:
                out[chip, 0, start : start + rows, :] = keep[x, 0, y] + got[x, 0, y]
            start += rows


def plane_sum_kernel(info, pieces, *outs, sizes):
    for e in range(4):
        zi = lax.rem(info[0] + e, 4)
        start = 0
        for rows in sizes:
            small, rows = rows < 0, abs(rows)
            span = slice(start, start + rows)
            start += rows
            total = sum(pieces[chip, zi, span, :].astype(F32) for chip in range(4))
            if e == 0:
                outs[0][span, :] = total
            elif small:
                outs[e][span, :] = round_small(total)
            else:
                outs[e][span, :] = total.astype(LOW)


def line_sum_kernel(info, keep, one, two, three, *refs, pieces):
    refs = list(refs)
    start = 0
    for rows, what in pieces:
        span = slice(start, start + rows)
        start += rows
        total = keep[span, :]
        for piece in (one, two, three):
            total += piece[span, :].astype(F32)
        if what == "small":
            quads = [total[:, CHAN * q : CHAN * (q + 1)] for q in range(4)]
            gate_taps, merge_taps, heads_gain, gated_gain, rear_gain, final_gain, gate_gain, stats = refs
            gate_taps[0:SMALL, :] = quads[0][:, :48]
            gate_taps[SMALL : 2 * SMALL - 1, :] = quads[1][: SMALL - 1, :48]
            merge_taps[0:SMALL, :] = quads[2][:, :32]
            merge_taps[SMALL : 2 * SMALL - 1, :] = quads[3][: SMALL - 1, :32]
            line = quads[1][SMALL - 1 :, :]
            for g, target in enumerate((heads_gain, gated_gain, rear_gain, final_gain)):
                target[...] = pltpu.roll(line, CHAN - 16 * (g + 1), 1)[:, :16]
            gate_gain[...] = pltpu.roll(line, CHAN - 80, 1)[:, :48]
            line = quads[3][SMALL - 1 :, :]
            line += pltpu.roll(line, CHAN - STATS, 1)
            frames = jnp.sum(line[:, STATS - 1 : STATS])
            stats[...] = jnp.sqrt(line[:, : STATS - 1] / (frames * WIDTH))
        elif what == "gain":
            owner = info[4]
            line = jnp.zeros((1, CHAN), F32)
            for b in range(WIDTH // CHAN):
                block = total[0:1, CHAN * b : CHAN * (b + 1)]
                line = jnp.where(owner // 8 == b, block, line)
            line = pltpu.roll(line, lax.rem(CHAN - 16 * lax.rem(owner, 8), CHAN), 1)
            refs.pop(0)[...] = line[:, :16]
        elif what == "left":
            given, target = refs.pop(0), refs[0]
            target[:, : given.shape[1]] = given[...]
        else:
            shift = 0
            if what == "right":
                target = refs.pop(0)
                shift = target.shape[1] // 2
            else:
                target = refs.pop(0)
            height = target.shape[0]
            for q in range(rows // height):
                lanes = slice(shift + WIDTH * q, shift + WIDTH * (q + 1))
                target[:, lanes] = total[height * q : height * (q + 1), :]


def core_sum(pairs, spots, after=()):
    sizes = [(pair[0].shape[2], pair[0].shape[2] == SMALL) for pair in pairs]
    arrays = [pair[i] for i in (0, 1) for pair in pairs]
    arrays = [array.reshape(2, 4, 2, array.shape[2], WIDTH) for array in arrays]
    total = sum(array.shape[3] for array in arrays) // 2
    (out,) = call(
        functools.partial(core_sum_kernel, sizes=tuple(sizes)),
        (4,),
        [
            (array, (2, 1, 2, array.shape[3], WIDTH), lambda i, _: (0, i, 0, 0, 0))
            for array in arrays
        ],
        [((4, 4, total, WIDTH), LOW, (4, 1, total, WIDTH), lambda i, _: (0, i, 0, 0))],
        [],
        spots,
        after=after,
    )
    return out


def plane_sum(pieces, sizes, spots, after=()):
    total = pieces.shape[2]
    return call(
        functools.partial(plane_sum_kernel, sizes=sizes),
        (1,),
        all_of(pieces),
        plain(((total, WIDTH), F32), *[((total, WIDTH), LOW)] * 3),
        [],
        spots,
        after=after,
    )


def line_sum(sums, pieces, outputs, spots, given=(), after=()):
    own, rest = sums
    return call(
        functools.partial(line_sum_kernel, pieces=pieces),
        (1,),
        all_of(own, *rest, *given),
        plain(*[(shape, F32) for shape in outputs]),
        [],
        spots,
        after=after,
    )


def line_swap(sums):
    return sums[0], [lax.ppermute(array, "z", ring(4, d)) for d, array in zip((1, 2, 3), sums[1:])]


def pack_small(layer, mine_info, count, after=()):
    return call(
        functools.partial(pack_small_kernel, count_at=1 + 2 * count),
        (1,),
        all_of(*layer.small_grads(), *layer.stats()),
        plain(*[((2, 8, SMALL, WIDTH), LOW)] * 2),
        [],
        mine_info,
        after=after,
    )


def unpack_small(front, mine):
    block = (4, 4, SMALL, WIDTH), lambda *_: (0, 0, 8, 0)
    gate_taps, merge_taps, gains, gate_full = call(
        unpack_kernel,
        (1,),
        [(array, *block) for array in front],
        plain(
            ((32, 3 * WIDTH), F32), ((32, 2 * WIDTH), F32), ((8, WIDTH), F32), ((1, 3 * WIDTH), F32)
        ),
        [],
        mine.reshape(1),
    )
    lines = [gains[g : g + 1] for g in range(5)]
    return gate_taps, merge_taps, lines[0], lines[1], lines[2], gate_full, lines[3], lines[4]


def grid_device(
    features, cotangent, lengths, front_up, front_down, heads_input, heads_output, gated_input,
    gated_output, merge_output, rear_up, rear_down, gate_kernel, merge_kernel, front_gain,
    heads_gain, gated_gain, gate_gain, rear_gain, final_gain,
):
    x, k, z, y = (lax.axis_index(name) for name in ("x", "k", "z", "y"))
    places = [lax.rem(place, 4) for place in (z, z + 3, z + 2, z + 1)]
    places.append(((x * 2 + k) * 4 + z) * 2 + y)
    spots = jnp.stack([place.astype(jnp.int32) for place in places])
    mine = k.astype(jnp.int32)
    layer = Layer(features, cotangent, lengths[0], mine, gate_kernel.shape[0])

    front, middle, rear = call(
        pack_kernel,
        (1,),
        all_of(
            front_up, front_down, heads_input, heads_output, gated_input, gated_output,
            merge_output, rear_up, rear_down, gate_kernel, merge_kernel,
            *[
                gain.reshape(1, -1)
                for gain in (front_gain, heads_gain, gated_gain, rear_gain, final_gain, gate_gain)
            ],
        ),
        plain(((144, WIDTH), LOW), ((208, WIDTH), LOW), ((160, WIDTH), LOW)),
        [pltpu.VMEM((SMALL, WIDTH), F32)],
        spots,
    )
    front_four = place(place_line_kernel, [front] + line_sends(front), 144, spots)
    front = plane_exchange(front_four)
    middle = tie(middle, front_four)
    middle_four = place(place_line_kernel, [middle] + line_sends(middle), 208, spots)
    front = tie(front, middle_four)
    middle = plane_exchange(tie(middle_four, front))
    rear = tie(rear, front)
    rear_lines = line_sends(rear)
    front = front, core_swap(front)
    layer.set_small(unpack_small(front, mine))
    mark = layer.front_forward(front)
    rear_four = place(place_line_kernel, [rear] + rear_lines, 160, spots, after=(mark,))
    middle = tie(middle, rear_four)
    rear = plane_exchange(tie(rear_four, middle))
    middle = middle, core_swap(middle)
    mark = layer.heads_forward(middle)
    mark = layer.gated_forward(middle, after=(mark,))
    rear = tie(rear, mark)
    rear = rear, core_swap(rear)
    layer.merge_forward(rear)

    wide = ((32, None), (48, "half"), (48, None), (48, None), (16, None))
    last = ((48, "right"), (64, None), (16, "small"))
    send, rear_keep = layer.rear_both()
    rear_got = core_swap(send)
    merge_send, merge_keep = layer.merge_backward()
    rear_four = core_sum([(rear_keep, rear_got)], spots, after=(layer.attended_grad,))
    merge_got = core_swap(merge_send)
    rear_plane = plane_exchange(rear_four)
    send, heads_keep = layer.heads_backward(after=(rear_four,))
    heads_got = core_swap(send)
    send, gated_keep = layer.gated_linear(after=(layer.heads_stream,))
    gated_got = core_swap(send)
    rear_sums = plane_sum(rear_plane, (128,), spots, after=(layer.gated_total,))
    wide_four = core_sum(
        [(merge_keep, merge_got), (gated_keep, gated_got), (heads_keep, heads_got)], spots,
        after=(rear_sums[0],),
    )
    rear_sums = line_swap(rear_sums)
    wide_plane = plane_exchange(tie(wide_four, rear_plane))
    layer.gated_conv(after=(wide_four,))
    send, gate_keep = layer.gated_gate()
    gate_got = core_swap(send)
    small_send, small_keep = pack_small(layer, layer.info, lengths.shape[1])
    small_got = core_swap(small_send)
    rear_up_grad, rear_down_grad = line_sum(
        rear_sums, ((64, None), (64, None)), (rear_up.shape, rear_down.shape), spots,
        after=(small_send,),
    )
    send, down_keep = layer.front_hidden(after=(small_send, rear_up_grad))
    down_got = core_swap(send)
    wide_sums = plane_sum(wide_plane, (192,), spots, after=(layer.front_grad,))
    last_four = core_sum(
        [(gate_keep, gate_got), (down_keep, down_got), (small_keep, small_got)], spots,
        after=(wide_sums[0],),
    )
    wide_sums = line_swap(wide_sums)
    last_plane = plane_exchange(tie(last_four, wide_plane))
    send, up_keep = layer.front_input(after=(last_four,))
    up_got = core_swap(send)
    half_shape = (gated_input.shape[0], gated_input.shape[1] // 2)
    merge_output_grad, gated_left_grad, gated_output_grad, heads_input_grad, heads_output_grad = (
        line_sum(
            wide_sums,
            ((32, None), (48, None), (48, None), (48, None), (16, None)),
            (
                merge_output.shape, half_shape, gated_output.shape, heads_input.shape,
                heads_output.shape,
            ),
            spots,
            after=(layer.features_grad,),
        )
    )
    front_four = core_sum([(up_keep, up_got)], spots, after=(merge_output_grad,))
    last_sums = plane_sum(last_plane, (48, 64, -SMALL), spots, after=(front_four,))
    last_sums = line_swap(last_sums)
    front_plane = plane_exchange(tie(front_four, last_plane))
    vector = (1, front_gain.shape[0])
    (
        gated_input_grad, front_down_grad, gate_kernel_grad, merge_kernel_grad, heads_gain_grad,
        gated_gain_grad, rear_gain_grad, final_gain_grad, gate_gain_grad, statistics,
    ) = line_sum(
        last_sums,
        ((0, "left"), (48, "right"), (64, None), (16, "small")),
        (
            gated_input.shape, front_down.shape, gate_kernel.shape, merge_kernel.shape,
            vector, vector, vector, vector, (1, gate_gain.shape[0]), (1, STATS - 1),
        ),
        spots,
        given=(gated_left_grad,),
    )
    front_sums = plane_sum(front_plane, (80,), spots, after=(statistics,))
    front_up_grad, front_gain_grad = line_sum(
        line_swap(front_sums), ((64, None), (16, "gain")), (front_up.shape, vector), spots
    )
    return (
        layer.encoded, layer.features_grad, front_up_grad, front_down_grad, heads_input_grad,
        heads_output_grad, gated_input_grad, gated_output_grad, merge_output_grad, rear_up_grad,
        rear_down_grad, gate_kernel_grad, merge_kernel_grad, front_gain_grad[0],
        heads_gain_grad[0], gated_gain_grad[0], gate_gain_grad[0], rear_gain_grad[0],
        final_gain_grad[0], statistics[0],
    )


def pack_rows(shard):
    rows, columns = shard.shape
    pieces = shard.reshape(rows, columns // WIDTH, WIDTH).transpose(1, 0, 2)
    return pieces.reshape(rows * columns // WIDTH, WIDTH)


def pad_lines(flat):
    rows = -(-flat.shape[-1] // (WIDTH * 16)) * 16
    spare = [(0, 0)] * (flat.ndim - 1) + [(0, rows * WIDTH - flat.shape[-1])]
    return jnp.pad(flat, spare).reshape(flat.shape[:-1] + (rows, WIDTH))


def to_owners(weight):
    rows, columns = weight.shape
    pieces = weight.reshape(BLOCKS, rows // BLOCKS, columns // WIDTH, WIDTH)
    pieces = pieces.transpose(0, 2, 1, 3).reshape(2, 2, 4, 2, -1, WIDTH)
    pieces = pieces.transpose(1, 0, 3, 2, 4, 5)
    return pieces.reshape(2, 4, 4, -1, WIDTH)


def from_owners(halves, rows, columns):
    send, keep = halves
    pieces = jnp.stack([keep, send], axis=1)
    pieces = pieces.reshape(BLOCKS, columns // WIDTH, rows // BLOCKS, WIDTH)
    return pieces.transpose(0, 2, 1, 3).reshape(rows, columns)


def any_device(features, cotangent, lengths, *shards, axes):
    count = lax.axis_size(axes)
    matrices, smaller = shards[:9], shards[9:]
    packed = [pack_rows(element) for element in matrices]
    packed.append(pad_lines(jnp.concatenate([element.reshape(-1) for element in smaller])))
    gathered = lax.all_gather(jnp.concatenate(packed), axes, axis=0)
    weights = []
    start = 0
    for element, piece in zip(matrices, packed):
        rows, columns = element.shape
        window = gathered[:, start : start + piece.shape[0]]
        start += piece.shape[0]
        window = window.reshape(count, columns // WIDTH, rows, WIDTH).transpose(0, 2, 1, 3)
        weights.append(to_owners(window.reshape(count * rows, columns)))
    flat = gathered[:, start:].reshape(count, -1).astype(F32)
    lines = []
    start = 0
    for element in smaller:
        window = flat[:, start : start + element.size]
        start += element.size
        if element.ndim == 2:
            window = window.reshape((count,) + element.shape).transpose(1, 0, 2)
            window = window.reshape(element.shape[0], -1)
            lines.append(jnp.pad(window, ((0, 1), (0, 0))))
        else:
            lines.append(window.reshape(1, -1))
    up, down, h_in, h_out, g_in, g_out, m_out, r_up, r_down = weights

    def chunk(*members):
        return tuple(jnp.concatenate([member[i] for member in members], axis=2) for i in (0, 1))

    front = chunk(up, down)
    rear = chunk(r_up, r_down, m_out)
    layer = Layer(features, cotangent, lengths[0], jnp.int32(0), smaller[0].shape[0])
    layer.set_small(lines)
    layer.front_forward(front)
    middle = chunk(g_in, g_out, h_in, h_out)
    layer.heads_forward(middle)
    layer.gated_forward(middle)
    layer.merge_forward(rear)
    rear = layer.rear_both()
    merge = layer.merge_backward()
    left = layer.gated_linear()
    heads = layer.heads_backward()
    layer.gated_conv()
    right = layer.gated_gate()
    front_down_halves = layer.front_hidden()
    front_up_halves = layer.front_input()

    def part(pair, start, stop):
        return tuple(array[:, :, start:stop] for array in pair)

    gated_halves = tuple(
        jnp.concatenate([one[:, :, :48], two], axis=2) for one, two in zip(left, right)
    )
    ordered = (
        part(front_up_halves, 0, 64), front_down_halves, part(heads, 0, 48), part(heads, 48, 64),
        gated_halves, part(left, 48, 96), merge, part(rear, 0, 64), part(rear, 64, 128),
    )
    front_gain = front_up_halves[1][0, 0, 64].astype(F32)
    small_grads = layer.small_grads()
    pieces = []
    for element, halves in zip(matrices, ordered):
        rows, columns = element.shape
        full = from_owners(halves, rows * count, columns)
        full = full.reshape(count, rows, columns // WIDTH, WIDTH).transpose(0, 2, 1, 3)
        pieces.append(full.reshape(count, -1, WIDTH))
    gate_taps, merge_taps, heads_gain, gated_gain, rear_gain, final_gain, gate_gain = small_grads
    small_full = (gate_taps, merge_taps, front_gain, heads_gain, gated_gain, gate_gain, rear_gain, final_gain)
    flat = []
    for element, full in zip(smaller, small_full):
        if element.ndim == 2:
            full = full[: element.shape[0]].reshape(element.shape[0], count, -1).transpose(1, 0, 2)
        flat.append(full.reshape(count, -1))
    pieces.append(pad_lines(jnp.concatenate(flat, axis=1).astype(LOW)))
    summed = lax.psum_scatter(jnp.concatenate(pieces, axis=1), axes, scatter_dimension=0)
    outputs = []
    start = 0
    for element, piece in zip(matrices, pieces):
        rows, columns = element.shape
        window = summed[start : start + piece.shape[1]].astype(F32)
        start += piece.shape[1]
        window = window.reshape(columns // WIDTH, rows, WIDTH).transpose(1, 0, 2)
        outputs.append(window.reshape(rows, columns))
    flat = summed[start:].reshape(-1).astype(F32)
    start = 0
    for element in smaller:
        outputs.append(flat[start : start + element.size].reshape(element.shape))
        start += element.size
    front_stat, merge_stat, rear_stat = layer.stats()
    squares = jnp.stack(
        [
            front_stat[0], front_stat[1], merge_stat[0], rear_stat[0], front_stat[2],
            merge_stat[1], rear_stat[1],
        ]
    )
    totals = lax.psum(
        jnp.append(jnp.sum(squares, axis=1), jnp.sum(lengths).astype(F32)), axes
    )
    statistics = jnp.sqrt(totals[:7] / (totals[7] * features.shape[1]))
    return (layer.encoded, layer.features_grad) + tuple(outputs) + (statistics,)


def solution(mesh):
    body = grid_device
    axes = ("x", "k", "z", "y")
    if mesh.devices.shape == (4, 8):
        mesh = Mesh(mesh.devices.reshape(2, 2, 4, 2), axes)
    else:
        axes = tuple(mesh.axis_names)
        body = functools.partial(any_device, axes=axes)
    rows, columns, vector = P(axes, None), P(None, axes), P(axes)
    weights = (rows,) * 9 + (columns,) * 2 + (vector,) * 6
    return jax.shard_map(
        body,
        mesh=mesh,
        in_specs=(rows, rows, rows) + weights,
        out_specs=(rows, rows) + weights + (P(),),
        check_vma=False,
    )
```

time: 471 us -> 393 us (0.83); the launches traced: 462 us -> 391 us
  waiting for transfers between devices: 196 us -> 80.4 us
  Pallas kernels: 182 us -> 221 us
  starting transfers between devices: 57 us -> 66.8 us
    ppermute x51 -> x32, waiting for transfers between devices: 196 us -> 61.5 us  [the longest x9 30 us: line_sends(): return [lax.ppermute(array, 'z', ring(4, d)) for d in (1, 2, 3)]]
    pallas_call x27 -> x30, Pallas kernels: 182 us -> 221 us  [the longest x27 211 us: call(): pl.pallas_call(body, grid_spec=pltpu.PrefetchScalarGridSpec(num_scalar_pr...]
    all_to_all x0 -> x7, starting transfers between devices: none -> 29.8 us  [plane_exchange(): return lax.all_to_all(array, ('x', 'y'), 0, 0, tiled=True)]
    ppermute x51 -> x32, starting transfers between devices: 57 us -> 36.9 us  [the longest x12 20.9 us: line_swap(): lax.ppermute(array, 'z', ring(4, d))]
    all_to_all x0 -> x7, waiting for transfers between devices: none -> 18.8 us  [plane_exchange(): return lax.all_to_all(array, ('x', 'y'), 0, 0, tiled=True)]
    unnamed x78 -> x72, local copies, waits for them, and re-layouts: 12.2 us -> 16.3 us
  transfers between devices with their start and end apart: 51 -> 39, of which waited for: 22 -> 16; matrix products, arithmetic and copies ran while one was open for 1% -> 1% of each run, Pallas kernels for 14% -> 43%
where the time goes in v2:
time: 393 us; the launch traced here: 391 us
  Pallas kernels  221 us (56%)
  waiting for transfers between devices  80.4 us (20%)
  starting transfers between devices  66.8 us (17%)
  local copies, waits for them, and re-layouts  20.4 us (5%)
    pallas_call x27, Pallas kernels, call(): pl.pallas_call(body, grid_spec=pltpu.PrefetchScalarGridSpec(num_scalar_pr...  211 us
    ppermute x9, waiting for transfers between devices, line_sends(): return [lax.ppermute(array, 'z', ring(4, d)) for d in (1, 2, 3)]  30 us
    all_to_all x7, starting transfers between devices, plane_exchange(): return lax.all_to_all(array, ('x', 'y'), 0, 0, tiled=True)  29.8 us
    ppermute x12, waiting for transfers between devices, line_swap(): lax.ppermute(array, 'z', ring(4, d))  25.7 us
    ppermute x12, starting transfers between devices, line_swap(): lax.ppermute(array, 'z', ring(4, d))  20.9 us
    all_to_all x7, waiting for transfers between devices, plane_exchange(): return lax.all_to_all(array, ('x', 'y'), 0, 0, tiled=True)  18.8 us
    unnamed x72, local copies, waits for them, and re-layouts  16.3 us
    ppermute x9, starting transfers between devices, line_sends(): return [lax.ppermute(array, 'z', ring(4, d)) for d in (1, 2, 3)]  14.4 us
  transfers between devices with their start and end apart: 39, of which 16 were waited for; matrix products, arithmetic and copies ran while one was open for 1% of the time, Pallas kernels for 43%

profile of v2, /device:TPU:0, one launch (start us, length us, event | category | flops | bytes accessed | tf_op | source)
XLA Modules:
  0.0 391.1 jit_solution(18070714410930778723)
XLA Ops:
  4.0 5.0 %collective-permute-start.2 = (bf16[144,512]{1,0:T(8,128)(2,1)}, bf16[144,512]{1,0:T(8,128)(2,1)S(1)}, u32[]{:S(2)}, u32[]{:S(2)}) collective-permute-start(bf16[144,512]{1,0:T(8,128)(2,1)} %get-tuple-element.123.refs_0_), channel_id=1, source_target_pairs={{0,6},{2,0},{4,2},{6,4},{1,7},{3,1},{5,3},{7,5},{8,14},{10,8},{12,... | collective-permute-start | bytes 442376 | tf_op jit(solution)/shard_map/ppermute | solution.py:1001
  13.6 8.1 %collective-permute-done.1.refs_2_ = bf16[144,512]{1,0:T(8,128)(2,1)S(1)} collective-permute-done((bf16[144,512]{1,0:T(8,128)(2,1)}, bf16[144,512]{1,0:T(8,128)(2,1)S(1)}, u32[]{:S(2)}, u32[]{:S(2)}) %collective-permute-start.1) | collective-permute-done | bytes 147488 | tf_op jit(solution)/shard_map/ppermute | solution.py:1001
  26.4 4.6 %all-to-all-start = ((bf16[4,4,144,512]{3,2,1,0:T(8,128)(2,1)}), bf16[4,4,144,512]{3,2,1,0:T(8,128)(2,1)}, u32[]{:S(2)}, u32[]{:S(2)}) async-start(bf16[4,4,144,512]{3,2,1,0:T(8,128)(2,1)} %place_line_kernel.3), calls=%async_computation | async-start | bytes 4718592 | tf_op jit(solution)/shard_map/all_to_all | solution.py:1005
  38.4 13.3 %collective-permute-done.4.refs_2_ = bf16[208,512]{1,0:T(8,128)(2,1)S(1)} collective-permute-done((bf16[208,512]{1,0:T(8,128)(2,1)S(1)}, bf16[208,512]{1,0:T(8,128)(2,1)S(1)}, u32[]{:S(2)}, u32[]{:S(2)}) %collective-permute-start.4) | collective-permute-done | bytes 213024 | tf_op jit(solution)/shard_map/ppermute | solution.py:1001
  71.7 8.1 %front_forward_kernel.1 = (f32[384,512]{1,0:T(8,128)}, f32[384,2048]{1,0:T(8,128)}, f32[8,512]{1,0:T(8,128)}) custom-call(s32[11]{0:T(128)} %concatenate.3.info_ref, bf16[384,512]{1,0:T(8,128)(2,1)} %refs_3_.3, f32[1,512]{1,0:T(1,128)} %get-tuple-element.230.refs_1_.refs_4_, f32[384,1]{1,0:T(8,128)} %compare_convert_fusion.refs_2_.refs_4_.refs_3_, ...), custom_call_target="tpu_custom_call" | custom-call | flops 1610612736 | bytes 13782528 | tf_op jit(solution)/shard_map/front_forward_kernel/pallas_call | solution.py:600
  85.2 17.0 %all-to-all-done.1.refs_4_.refs_6_.refs_5_.refs_7_.refs_8_.refs_10_.refs_9_ = bf16[4,4,208,512]{3,2,1,0:T(8,128)(2,1)S(1)} async-done(((bf16[4,4,208,512]{3,2,1,0:T(8,128)(2,1)}), bf16[4,4,208,512]{3,2,1,0:T(8,128)(2,1)S(1)}, u32[]{:S(2)}, u32[]{:S(2)}) %all-to-all-start.1) | async-done | bytes 3407904 | tf_op jit(solution)/shard_map/all_to_all | solution.py:1005
  104.0 4.6 %all-to-all-start.2 = ((bf16[4,4,160,512]{3,2,1,0:T(8,128)(2,1)}), bf16[4,4,160,512]{3,2,1,0:T(8,128)(2,1)}, u32[]{:S(2)}, u32[]{:S(2)}) async-start(bf16[4,4,160,512]{3,2,1,0:T(8,128)(2,1)} %place_line_kernel.5), calls=%async_computation.2 | async-start | bytes 5242880 | tf_op jit(solution)/shard_map/all_to_all | solution.py:1005
  109.9 9.1 %heads_forward_kernel.1 = (f32[384,512]{1,0:T(8,128)}, bf16[384,1536]{1,0:T(8,128)(2,1)}, bf16[384,512]{1,0:T(8,128)(2,1)}) custom-call(s32[11]{0:T(128)} %concatenate.3.info_ref, f32[384,512]{1,0:T(8,128)} %get-tuple-element.128.refs_0_.refs_1_.refs_2_, f32[1,512]{1,0:T(1,128)} %get-tuple-element.229.refs_1_.refs_3_, s32[384,1]{1,0:T(8,128)} %reduce_sum.13.refs_2_.refs_4_, ...), custom_call_target="tpu_custom_call" | custom-call | flops 3221225472 | bytes 16782336 | tf_op jit(solution)/shard_map/heads_forward_kernel/pallas_call | solution.py:600
  119.0 20.7 %gated_forward_kernel.1 = (f32[384,512]{1,0:T(8,128)}, f32[384,3072]{1,0:T(8,128)}, f32[384,1536]{1,0:T(8,128)}, f32[384,1]{1,0:T(8,128)}, f32[384,1536]{1,0:T(8,128)}, /*index=5*/bf16[384,1536]{1,0:T(8,128)(2,1)}) custom-call(s32[11]{0:T(128)} %concatenate.3.info_ref, bf16[384,512]{1,0:T(8,128)(2,1)} %get-tuple-element.135.refs_0_.refs_7_, ...), custom_call_target="tpu_custom_call" | custom-call | flops 7247757312 | bytes 26027520 | tf_op jit(solution)/shard_map/gated_forward_kernel/pallas_call | solution.py:600
  139.8 5.1 %collective-permute-done.11.refs_6_.refs_8_ = bf16[4,4,160,512]{3,2,1,0:T(8,128)(2,1)S(1)} collective-permute-done((bf16[4,4,160,512]{3,2,1,0:T(8,128)(2,1)}, bf16[4,4,160,512]{3,2,1,0:T(8,128)(2,1)S(1)}, u32[]{:S(2)}, u32[]{:S(2)}) %collective-permute-start.11) | collective-permute-done | bytes 2621472 | tf_op jit(solution)/shard_map/ppermute | solution.py:1009
  146.4 10.3 %merge_forward_kernel.1 = (f32[384,512]{1,0:T(8,128)}, bf16[384,1024]{1,0:T(8,128)(2,1)}, f32[8,512]{1,0:T(8,128)}) custom-call(s32[11]{0:T(128)} %concatenate.3.info_ref, f32[384,512]{1,0:T(8,128)} %get-tuple-element.128.refs_0_.refs_1_.refs_2_, f32[384,512]{1,0:T(8,128)} %get-tuple-element.134.refs_1_, f32[384,512]{1,0:T(8,128)} %get-tuple-element.138.refs_2_, ...), custom_call_target="tpu_custom_call" | custom-call | flops 3623878656 | bytes 9324032 | tf_op jit(solution)/shard_map/merge_forward_kernel/pallas_call | solution.py:600
  156.7 18.4 %rear_kernel.1 = (bf16[384,512]{1,0:T(8,128)(2,1)}, f32[384,512]{1,0:T(8,128)}, f32[1,512]{1,0:T(1,128)}, f32[1,512]{1,0:T(1,128)}, f32[8,512]{1,0:T(8,128)}, /*...) custom-call(s32[11]{0:T(128)} %concatenate.3.info_ref, f32[384,512]{1,0:T(8,128)} %get-tuple-element.143.refs_0_, ...), custom_call_target="tpu_custom_call" | custom-call | flops 6442450944 | bytes 17065472 | tf_op jit(solution)/shard_map/rear_kernel/pallas_call | solution.py:600
  175.2 17.3 %merge_backward_kernel.1 = (f32[384,512]{1,0:T(8,128)}, f32[384,512]{1,0:T(8,128)}, f32[32,1024]{1,0:T(8,128)}, bf16[2,8,32,512]{3,2,1,0:T(8,128)(2,1)}, bf16[2,8,32,512]{3,2,1,0:T(8,128)(2,1)}) custom-call(s32[11]{0:T(128)} %concatenate.3.info_ref, f32[384,512]{1,0:T(8,128)} %get-tuple-element.145.refs_0_.refs_2_, f32[384,512]{1,0:T(8,128)} %get-tuple-element.134.refs_1_, ...), custom_call_target="tpu_custom_call" | custom-call | flops 6039797760 | bytes 11272192 | tf_op jit(solution)/shard_map/merge_backward_kernel/pallas_call | solution.py:600
  193.9 4.9 %core_sum_kernel.4.refs_0_ = bf16[4,4,128,512]{3,2,1,0:T(8,128)(2,1)} custom-call(s32[5]{0:T(128)} %stack.23.info_ref.info, f32[384,512]{1,0:T(8,128)} %get-tuple-element.147.refs_0_.refs_1_, bf16[2,4,2,128,512]{4,3,2,1,0:T(8,128)(2,1)} %bitcast.37, bf16[2,4,2,128,512]{4,3,2,1,0:T(8,128)(2,1)} %bitcast.38), custom_call_target="tpu_custom_call" | custom-call | bytes 6291456 | tf_op jit(solution)/shard_map/core_sum_kernel/pallas_call | solution.py:600
  203.0 14.8 %heads_backward_kernel.1 = (f32[384,512]{1,0:T(8,128)}, f32[1,512]{1,0:T(1,128)}, bf16[2,8,64,512]{3,2,1,0:T(8,128)(2,1)}, bf16[2,8,64,512]{3,2,1,0:T(8,128)(2,1)}) custom-call(s32[11]{0:T(128)} %concatenate.3.info_ref, bf16[4,4,128,512]{3,2,1,0:T(8,128)(2,1)} %core_sum_kernel.4.refs_0_, f32[384,512]{1,0:T(8,128)} %get-tuple-element.147.refs_0_.refs_1_, ...), custom_call_target="tpu_custom_call" | custom-call | flops 5234491392 | bytes 19662848 | tf_op jit(solution)/shard_map/heads_backward_kernel/pallas_call | solution.py:600
  217.8 11.5 %gated_linear_kernel.1 = (f32[384,1536]{1,0:T(8,128)}, f32[384,512]{1,0:T(8,128)}, bf16[2,8,96,512]{3,2,1,0:T(8,128)(2,1)}, bf16[2,8,96,512]{3,2,1,0:T(8,128)(2,1)}) custom-call(s32[11]{0:T(128)} %concatenate.3.info_ref, f32[384,512]{1,0:T(8,128)} %get-tuple-element.151.refs_0_.refs_3_, f32[384,512]{1,0:T(8,128)} %get-tuple-element.152.refs_1_, ...), custom_call_target="tpu_custom_call" | custom-call | flops 2818572288 | bytes 23068672 | tf_op jit(solution)/shard_map/gated_linear_kernel/pallas_call | solution.py:600
  236.4 5.6 %core_sum_kernel.5.refs_0_ = bf16[4,4,192,512]{3,2,1,0:T(8,128)(2,1)} custom-call(s32[5]{0:T(128)} %stack.23.info_ref.info, f32[128,512]{1,0:T(8,128)} %get-tuple-element.157.refs_0_.refs_1_, bf16[2,4,2,32,512]{4,3,2,1,0:T(8,128)(2,1)} %bitcast.46, bf16[2,4,2,96,512]{4,3,2,1,0:T(8,128)(2,1)} %bitcast.39, bf16[2,4,2,64,512]{4,3,2,1,0:T(8,128)(2,1)} %bitcast.42, ...), custom_call_target="tpu_custom_call" | custom-call | bytes 9437184 | tf_op jit(solution)/shard_map/core_sum_kernel/pallas_call | solution.py:600
  251.3 22.3 %gated_conv_kernel.1 = (f32[384,1536]{1,0:T(8,128)}, f32[1,1536]{1,0:T(1,128)}, f32[32,1536]{1,0:T(8,128)}) custom-call(s32[11]{0:T(128)} %concatenate.3.info_ref, bf16[4,4,192,512]{3,2,1,0:T(8,128)(2,1)} %core_sum_kernel.5.refs_0_, f32[384,1536]{1,0:T(8,128)} %get-tuple-element.164.refs_1_, f32[384,1536]{1,0:T(8,128)} %get-tuple-element.165.refs_2_, ...), custom_call_target="tpu_custom_call" | custom-call | flops 7247757312 | bytes 7484928 | tf_op jit(solution)/shard_map/gated_conv_kernel/pallas_call | solution.py:600
  273.6 8.9 %gated_gate_kernel.1 = (f32[384,512]{1,0:T(8,128)}, f32[1,512]{1,0:T(1,128)}, bf16[2,8,48,512]{3,2,1,0:T(8,128)(2,1)}, bf16[2,8,48,512]{3,2,1,0:T(8,128)(2,1)}) custom-call(s32[11]{0:T(128)} %concatenate.3.info_ref, f32[384,1536]{1,0:T(8,128)} %get-tuple-element.169.refs_0_, f32[384,512]{1,0:T(8,128)} %get-tuple-element.128.refs_0_.refs_1_.refs_2_, ...), custom_call_target="tpu_custom_call" | custom-call | flops 2415919104 | bytes 17829888 | tf_op jit(solution)/shard_map/gated_gate_kernel/pallas_call | solution.py:600
  289.7 9.0 %front_hidden_kernel.1 = (f32[384,512]{1,0:T(8,128)}, bf16[384,2048]{1,0:T(8,128)(2,1)}, bf16[2,8,64,512]{3,2,1,0:T(8,128)(2,1)}, bf16[2,8,64,512]{3,2,1,0:T(8,128)(2,1)}) custom-call(s32[11]{0:T(128)} %concatenate.3.info_ref, bf16[2,8,16,512]{3,2,1,0:T(8,128)(2,1)} %get-tuple-element.176.refs_0_, f32[16,2048]{1,0:T(8,128)} %get-tuple-element.112.refs_1_, ...), custom_call_target="tpu_custom_call" | custom-call | flops 2415919104 | bytes 14680064 | tf_op jit(solution)/shard_map/front_hidden_kernel/pallas_call | solution.py:600
  304.7 4.9 %core_sum_kernel.6.refs_0_ = bf16[4,4,128,512]{3,2,1,0:T(8,128)(2,1)} custom-call(s32[5]{0:T(128)} %stack.23.info_ref.info, f32[192,512]{1,0:T(8,128)} %get-tuple-element.185.refs_0_.refs_1_, bf16[2,4,2,48,512]{4,3,2,1,0:T(8,128)(2,1)} %bitcast.45, bf16[2,4,2,64,512]{4,3,2,1,0:T(8,128)(2,1)} %bitcast.44, bf16[2,4,2,16,512]{4,3,2,1,0:T(8,128)(2,1)} %bitcast.47, ...), custom_call_target="tpu_custom_call" | custom-call | bytes 6291456 | tf_op jit(solution)/shard_map/core_sum_kernel/pallas_call | solution.py:600
  313.8 8.9 %front_input_kernel.1 = (bf16[384,512]{1,0:T(8,128)(2,1)}, bf16[2,8,80,512]{3,2,1,0:T(8,128)(2,1)}, bf16[2,8,80,512]{3,2,1,0:T(8,128)(2,1)}) custom-call(s32[11]{0:T(128)} %concatenate.3.info_ref, bf16[4,4,128,512]{3,2,1,0:T(8,128)(2,1)} %core_sum_kernel.6.refs_0_, f32[384,512]{1,0:T(8,128)} %get-tuple-element.183.refs_0_.refs_1_, ...), custom_call_target="tpu_custom_call" | custom-call | flops 2415919104 | bytes 10487808 | tf_op jit(solution)/shard_map/front_input_kernel/pallas_call | solution.py:600
  326.8 5.8 %collective-permute-done.22.refs_2_ = bf16[192,512]{1,0:T(8,128)(2,1)S(1)} collective-permute-done((bf16[192,512]{1,0:T(8,128)(2,1)S(1)}, bf16[192,512]{1,0:T(8,128)(2,1)S(1)}, u32[]{:S(2)}, u32[]{:S(2)}) %collective-permute-start.22) | collective-permute-done | bytes 196640 | tf_op jit(solution)/shard_map/ppermute | solution.py:1243
  332.6 7.5 %collective-permute-done.23.refs_3_ = bf16[192,512]{1,0:T(8,128)(2,1)S(1)} collective-permute-done((bf16[192,512]{1,0:T(8,128)(2,1)S(1)}, bf16[192,512]{1,0:T(8,128)(2,1)S(1)}, u32[]{:S(2)}, u32[]{:S(2)}) %collective-permute-start.23) | collective-permute-done | bytes 196640 | tf_op jit(solution)/shard_map/ppermute | solution.py:1243
  (164 shorter events, 144.4 us)
Async XLA Ops:
  4.0 9.7 %collective-permute-start.2 = (bf16[144,512]{1,0:T(8,128)(2,1)}, bf16[144,512]{1,0:T(8,128)(2,1)S(1)}, u32[]{:S(2)}, u32[]{:S(2)}) collective-permute-start(bf16[144,512]{1,0:T(8,128)(2,1)} %get-tuple-element.123.refs_0_), channel_id=1, source_target_pairs={{0,6},{2,0},{4,2},{6,4},{1,7},{3,1},{5,3},{7,5},{8,14},{10,8},{12,... | collective-permute-start | bytes 442376 | tf_op jit(solution)/shard_map/ppermute | solution.py:1001
  9.0 12.7 %collective-permute-start.1 = (bf16[144,512]{1,0:T(8,128)(2,1)}, bf16[144,512]{1,0:T(8,128)(2,1)S(1)}, u32[]{:S(2)}, u32[]{:S(2)}) collective-permute-start(bf16[144,512]{1,0:T(8,128)(2,1)} %get-tuple-element.123.refs_0_), channel_id=1, source_target_pairs={{0,4},{2,6},{4,0},{6,2},{1,5},{3,7},{5,1},{7,3},{8,12},{10,14},{12... | collective-permute-start | bytes 442376 | tf_op jit(solution)/shard_map/ppermute | solution.py:1001
  9.0 12.7 %collective-permute-start = (bf16[144,512]{1,0:T(8,128)(2,1)}, bf16[144,512]{1,0:T(8,128)(2,1)S(1)}, u32[]{:S(2)}, u32[]{:S(2)}) collective-permute-start(bf16[144,512]{1,0:T(8,128)(2,1)} %get-tuple-element.123.refs_0_), channel_id=1, source_target_pairs={{0,2},{2,4},{4,6},{6,0},{1,3},{3,5},{5,7},{7,1},{8,10},{10,12},{12... | collective-permute-start | bytes 442376 | tf_op jit(solution)/shard_map/ppermute | solution.py:1001
  26.4 32.2 %all-to-all-start = ((bf16[4,4,144,512]{3,2,1,0:T(8,128)(2,1)}), bf16[4,4,144,512]{3,2,1,0:T(8,128)(2,1)}, u32[]{:S(2)}, u32[]{:S(2)}) async-start(bf16[4,4,144,512]{3,2,1,0:T(8,128)(2,1)} %place_line_kernel.3), calls=%async_computation | async-start | bytes 4718592 | tf_op jit(solution)/shard_map/all_to_all | solution.py:1005
  32.5 19.1 %collective-permute-start.4 = (bf16[208,512]{1,0:T(8,128)(2,1)S(1)}, bf16[208,512]{1,0:T(8,128)(2,1)S(1)}, u32[]{:S(2)}, u32[]{:S(2)}) collective-permute-start(bf16[208,512]{1,0:T(8,128)(2,1)S(1)} %copy-done.9), channel_id=1, source_target_pairs={{0,4},{2,6},{4,0},{6,2},{1,5},{3,7},{5,1},{7,3},{8,12},{10,14},{12... | collective-permute-start | bytes 638984 | tf_op jit(solution)/shard_map/ppermute | solution.py:1001
  33.4 18.3 %collective-permute-start.3 = (bf16[208,512]{1,0:T(8,128)(2,1)S(1)}, bf16[208,512]{1,0:T(8,128)(2,1)S(1)}, u32[]{:S(2)}, u32[]{:S(2)}) collective-permute-start(bf16[208,512]{1,0:T(8,128)(2,1)S(1)} %copy-done.9), channel_id=1, source_target_pairs={{0,2},{2,4},{4,6},{6,0},{1,3},{3,5},{5,7},{7,1},{8,10},{10,12},{12... | collective-permute-start | bytes 638984 | tf_op jit(solution)/shard_map/ppermute | solution.py:1001
  58.6 9.4 %collective-permute-start.6 = (bf16[4,4,144,512]{3,2,1,0:T(8,128)(2,1)}, bf16[4,4,144,512]{3,2,1,0:T(8,128)(2,1)}, u32[]{:S(2)}, u32[]{:S(2)}) collective-permute-start(bf16[4,4,144,512]{3,2,1,0:T(8,128)(2,1)} %all-to-all-done.refs_0_.refs_3_.refs_5_.refs_6_), channel_id=1, source_target_pairs={{0,8},{8,0},{1,9},{9,1},{2,10},{10,2},{3,11},{11,3},{4,12},{12,4},... | collective-permute-start | bytes 7077896 | tf_op jit(solution)/shard_map/ppermute | solution.py:1009
  58.6 43.6 %all-to-all-start.1 = ((bf16[4,4,208,512]{3,2,1,0:T(8,128)(2,1)}), bf16[4,4,208,512]{3,2,1,0:T(8,128)(2,1)S(1)}, u32[]{:S(2)}, u32[]{:S(2)}) async-start(bf16[4,4,208,512]{3,2,1,0:T(8,128)(2,1)} %place_line_kernel.4), calls=%async_computation.1 | async-start | bytes 6815744 | tf_op jit(solution)/shard_map/all_to_all | solution.py:1005
  64.0 15.7 %collective-permute-start.9 = (bf16[160,512]{1,0:T(8,128)(2,1)}, bf16[160,512]{1,0:T(8,128)(2,1)}, u32[]{:S(2)}, u32[]{:S(2)}) collective-permute-start(bf16[160,512]{1,0:T(8,128)(2,1)} %get-tuple-element.132.refs_1_), channel_id=1, source_target_pairs={{0,6},{2,0},{4,2},{6,4},{1,7},{3,1},{5,3},{7,5},{8,14},{10,8},{12,... | collective-permute-start | bytes 491528 | tf_op jit(solution)/shard_map/ppermute | solution.py:1001
  64.4 17.3 %collective-permute-start.8 = (bf16[160,512]{1,0:T(8,128)(2,1)}, bf16[160,512]{1,0:T(8,128)(2,1)}, u32[]{:S(2)}, u32[]{:S(2)}) collective-permute-start(bf16[160,512]{1,0:T(8,128)(2,1)} %get-tuple-element.132.refs_1_), channel_id=1, source_target_pairs={{0,4},{2,6},{4,0},{6,2},{1,5},{3,7},{5,1},{7,3},{8,12},{10,14},{12... | collective-permute-start | bytes 491528 | tf_op jit(solution)/shard_map/ppermute | solution.py:1001
  66.0 15.7 %collective-permute-start.7 = (bf16[160,512]{1,0:T(8,128)(2,1)}, bf16[160,512]{1,0:T(8,128)(2,1)}, u32[]{:S(2)}, u32[]{:S(2)}) collective-permute-start(bf16[160,512]{1,0:T(8,128)(2,1)} %get-tuple-element.132.refs_1_), channel_id=1, source_target_pairs={{0,2},{2,4},{4,6},{6,0},{1,3},{3,5},{5,7},{7,1},{8,10},{10,12},{12... | collective-permute-start | bytes 491528 | tf_op jit(solution)/shard_map/ppermute | solution.py:1001
  104.0 35.7 %all-to-all-start.2 = ((bf16[4,4,160,512]{3,2,1,0:T(8,128)(2,1)}), bf16[4,4,160,512]{3,2,1,0:T(8,128)(2,1)}, u32[]{:S(2)}, u32[]{:S(2)}) async-start(bf16[4,4,160,512]{3,2,1,0:T(8,128)(2,1)} %place_line_kernel.5), calls=%async_computation.2 | async-start | bytes 5242880 | tf_op jit(solution)/shard_map/all_to_all | solution.py:1005
  175.1 17.5 %collective-permute-start.12 = (bf16[2,8,128,512]{3,2,1,0:T(8,128)(2,1)}, bf16[2,8,128,512]{3,2,1,0:T(8,128)(2,1)S(1)}, u32[]{:S(2)}, u32[]{:S(2)}) collective-permute-start(bf16[2,8,128,512]{3,2,1,0:T(8,128)(2,1)} %get-tuple-element.149), channel_id=1, source_target_pairs={{0,8},{8,0},{1,9},{9,1},{2,10},{10,2},{3,11},{11,3},{4,12},{12,4},... | collective-permute-start | bytes 6291464 | tf_op jit(solution)/shard_map/ppermute | solution.py:1009
  198.8 31.2 %all-to-all-start.3 = ((bf16[4,4,128,512]{3,2,1,0:T(8,128)(2,1)}), bf16[4,4,128,512]{3,2,1,0:T(8,128)(2,1)S(1)}, u32[]{:S(2)}, u32[]{:S(2)}) async-start(bf16[4,4,128,512]{3,2,1,0:T(8,128)(2,1)} %core_sum_kernel.4.refs_0_), calls=%async_computation.3 | async-start | bytes 4194304 | tf_op jit(solution)/shard_map/all_to_all | solution.py:1005
  242.0 57.3 %all-to-all-start.4 = ((bf16[4,4,192,512]{3,2,1,0:T(8,128)(2,1)}), bf16[4,4,192,512]{3,2,1,0:T(8,128)(2,1)S(1)}, u32[]{:S(2)}, u32[]{:S(2)}) async-start(bf16[4,4,192,512]{3,2,1,0:T(8,128)(2,1)} %core_sum_kernel.5.refs_0_), calls=%async_computation.4 | async-start | bytes 6291456 | tf_op jit(solution)/shard_map/all_to_all | solution.py:1005
  246.3 40.1 %collective-permute-start.16 = (bf16[128,512]{1,0:T(8,128)(2,1)S(1)}, bf16[128,512]{1,0:T(8,128)(2,1)S(1)}, u32[]{:S(2)}, u32[]{:S(2)}) collective-permute-start(bf16[128,512]{1,0:T(8,128)(2,1)S(1)} %copy-done.34), channel_id=1, source_target_pairs={{0,2},{2,4},{4,6},{6,0},{1,3},{3,5},{5,7},{7,1},{8,10},{10,12},{12... | collective-permute-start | bytes 393224 | tf_op jit(solution)/shard_map/ppermute | solution.py:1243
  246.5 39.9 %collective-permute-start.17 = (bf16[128,512]{1,0:T(8,128)(2,1)S(1)}, bf16[128,512]{1,0:T(8,128)(2,1)S(1)}, u32[]{:S(2)}, u32[]{:S(2)}) collective-permute-start(bf16[128,512]{1,0:T(8,128)(2,1)S(1)} %copy-done.33), channel_id=1, source_target_pairs={{0,4},{2,6},{4,0},{6,2},{1,5},{3,7},{5,1},{7,3},{8,12},{10,14},{12... | collective-permute-start | bytes 393224 | tf_op jit(solution)/shard_map/ppermute | solution.py:1243
  248.4 38.0 %collective-permute-start.18 = (bf16[128,512]{1,0:T(8,128)(2,1)S(1)}, bf16[128,512]{1,0:T(8,128)(2,1)S(1)}, u32[]{:S(2)}, u32[]{:S(2)}) collective-permute-start(bf16[128,512]{1,0:T(8,128)(2,1)S(1)} %copy-done.32), channel_id=1, source_target_pairs={{0,6},{2,0},{4,2},{6,4},{1,7},{3,1},{5,3},{7,5},{8,14},{10,8},{12,... | collective-permute-start | bytes 393224 | tf_op jit(solution)/shard_map/ppermute | solution.py:1243
  309.6 39.4 %all-to-all-start.5 = ((bf16[4,4,128,512]{3,2,1,0:T(8,128)(2,1)}), bf16[4,4,128,512]{3,2,1,0:T(8,128)(2,1)S(1)}, u32[]{:S(2)}, u32[]{:S(2)}) async-start(bf16[4,4,128,512]{3,2,1,0:T(8,128)(2,1)} %core_sum_kernel.6.refs_0_), calls=%async_computation.5 | async-start | bytes 4194304 | tf_op jit(solution)/shard_map/all_to_all | solution.py:1005
  322.8 20.7 %collective-permute-start.25 = (bf16[2,8,80,512]{3,2,1,0:T(8,128)(2,1)}, bf16[2,8,80,512]{3,2,1,0:T(8,128)(2,1)S(1)}, u32[]{:S(2)}, u32[]{:S(2)}) collective-permute-start(bf16[2,8,80,512]{3,2,1,0:T(8,128)(2,1)} %get-tuple-element.198), channel_id=1, source_target_pairs={{0,8},{8,0},{1,9},{9,1},{2,10},{10,2},{3,11},{11,3},{4,12},{12,4},... | collective-permute-start | bytes 3932168 | tf_op jit(solution)/shard_map/ppermute | solution.py:1009
  323.0 9.7 %collective-permute-start.22 = (bf16[192,512]{1,0:T(8,128)(2,1)S(1)}, bf16[192,512]{1,0:T(8,128)(2,1)S(1)}, u32[]{:S(2)}, u32[]{:S(2)}) collective-permute-start(bf16[192,512]{1,0:T(8,128)(2,1)S(1)} %copy-done.31), channel_id=1, source_target_pairs={{0,2},{2,4},{4,6},{6,0},{1,3},{3,5},{5,7},{7,1},{8,10},{10,12},{12... | collective-permute-start | bytes 589832 | tf_op jit(solution)/shard_map/ppermute | solution.py:1243
  323.0 17.2 %collective-permute-start.23 = (bf16[192,512]{1,0:T(8,128)(2,1)S(1)}, bf16[192,512]{1,0:T(8,128)(2,1)S(1)}, u32[]{:S(2)}, u32[]{:S(2)}) collective-permute-start(bf16[192,512]{1,0:T(8,128)(2,1)S(1)} %copy-done.30), channel_id=1, source_target_pairs={{0,4},{2,6},{4,0},{6,2},{1,5},{3,7},{5,1},{7,3},{8,12},{10,14},{12... | collective-permute-start | bytes 589832 | tf_op jit(solution)/shard_map/ppermute | solution.py:1243
  323.9 16.2 %collective-permute-start.24 = (bf16[192,512]{1,0:T(8,128)(2,1)S(1)}, bf16[192,512]{1,0:T(8,128)(2,1)S(1)}, u32[]{:S(2)}, u32[]{:S(2)}) collective-permute-start(bf16[192,512]{1,0:T(8,128)(2,1)S(1)} %copy-done.29), channel_id=1, source_target_pairs={{0,6},{2,0},{4,2},{6,4},{1,7},{3,1},{5,3},{7,5},{8,14},{10,8},{12,... | collective-permute-start | bytes 589832 | tf_op jit(solution)/shard_map/ppermute | solution.py:1243
  349.0 24.0 %all-to-all-start.6 = ((bf16[4,4,80,512]{3,2,1,0:T(8,128)(2,1)}), bf16[4,4,80,512]{3,2,1,0:T(8,128)(2,1)S(1)}, u32[]{:S(2)}, u32[]{:S(2)}) async-start(bf16[4,4,80,512]{3,2,1,0:T(8,128)(2,1)} %core_sum_kernel.7.refs_0_), calls=%async_computation.6 | async-start | bytes 2621440 | tf_op jit(solution)/shard_map/all_to_all | solution.py:1005
  (51 other events, 226.5 us)

commit v3 on v2

--- a/solution.py
+++ b/solution.py
@@ -13,6 +13,9 @@
 TILE = 8
 GAP = 16
 CHAN = 128
+PLACE = 1
+OWNER = 5
+SEG = 6
 WIDTH = 512
 BLOCKS = 32
 F32 = jnp.float32
@@ -43,6 +46,10 @@
     mean_scaled = jnp.mean(scaled, axis=-1, keepdims=True)
     mean_cross = jnp.mean(scaled * normal, axis=-1, keepdims=True)
     return inverse * (scaled - mean_scaled - normal * mean_cross)
+
+
+def part_of(index):
+    return slice(None), pl.ds(pl.multiple_of(index * WIDTH, WIDTH), WIDTH)
 
 
 def row_sum(values):
@@ -99,7 +106,7 @@
 
 def visits(info, segments, body):
     for s in range(segments):
-        begin, end = info[1 + s], info[1 + segments + s]
+        begin, end = info[SEG + s], info[SEG + segments + s]
 
         def visit(i, _, s=s, begin=begin, end=end):
             row = i * TILE + lax.broadcasted_iota(jnp.int32, (TILE, CHAN), 0)
@@ -220,14 +227,11 @@
     return exponent / jnp.sum(exponent, axis=-1, keepdims=True)
 
 
-def heads_forward_kernel(
-    info, x_ref, gain, segs_col, segs_row, w_in, w_in_two, w_out, w_out_two,
-    attended, packed, mixed,
+def heads_forward(
+    info, low, segs_col, segs_row, w_in, w_in_two, w_out, w_out_two, attended, packed, mixed,
 ):
     mine = info[0]
     scale = (WIDTH // HEADS) ** -0.5
-    normal, _ = normalize(x_ref[...])
-    low = (normal * gain[...]).astype(LOW)
     for q in range(3):
         rows = slice(16 * q, 16 * (q + 1))
         weight = join_rows(w_in[:, :, rows, :], w_in_two[:, :, rows, :], mine)
@@ -250,14 +254,14 @@
     attended[...] = dot(mixed[...], join_rows(w_out[...], w_out_two[...], mine))
 
 
-def heads_backward_kernel(
+def heads_backward(
     info, grad, x_ref, gain, segs_col, segs_row, packed, mixed, w_in, w_in_two, w_out, w_out_two,
     stream, gain_grad, send, keep, mixed_grad, packed_grad, low,
 ):
     scale = (WIDTH // HEADS) ** -0.5
     mine = info[0]
     attended_low = grad[...].astype(LOW)
-    store_halves(dot_tn(mixed[...], attended_low), send, keep, mine, 16, 48)
+    store_halves(dot_tn(mixed[...], attended_low), send, keep, mine, 16, 144)
     mixed_grad[...] = dot_nt(attended_low, join_rows(w_out[...], w_out_two[...], mine)).astype(LOW)
     normal, inverse = normalize(x_ref[...])
     low[...] = (normal * gain[...]).astype(LOW)
@@ -289,14 +293,15 @@
         rows = slice(16 * q, 16 * (q + 1))
         weight = join_rows(w_in[:, :, rows, :], w_in_two[:, :, rows, :], mine)
         piece = packed_grad[:, WIDTH * q : WIDTH * (q + 1)]
-        store_halves(dot_tn(low[...], piece), send, keep, mine, 16, 16 * q)
+        store_halves(dot_tn(low[...], piece), send, keep, mine, 16, 96 + 16 * q)
         total += dot_nt(piece, weight)
     gain_grad[...] = row_sum(total * normal)
     stream[...] = normalize_back(total, gain[...], normal, inverse)
 
 
-def gated_forward_kernel(
-    info, x_ref, gain, gate_gain, taps_ref, w_in, w_in_two, w_out, w_out_two,
+def branches_forward_kernel(
+    info, x_ref, heads_gain, segs_col, segs_row, w_heads, w_heads_two, w_mix, w_mix_two,
+    gain, gate_gain, taps_ref, w_in, w_in_two, w_out, w_out_two, attended, packed, mixed,
     gated, before_out, normal_out, inverse_out, part_out, product,
     low, act, padded, conv, *, segments, row_block, taps,
 ):
@@ -307,6 +312,10 @@
     def _():
         normal, _ = normalize(x_ref[...])
         low[...] = (normal * gain[...]).astype(LOW)
+        heads_forward(
+            info, (normal * heads_gain[...]).astype(LOW), segs_col, segs_row, w_heads,
+            w_heads_two, w_mix, w_mix_two, attended, packed, mixed,
+        )
 
     before = dot(low[...], join_rows(w_in[...], w_in_two[...], info[0]))
     before_out[...] = before
@@ -337,15 +346,23 @@
         gated[...] = dot(product[...], join_rows(w_out[...], w_out_two[...], info[0]))
 
 
-def gated_linear_kernel(
-    info, grad, x_ref, gain, before, part, product, w_in, w_in_two, w_out, w_out_two,
-    part_grad, total_out, send, keep, low, product_grad, gated_low,
+def branches_backward_kernel(
+    info, attended_grad, x_ref, heads_gain, segs_col, segs_row, packed, mixed, w_heads,
+    w_heads_two, w_mix, w_mix_two, grad, gain, before, part, product, w_in, w_in_two, w_out,
+    w_out_two,
+    stream, heads_gain_grad, part_grad, total_out, send, keep, low, product_grad, gated_low,
+    mixed_grad, packed_grad,
 ):
     j = pl.program_id(0)
     mine = info[0]
 
     @pl.when(j == 0)
     def _():
+        heads_backward(
+            info, attended_grad, x_ref, heads_gain, segs_col, segs_row, packed, mixed, w_heads,
+            w_heads_two, w_mix, w_mix_two, stream, heads_gain_grad, send, keep, mixed_grad,
+            packed_grad, low,
+        )
         normal, _ = normalize(x_ref[...])
         low[...] = (normal * gain[...]).astype(LOW)
         total_out[...] = jnp.zeros_like(total_out)
@@ -364,10 +381,9 @@
     total_out[...] += dot_nt(before_grad, join_rows(w_in[...], w_in_two[...], mine))
 
 
-def gated_conv_kernel(
+def gated_conv(
     info, part_grad, normal_ref, inverse_ref, gate_gain, taps_ref,
-    gate_grad, gate_gain_grad, taps_grad, padded, padded_grad, conv, work,
-    *, segments, row_block, taps,
+    gate_gain_grad, taps_grad, padded, padded_grad, conv, work, segments, row_block, taps,
 ):
     blocks = 3 * WIDTH // CHAN
     spread(part_grad, padded_grad, info, segments, blocks)
@@ -379,24 +395,30 @@
     upstream = work[...]
     normal = normal_ref[...]
     gate_gain_grad[...] = row_sum(upstream * normal)
-    gate_grad[...] = normalize_back(upstream, gate_gain[...], normal, inverse_ref[...])
+    work[...] = normalize_back(upstream, gate_gain[...], normal, inverse_ref[...])
 
 
 def gated_gate_kernel(
-    info, gate_grad, x_ref, gain, before, total_in, w_in, w_in_two,
-    stream, gain_grad, send, keep, low, total,
+    info, part_grad, normal_ref, inverse_ref, gate_gain, taps_ref, x_ref, gain, before, total_in,
+    w_in, w_in_two,
+    stream, gain_grad, gate_gain_grad, taps_grad, send, keep,
+    low, total, padded, padded_grad, conv, work, *, segments, row_block, taps,
 ):
     j = pl.program_id(0)
     mine = info[0]
 
     @pl.when(j == 0)
     def _():
+        gated_conv(
+            info, part_grad, normal_ref, inverse_ref, gate_gain, taps_ref, gate_gain_grad,
+            taps_grad, padded, padded_grad, conv, work, segments, row_block, taps,
+        )
         normal, _ = normalize(x_ref[...])
         low[...] = (normal * gain[...]).astype(LOW)
         total[...] = total_in[...]
 
     _, slope = gelu_pair(before[...])
-    before_grad = (gate_grad[...] * slope).astype(LOW)
+    before_grad = (work[part_of(j)] * slope).astype(LOW)
     store_halves(
         dot_tn(low[...], before_grad), send, keep, mine, 16, pl.multiple_of(j * 16, 16)
     )
@@ -409,48 +431,10 @@
         stream[...] = normalize_back(total[...], gain[...], normal, inverse)
 
 
-def merge_forward_kernel(
-    info, x_ref, attended, gated, taps_ref, valid, weight, weight_two,
-    out, merged_low, stat, joined, padded, conv, *, segments, row_block, taps,
-):
-    blocks = 2 * WIDTH // CHAN
-    joined[:, :WIDTH] = attended[...]
-    joined[:, WIDTH:] = gated[...]
-    spread(joined, padded, info, segments, blocks)
-    conv_rows(padded, taps_ref, conv, blocks, row_block, taps, False)
+def conv_add(padded, conv, taps_ref, blocks, row_block, taps, flip):
+    conv_rows(padded, taps_ref, conv, blocks, row_block, taps, flip)
     for c in range(blocks):
         conv[c] += padded[c]
-    unspread(conv, joined, info, segments, blocks)
-    merged_low[...] = joined[...].astype(LOW)
-    part = dot(merged_low[...], join_rows(weight[...], weight_two[...], info[0]))
-    after = x_ref[...] + part
-    out[...] = after
-    v = valid[...]
-    stat[0:1, :] = row_sum(after * after * v)
-    stat[1:2, :] = row_sum(part * part * v)
-    stat[2:, :] = jnp.zeros((6, WIDTH), F32)
-
-
-def merge_backward_kernel(
-    info, grad, attended, gated, merged_low, taps_ref, weight, weight_two,
-    attended_grad, gated_grad, taps_grad, send, keep,
-    joined, padded, padded_grad, conv, *, segments, row_block, taps,
-):
-    blocks = 2 * WIDTH // CHAN
-    low = grad[...].astype(LOW)
-    store_halves(dot_tn(merged_low[...], low), send, keep, info[0], 32, 0)
-    joined[:, :WIDTH] = attended[...]
-    joined[:, WIDTH:] = gated[...]
-    spread(joined, padded, info, segments, blocks)
-    joined[...] = dot_nt(low, join_rows(weight[...], weight_two[...], info[0]))
-    spread(joined, padded_grad, info, segments, blocks)
-    conv_taps(padded_grad, padded, taps_grad, blocks, row_block, taps)
-    conv_rows(padded_grad, taps_ref, conv, blocks, row_block, taps, True)
-    for c in range(blocks):
-        conv[c] += padded_grad[c]
-    unspread(conv, joined, info, segments, blocks)
-    attended_grad[...] = joined[:, :WIDTH]
-    gated_grad[...] = joined[:, WIDTH:]
 
 
 def hidden_back(h, mine, before, part_low, down, send, keep, start):
@@ -471,19 +455,35 @@
     return before_grad
 
 
-def rear_kernel(
-    info, x_ref, gain, final_gain, valid, cotangent, up, up_two, down, down_two,
-    encoded, stream, gain_grad, final_gain_grad, stat,
-    send, keep, low, before, part_grad, stream_grad, total,
+def merge_rear_kernel(
+    info, x_ref, attended, gated, taps_ref, weight, weight_two, gain, final_gain, valid, cotangent,
+    up, up_two, down, down_two,
+    encoded, stream, gain_grad, final_gain_grad, stat, attended_grad, gated_grad, taps_grad,
+    send, keep, merge_send, merge_keep,
+    low, before, part_grad, stream_grad, total, middle, joined, joined_low, padded, padded_grad,
+    conv, *, segments, row_block, taps,
 ):
     step = pl.program_id(0)
     h = jnp.where(step < 4, step, 7 - step)
     up_value = join_rows(up[...], up_two[...], info[0])
     down_value = pick_rows(down[...], down_two[...], h % 2 == info[0])
+    blocks = 2 * WIDTH // CHAN
 
     @pl.when(step == 0)
     def _():
-        normal, _ = normalize(x_ref[...])
+        joined[:, :WIDTH] = attended[...]
+        joined[:, WIDTH:] = gated[...]
+        spread(joined, padded, info, segments, blocks)
+        conv_add(padded, conv, taps_ref, blocks, row_block, taps, False)
+        unspread(conv, joined, info, segments, blocks)
+        joined_low[...] = joined[...].astype(LOW)
+        part = dot(joined_low[...], join_rows(weight[...], weight_two[...], info[0]))
+        after = x_ref[...] + part
+        middle[...] = after
+        v = valid[...]
+        stat[0:1, :] = row_sum(after * after * v)
+        stat[1:2, :] = row_sum(part * part * v)
+        normal, _ = normalize(after)
         low[...] = (normal * gain[...]).astype(LOW)
         total[...] = jnp.zeros_like(total)
 
@@ -496,11 +496,11 @@
     @pl.when(step == 3)
     def _():
         part = 0.5 * total[...]
-        after = x_ref[...] + part
+        after = middle[...] + part
         v = valid[...]
-        stat[0:1, :] = row_sum(after * after * v)
-        stat[1:2, :] = row_sum(part * part * v)
-        stat[2:, :] = jnp.zeros((6, WIDTH), F32)
+        stat[2:3, :] = row_sum(after * after * v)
+        stat[3:4, :] = row_sum(part * part * v)
+        stat[4:, :] = jnp.zeros((4, WIDTH), F32)
         normal, inverse = normalize(after)
         encoded[...] = (normal * final_gain[...] * v).astype(LOW)
         upstream = cotangent[...].astype(F32) * v
@@ -522,9 +522,19 @@
 
     @pl.when(step == 7)
     def _():
-        normal, inverse = normalize(x_ref[...])
+        normal, inverse = normalize(middle[...])
         gain_grad[...] = row_sum(total[...] * normal)
-        stream[...] = stream_grad[...] + normalize_back(total[...], gain[...], normal, inverse)
+        grad = stream_grad[...] + normalize_back(total[...], gain[...], normal, inverse)
+        stream[...] = grad
+        grad_low = grad.astype(LOW)
+        store_halves(dot_tn(joined_low[...], grad_low), merge_send, merge_keep, info[0], 32, 0)
+        joined[...] = dot_nt(grad_low, join_rows(weight[...], weight_two[...], info[0]))
+        spread(joined, padded_grad, info, segments, blocks)
+        conv_taps(padded_grad, padded, taps_grad, blocks, row_block, taps)
+        conv_add(padded_grad, conv, taps_ref, blocks, row_block, taps, True)
+        unspread(conv, joined, info, segments, blocks)
+        attended_grad[...] = joined[:, :WIDTH]
+        gated_grad[...] = joined[:, WIDTH:]
 
 
 def front_hidden_kernel(
@@ -613,14 +623,13 @@
     )(info, *after, *arrays)
 
 
-def segment_table(lengths, mine, row_count):
+def segment_table(lengths, spots, row_count):
     ends = jnp.cumsum(lengths)
     position = jnp.arange(row_count, dtype=jnp.int32)
     segments = jnp.sum((position[None, :] >= ends[:, None]).astype(jnp.int32), axis=0)
     zero = jnp.zeros((1,), jnp.int32)
     last = jnp.full((1,), row_count, jnp.int32)
-    info = jnp.concatenate([jnp.full((1,), mine, jnp.int32), zero, ends, ends, last])
-    return segments, info.astype(jnp.int32)
+    return segments, jnp.concatenate([spots, zero, ends, ends, last]).astype(jnp.int32)
 
 
 def all_of(*arrays):
@@ -654,12 +663,12 @@
 
 
 class Layer:
-    def __init__(self, features, cotangent, lengths, mine, taps):
+    def __init__(self, features, cotangent, lengths, spots, taps):
         self.features, self.cotangent, self.taps = features, cotangent, taps
         self.tokens = features.shape[0]
         self.count = lengths.shape[0]
         self.segments = self.count + 1
-        seg_ids, self.info = segment_table(lengths, mine, self.tokens)
+        seg_ids, self.info = segment_table(lengths, spots, self.tokens)
         self.segs_col, self.segs_row = seg_ids[:, None], seg_ids[None, :]
         self.valid = (self.segs_col < self.count).astype(F32)
         self.stream = ((self.tokens, WIDTH), F32)
@@ -706,165 +715,120 @@
         )
         return self.front_stat
 
-    def heads_forward(self, heads, after=()):
-        self.heads = columns(heads, 48, 144, first) + columns(heads, 16, 192, first)
-        self.attended, self.packed, self.mixed = call(
-            heads_forward_kernel,
-            (1,),
-            all_of(self.after_front, self.heads_gain, self.segs_col, self.segs_row) + self.heads,
-            plain(self.stream, self.tall(3 * WIDTH, LOW), self.tall(WIDTH, LOW)),
-            [],
-            self.info,
-            16 * self.flop,
-            after,
-        )
-        return self.mixed
-
-    def gated_forward(self, gated, after=()):
-        self.gated_weights = gated
+    def branches_forward(self, middle, after=()):
+        self.middle = middle
+        self.heads = columns(middle, 48, 144, first) + columns(middle, 16, 192, first)
         (
-            self.gated, self.gated_before, self.gate_normal, self.gate_inverse, self.gate_part,
-            self.product,
+            self.attended, self.packed, self.mixed, self.gated, self.gated_before,
+            self.gate_normal, self.gate_inverse, self.gate_part, self.product,
         ) = call(
-            functools.partial(gated_forward_kernel, **self.conv),
+            functools.partial(branches_forward_kernel, **self.conv),
             (6,),
-            all_of(self.after_front, self.gated_gain, self.gate_gain, self.gate_taps)
-            + columns(gated, 16, 0, lambda j, _: (j + 3) % 6)
-            + columns(gated, 48, 96, first),
-            plain(self.stream)
+            all_of(self.after_front, self.heads_gain, self.segs_col, self.segs_row)
+            + self.heads
+            + all_of(self.gated_gain, self.gate_gain, self.gate_taps)
+            + columns(middle, 16, 0, lambda j, _: (j + 3) % 6)
+            + columns(middle, 48, 96, first),
+            plain(self.stream, self.tall(3 * WIDTH, LOW), self.tall(WIDTH, LOW), self.stream)
             + [(*self.tall(6 * WIDTH), (self.tokens, WIDTH), lambda j, _: (0, (j + 3) % 6))]
             + plain(
                 self.tall(3 * WIDTH), self.tall(1), self.tall(3 * WIDTH), self.tall(3 * WIDTH, LOW)
             ),
             [self.low, pltpu.VMEM((self.tokens, 3 * WIDTH), F32)] + [self.padded(3 * WIDTH)] * 2,
             self.info,
-            36 * self.flop,
+            52 * self.flop,
             after,
         )
         return self.gate_inverse
 
-    def merge_forward(self, rear, after=()):
-        self.rear = rear
-        self.merge_weight = columns(rear, 32, 128, first)
-        self.after_merge, self.merged_low, self.merge_stat = call(
-            functools.partial(merge_forward_kernel, **self.conv),
-            (1,),
-            all_of(self.after_front, self.attended, self.gated, self.merge_taps, self.valid)
-            + self.merge_weight,
-            plain(self.stream, self.tall(2 * WIDTH, LOW), self.stat),
-            [pltpu.VMEM((self.tokens, 2 * WIDTH), F32)] + [self.padded(2 * WIDTH)] * 2,
-            self.info,
-            18 * self.flop,
-            after,
-        )
-        return self.merge_stat
-
-    def rear_both(self, after=()):
+    def merge_rear(self, rear, after=()):
         def bounce(i, _):
             return jnp.where(i < 4, i, 7 - i)
 
+        padded = self.padded(2 * WIDTH)
         (
             self.encoded, self.merge_grad, self.rear_gain_grad, self.final_gain_grad,
-            self.rear_stat, *pair,
+            self.rear_stat, self.attended_grad, self.gated_grad, self.merge_taps_grad, *pair,
         ) = call(
-            rear_kernel,
+            functools.partial(merge_rear_kernel, **self.conv),
             (8,),
-            all_of(self.after_merge, self.rear_gain, self.final_gain, self.valid, self.cotangent)
-            + columns(self.rear, 16, 0, bounce)
-            + lines(self.rear, bounce),
-            plain(self.tall(WIDTH, LOW), self.stream, self.vector, self.vector, self.stat)
-            + halves(128),
-            [self.low, pltpu.VMEM((4, self.tokens, WIDTH), F32), self.low, self.wide, self.wide],
+            all_of(self.after_front, self.attended, self.gated, self.merge_taps)
+            + columns(rear, 32, 128, first)
+            + all_of(self.rear_gain, self.final_gain, self.valid, self.cotangent)
+            + columns(rear, 16, 0, bounce)
+            + lines(rear, bounce),
+            plain(
+                self.tall(WIDTH, LOW), self.stream, self.vector, self.vector, self.stat,
+                self.stream, self.stream, ((self.taps + 1, 2 * WIDTH), F32),
+            )
+            + halves(128)
+            + halves(32),
+            [
+                self.low, pltpu.VMEM((4, self.tokens, WIDTH), F32), self.low, self.wide, self.wide,
+                self.wide, pltpu.VMEM((self.tokens, 2 * WIDTH), F32),
+                pltpu.VMEM((self.tokens, 2 * WIDTH), LOW), padded, padded, padded,
+            ],
             self.info,
-            32 * self.flop,
+            80 * self.flop,
             after,
         )
         return pair
 
-    def merge_backward(self, after=()):
-        self.attended_grad, self.gated_grad, self.merge_taps_grad, *pair = call(
-            functools.partial(merge_backward_kernel, **self.conv),
-            (1,),
-            all_of(
-                self.merge_grad, self.attended, self.gated, self.merged_low, self.merge_taps
-            )
-            + self.merge_weight,
-            plain(self.stream, self.stream, ((self.taps + 1, 2 * WIDTH), F32)) + halves(32),
-            [pltpu.VMEM((self.tokens, 2 * WIDTH), F32)] + [self.padded(2 * WIDTH)] * 3,
-            self.info,
-            30 * self.flop,
-            after,
-        )
-        return pair
-
-    def heads_backward(self, after=()):
-        self.heads_stream, self.heads_gain_grad, *pair = call(
-            heads_backward_kernel,
-            (1,),
+    def branches_backward(self, after=()):
+        self.heads_stream, self.heads_gain_grad, self.part_grad, self.gated_total, *pair = call(
+            branches_backward_kernel,
+            (3,),
             all_of(
                 self.attended_grad, self.after_front, self.heads_gain, self.segs_col,
                 self.segs_row, self.packed, self.mixed,
             )
-            + self.heads,
-            plain(self.stream, self.vector) + halves(64),
-            [self.low, pltpu.VMEM((self.tokens, 3 * WIDTH), LOW), self.low],
+            + self.heads
+            + all_of(self.gated_grad, self.gated_gain)
+            + self.by_column(self.gated_before)
+            + self.by_column(self.gate_part)
+            + all_of(self.product)
+            + columns(self.middle, 16, 0, step)
+            + columns(self.middle, 48, 96, first),
+            plain(self.stream, self.vector)
+            + [(*self.tall(3 * WIDTH), (self.tokens, WIDTH), lambda j, _: (0, j))]
+            + plain(self.stream)
+            + halves(160),
+            [
+                self.low, pltpu.VMEM((self.tokens, 3 * WIDTH), F32), self.low, self.low,
+                pltpu.VMEM((self.tokens, 3 * WIDTH), LOW),
+            ],
             self.info,
-            26 * self.flop,
+            40 * self.flop,
             after,
         )
         return pair
 
-    def gated_linear(self, after=()):
-        self.part_grad, self.gated_total, *pair = call(
-            gated_linear_kernel,
+    def gated_gate(self, after=()):
+        padded = self.padded(3 * WIDTH)
+        (
+            self.gated_stream, self.gated_gain_grad, self.gate_gain_grad, self.gate_taps_grad,
+            *pair,
+        ) = call(
+            functools.partial(gated_gate_kernel, **self.conv),
             (3,),
-            all_of(self.gated_grad, self.after_front, self.gated_gain)
-            + self.by_column(self.gated_before)
-            + self.by_column(self.gate_part)
-            + all_of(self.product)
-            + columns(self.gated_weights, 16, 0, step)
-            + columns(self.gated_weights, 48, 96, first),
-            [(*self.tall(3 * WIDTH), (self.tokens, WIDTH), lambda j, _: (0, j))]
-            + plain(self.stream)
-            + halves(96),
-            [self.low, pltpu.VMEM((self.tokens, 3 * WIDTH), F32), self.low],
-            self.info,
-            14 * self.flop,
-            after,
-        )
-        return pair
-
-    def gated_conv(self, after=()):
-        self.gate_grad, self.gate_gain_grad, self.gate_taps_grad = call(
-            functools.partial(gated_conv_kernel, **self.conv),
-            (1,),
             all_of(
                 self.part_grad, self.gate_normal, self.gate_inverse, self.gate_gain,
-                self.gate_taps,
-            ),
-            plain(
-                self.tall(3 * WIDTH), ((1, 3 * WIDTH), F32), ((self.taps + 1, 3 * WIDTH), F32)
-            ),
-            [self.padded(3 * WIDTH)] * 3 + [pltpu.VMEM((self.tokens, 3 * WIDTH), F32)],
-            self.info,
-            36 * self.flop,
-            after,
-        )
-        return self.gate_gain_grad
-
-    def gated_gate(self, after=()):
-        self.gated_stream, self.gated_gain_grad, *pair = call(
-            gated_gate_kernel,
-            (3,),
-            self.by_column(self.gate_grad)
-            + all_of(self.after_front, self.gated_gain)
+                self.gate_taps, self.after_front, self.gated_gain,
+            )
             + self.by_column(self.gated_before, 3)
             + all_of(self.gated_total)
-            + columns(self.gated_weights, 16, 0, lambda j, _: j + 3),
-            plain(self.stream, self.vector) + halves(48),
-            [self.low, self.wide],
+            + columns(self.middle, 16, 0, lambda j, _: j + 3),
+            plain(
+                self.stream, self.vector, ((1, 3 * WIDTH), F32),
+                ((self.taps + 1, 3 * WIDTH), F32),
+            )
+            + halves(48),
+            [
+                self.low, self.wide, padded, padded, padded,
+                pltpu.VMEM((self.tokens, 3 * WIDTH), F32),
+            ],
             self.info,
-            12 * self.flop,
+            48 * self.flop,
             after,
         )
         return pair
@@ -909,7 +873,7 @@
         )
 
     def stats(self):
-        return self.front_stat, self.merge_stat, self.rear_stat
+        return self.front_stat, self.rear_stat
 
 
 SMALL = 16
@@ -966,7 +930,7 @@
     pieces, out, sem = refs[:4], refs[4], refs[5]
     copy_all(
         [
-            pltpu.make_async_copy(piece, out.at[chip, info[i]], sem.at[chip, i])
+            pltpu.make_async_copy(piece, out.at[chip, info[PLACE + i]], sem.at[chip, i])
             for chip in range(4)
             for i, piece in enumerate(pieces)
         ]
@@ -1052,15 +1016,15 @@
 
 def pack_small_kernel(
     info, gate_taps, merge_taps, heads_gain, gated_gain, rear_gain, final_gain, gate_gain,
-    front_stat, merge_stat, rear_stat, send, keep, *, count_at,
+    front_stat, rear_stat, send, keep, *, count_at,
 ):
     mine = info[0]
     lane = lax.broadcasted_iota(jnp.int32, (SMALL, CHAN), 1)
     lane_row = lane[:1]
     last = lax.broadcasted_iota(jnp.int32, (SMALL, CHAN), 0) == SMALL - 1
     stats = [
-        front_stat[0:1, :], front_stat[1:2, :], merge_stat[0:1, :], rear_stat[0:1, :],
-        front_stat[2:3, :], merge_stat[1:2, :], rear_stat[1:2, :],
+        front_stat[0:1, :], front_stat[1:2, :], rear_stat[0:1, :], rear_stat[2:3, :],
+        front_stat[2:3, :], rear_stat[1:2, :], rear_stat[3:4, :],
     ]
     stat_line = jnp.where(lane_row == 7, info[count_at].astype(F32), 0.0)
     for i, stat in enumerate(stats):
@@ -1116,21 +1080,27 @@
     inputs, out = refs[:-1], refs[-1]
     half = len(inputs) // 2
     keeps, gots = inputs[:half], inputs[half:]
-    for chip in range(4):
-        x, y = chip // 2, chip % 2
-        start = 0
-        for keep, got, (rows, small) in zip(keeps, gots, sizes):
-            if small:
-                total = keep[x, 0, y].astype(F32) + got[x, 0, y].astype(F32)
-                out[chip, 0, start : start + rows, :] = round_small(total)
-            else:
-                out[chip, 0, start : start + rows, :] = keep[x, 0, y] + got[x, 0, y]
-            start += rows
+
+    def one(z, _):
+        for chip in range(4):
+            x, spot = chip // 2, 2 * z + chip % 2
+            start = 0
+            for keep, got, (rows, small) in zip(keeps, gots, sizes):
+                span = slice(start, start + rows)
+                start += rows
+                if small:
+                    total = keep[x, spot].astype(F32) + got[x, spot].astype(F32)
+                    out[chip, z, span, :] = round_small(total)
+                else:
+                    out[chip, z, span, :] = keep[x, spot] + got[x, spot]
+        return 0
+
+    lax.fori_loop(0, 4, one, 0)
 
 
 def plane_sum_kernel(info, pieces, *outs, sizes):
     for e in range(4):
-        zi = lax.rem(info[0] + e, 4)
+        zi = lax.rem(info[PLACE] + e, 4)
         start = 0
         for rows in sizes:
             small, rows = rows < 0, abs(rows)
@@ -1170,7 +1140,7 @@
             frames = jnp.sum(line[:, STATS - 1 : STATS])
             stats[...] = jnp.sqrt(line[:, : STATS - 1] / (frames * WIDTH))
         elif what == "gain":
-            owner = info[4]
+            owner = info[OWNER]
             line = jnp.zeros((1, CHAN), F32)
             for b in range(WIDTH // CHAN):
                 block = total[0:1, CHAN * b : CHAN * (b + 1)]
@@ -1193,49 +1163,57 @@
                 target[:, lanes] = total[height * q : height * (q + 1), :]
 
 
-def core_sum(pairs, spots, after=()):
-    sizes = [(pair[0].shape[2], pair[0].shape[2] == SMALL) for pair in pairs]
-    arrays = [pair[i] for i in (0, 1) for pair in pairs]
-    arrays = [array.reshape(2, 4, 2, array.shape[2], WIDTH) for array in arrays]
-    total = sum(array.shape[3] for array in arrays) // 2
-    (out,) = call(
-        functools.partial(core_sum_kernel, sizes=tuple(sizes)),
-        (4,),
-        [
-            (array, (2, 1, 2, array.shape[3], WIDTH), lambda i, _: (0, i, 0, 0, 0))
-            for array in arrays
-        ],
-        [((4, 4, total, WIDTH), LOW, (4, 1, total, WIDTH), lambda i, _: (0, i, 0, 0))],
+def run(tasks, info, after=()):
+    counts = [(len(inputs), len(outputs)) for _, inputs, outputs in tasks]
+
+    def tasks_kernel(info_ref, *refs):
+        total = sum(count for count, _ in counts)
+        ins, outs = list(refs[:total]), list(refs[total:])
+        for (kernel, _, _), (taken, given) in zip(tasks, counts):
+            kernel(info_ref, *ins[:taken], *outs[:given])
+            del ins[:taken], outs[:given]
+
+    results = call(
+        tasks_kernel,
+        (1,),
+        all_of(*[array for _, inputs, _ in tasks for array in inputs]),
+        plain(*[output for _, _, outputs in tasks for output in outputs]),
         [],
-        spots,
+        info,
         after=after,
     )
-    return out
-
-
-def plane_sum(pieces, sizes, spots, after=()):
+    grouped = []
+    for _, given in counts:
+        grouped.append(results[:given])
+        results = results[given:]
+    return grouped
+
+
+def core_sum(pairs):
+    sizes = tuple((pair[0].shape[2], pair[0].shape[2] == SMALL) for pair in pairs)
+    total = sum(rows for rows, _ in sizes)
+    return (
+        functools.partial(core_sum_kernel, sizes=sizes),
+        [pair[i] for i in (0, 1) for pair in pairs],
+        [((4, 4, total, WIDTH), LOW)],
+    )
+
+
+def plane_sum(pieces, sizes):
     total = pieces.shape[2]
-    return call(
+    return (
         functools.partial(plane_sum_kernel, sizes=sizes),
-        (1,),
-        all_of(pieces),
-        plain(((total, WIDTH), F32), *[((total, WIDTH), LOW)] * 3),
-        [],
-        spots,
-        after=after,
-    )
-
-
-def line_sum(sums, pieces, outputs, spots, given=(), after=()):
+        [pieces],
+        [((total, WIDTH), F32)] + [((total, WIDTH), LOW)] * 3,
+    )
+
+
+def line_sum(sums, pieces, outputs, given=()):
     own, rest = sums
-    return call(
+    return (
         functools.partial(line_sum_kernel, pieces=pieces),
-        (1,),
-        all_of(own, *rest, *given),
-        plain(*[(shape, F32) for shape in outputs]),
-        [],
-        spots,
-        after=after,
+        [own, *rest, *given],
+        [(shape, F32) for shape in outputs],
     )
 
 
@@ -1243,19 +1221,15 @@
     return sums[0], [lax.ppermute(array, "z", ring(4, d)) for d, array in zip((1, 2, 3), sums[1:])]
 
 
-def pack_small(layer, mine_info, count, after=()):
-    return call(
-        functools.partial(pack_small_kernel, count_at=1 + 2 * count),
-        (1,),
-        all_of(*layer.small_grads(), *layer.stats()),
-        plain(*[((2, 8, SMALL, WIDTH), LOW)] * 2),
-        [],
-        mine_info,
-        after=after,
-    )
-
-
-def unpack_small(front, mine):
+def pack_small(layer, count):
+    return (
+        functools.partial(pack_small_kernel, count_at=SEG + 2 * count),
+        [*layer.small_grads(), *layer.stats()],
+        [((2, 8, SMALL, WIDTH), LOW)] * 2,
+    )
+
+
+def unpack_small(front, info):
     block = (4, 4, SMALL, WIDTH), lambda *_: (0, 0, 8, 0)
     gate_taps, merge_taps, gains, gate_full = call(
         unpack_kernel,
@@ -1265,7 +1239,7 @@
             ((32, 3 * WIDTH), F32), ((32, 2 * WIDTH), F32), ((8, WIDTH), F32), ((1, 3 * WIDTH), F32)
         ),
         [],
-        mine.reshape(1),
+        info,
     )
     lines = [gains[g : g + 1] for g in range(5)]
     return gate_taps, merge_taps, lines[0], lines[1], lines[2], gate_full, lines[3], lines[4]
@@ -1277,11 +1251,11 @@
     heads_gain, gated_gain, gate_gain, rear_gain, final_gain,
 ):
     x, k, z, y = (lax.axis_index(name) for name in ("x", "k", "z", "y"))
-    places = [lax.rem(place, 4) for place in (z, z + 3, z + 2, z + 1)]
+    places = [k] + [lax.rem(place, 4) for place in (z, z + 3, z + 2, z + 1)]
     places.append(((x * 2 + k) * 4 + z) * 2 + y)
     spots = jnp.stack([place.astype(jnp.int32) for place in places])
-    mine = k.astype(jnp.int32)
-    layer = Layer(features, cotangent, lengths[0], mine, gate_kernel.shape[0])
+    layer = Layer(features, cotangent, lengths[0], spots, gate_kernel.shape[0])
+    info = layer.info
 
     front, middle, rear = call(
         pack_kernel,
@@ -1298,100 +1272,113 @@
         [pltpu.VMEM((SMALL, WIDTH), F32)],
         spots,
     )
-    front_four = place(place_line_kernel, [front] + line_sends(front), 144, spots)
+    front_four = place(place_line_kernel, [front] + line_sends(front), 144, info)
     front = plane_exchange(front_four)
     middle = tie(middle, front_four)
-    middle_four = place(place_line_kernel, [middle] + line_sends(middle), 208, spots)
+    middle_four = place(place_line_kernel, [middle] + line_sends(middle), 208, info)
     front = tie(front, middle_four)
     middle = plane_exchange(tie(middle_four, front))
     rear = tie(rear, front)
     rear_lines = line_sends(rear)
     front = front, core_swap(front)
-    layer.set_small(unpack_small(front, mine))
+    layer.set_small(unpack_small(front, info))
     mark = layer.front_forward(front)
-    rear_four = place(place_line_kernel, [rear] + rear_lines, 160, spots, after=(mark,))
+    rear_four = place(place_line_kernel, [rear] + rear_lines, 160, info, after=(mark,))
     middle = tie(middle, rear_four)
     rear = plane_exchange(tie(rear_four, middle))
     middle = middle, core_swap(middle)
-    mark = layer.heads_forward(middle)
-    mark = layer.gated_forward(middle, after=(mark,))
+    mark = layer.branches_forward(middle)
     rear = tie(rear, mark)
     rear = rear, core_swap(rear)
-    layer.merge_forward(rear)
-
-    wide = ((32, None), (48, "half"), (48, None), (48, None), (16, None))
-    last = ((48, "right"), (64, None), (16, "small"))
-    send, rear_keep = layer.rear_both()
+
+    send, rear_keep, merge_send, merge_keep = layer.merge_rear(rear)
     rear_got = core_swap(send)
-    merge_send, merge_keep = layer.merge_backward()
-    rear_four = core_sum([(rear_keep, rear_got)], spots, after=(layer.attended_grad,))
-    merge_got = core_swap(merge_send)
+    ((rear_four,),) = run([core_sum([(rear_keep, rear_got)])], info)
+    merge_got = core_swap(tie(merge_send, rear_got))
     rear_plane = plane_exchange(rear_four)
-    send, heads_keep = layer.heads_backward(after=(rear_four,))
-    heads_got = core_swap(send)
-    send, gated_keep = layer.gated_linear(after=(layer.heads_stream,))
-    gated_got = core_swap(send)
-    rear_sums = plane_sum(rear_plane, (128,), spots, after=(layer.gated_total,))
-    wide_four = core_sum(
-        [(merge_keep, merge_got), (gated_keep, gated_got), (heads_keep, heads_got)], spots,
+    send, wide_keep = layer.branches_backward(after=(rear_four,))
+    wide_got = core_swap(tie(send, rear_plane))
+    (rear_sums,) = run([plane_sum(rear_plane, (128,))], info, after=(layer.gated_total,))
+    ((wide_four,),) = run(
+        [core_sum([(merge_keep, merge_got), (wide_keep, wide_got)])], info,
         after=(rear_sums[0],),
     )
     rear_sums = line_swap(rear_sums)
     wide_plane = plane_exchange(tie(wide_four, rear_plane))
-    layer.gated_conv(after=(wide_four,))
-    send, gate_keep = layer.gated_gate()
+    send, gate_keep = layer.gated_gate(after=(wide_four,))
     gate_got = core_swap(send)
-    small_send, small_keep = pack_small(layer, layer.info, lengths.shape[1])
+    ((small_send, small_keep),) = run(
+        [pack_small(layer, lengths.shape[1])], info, after=rear_sums[1]
+    )
     small_got = core_swap(small_send)
-    rear_up_grad, rear_down_grad = line_sum(
-        rear_sums, ((64, None), (64, None)), (rear_up.shape, rear_down.shape), spots,
-        after=(small_send,),
-    )
-    send, down_keep = layer.front_hidden(after=(small_send, rear_up_grad))
-    down_got = core_swap(send)
-    wide_sums = plane_sum(wide_plane, (192,), spots, after=(layer.front_grad,))
-    last_four = core_sum(
-        [(gate_keep, gate_got), (down_keep, down_got), (small_keep, small_got)], spots,
+    send, down_keep = layer.front_hidden(after=(small_send,))
+    down_got = core_swap(tie(send, wide_plane))
+    (wide_sums,) = run([plane_sum(wide_plane, (192,))], info, after=(layer.front_grad,))
+    ((last_four,),) = run(
+        [
+            core_sum([(gate_keep, gate_got), (down_keep, down_got), (small_keep, small_got)]),
+        ],
+        info,
         after=(wide_sums[0],),
     )
     wide_sums = line_swap(wide_sums)
     last_plane = plane_exchange(tie(last_four, wide_plane))
-    send, up_keep = layer.front_input(after=(last_four,))
+    send, up_keep = layer.front_input(after=(last_four, *wide_sums[1]))
     up_got = core_swap(send)
+    ((front_four,),) = run([core_sum([(up_keep, up_got)])], info)
     half_shape = (gated_input.shape[0], gated_input.shape[1] // 2)
-    merge_output_grad, gated_left_grad, gated_output_grad, heads_input_grad, heads_output_grad = (
-        line_sum(
-            wide_sums,
-            ((32, None), (48, None), (48, None), (48, None), (16, None)),
-            (
-                merge_output.shape, half_shape, gated_output.shape, heads_input.shape,
-                heads_output.shape,
+    front_plane = plane_exchange(tie(front_four, last_plane))
+    (last_sums,) = run([plane_sum(last_plane, (48, 64, -SMALL))], info, after=(front_four,))
+    last_sums = line_swap(last_sums)
+    (
+        (rear_up_grad, rear_down_grad),
+        (
+            merge_output_grad, gated_left_grad, gated_output_grad, heads_input_grad,
+            heads_output_grad,
+        ),
+    ) = run(
+        [
+            line_sum(rear_sums, ((64, None), (64, None)), (rear_up.shape, rear_down.shape)),
+            line_sum(
+                wide_sums, ((32, None), (48, None), (48, None), (48, None), (16, None)),
+                (
+                    merge_output.shape, half_shape, gated_output.shape, heads_input.shape,
+                    heads_output.shape,
+                ),
             ),
-            spots,
-            after=(layer.features_grad,),
-        )
-    )
-    front_four = core_sum([(up_keep, up_got)], spots, after=(merge_output_grad,))
-    last_sums = plane_sum(last_plane, (48, 64, -SMALL), spots, after=(front_four,))
-    last_sums = line_swap(last_sums)
-    front_plane = plane_exchange(tie(front_four, last_plane))
+        ],
+        info,
+        after=(last_sums[0],),
+    )
+    (front_sums,) = run(
+        [plane_sum(front_plane, (80,))], info, after=(last_sums[0], merge_output_grad)
+    )
+    front_sums = line_swap(front_sums)
     vector = (1, front_gain.shape[0])
     (
-        gated_input_grad, front_down_grad, gate_kernel_grad, merge_kernel_grad, heads_gain_grad,
-        gated_gain_grad, rear_gain_grad, final_gain_grad, gate_gain_grad, statistics,
-    ) = line_sum(
-        last_sums,
-        ((0, "left"), (48, "right"), (64, None), (16, "small")),
         (
-            gated_input.shape, front_down.shape, gate_kernel.shape, merge_kernel.shape,
-            vector, vector, vector, vector, (1, gate_gain.shape[0]), (1, STATS - 1),
+            gated_input_grad, front_down_grad, gate_kernel_grad, merge_kernel_grad,
+            heads_gain_grad, gated_gain_grad, rear_gain_grad, final_gain_grad, gate_gain_grad,
+            statistics,
         ),
-        spots,
-        given=(gated_left_grad,),
-    )
-    front_sums = plane_sum(front_plane, (80,), spots, after=(statistics,))
-    front_up_grad, front_gain_grad = line_sum(
-        line_swap(front_sums), ((64, None), (16, "gain")), (front_up.shape, vector), spots
+    ) = run(
+        [
+            line_sum(
+                last_sums,
+                ((0, "left"), (48, "right"), (64, None), (16, "small")),
+                (
+                    gated_input.shape, front_down.shape, gate_kernel.shape, merge_kernel.shape,
+                    vector, vector, vector, vector, (1, gate_gain.shape[0]), (1, STATS - 1),
+                ),
+                given=(gated_left_grad,),
+            ),
+        ],
+        info,
+        after=(front_sums[0],),
+    )
+    ((front_up_grad, front_gain_grad),) = run(
+        [line_sum(front_sums, ((64, None), (16, "gain")), (front_up.shape, vector))], info,
+        after=(statistics,),
     )
     return (
         layer.encoded, layer.features_grad, front_up_grad, front_down_grad, heads_input_grad,
@@ -1462,18 +1449,13 @@
 
     front = chunk(up, down)
     rear = chunk(r_up, r_down, m_out)
-    layer = Layer(features, cotangent, lengths[0], jnp.int32(0), smaller[0].shape[0])
+    layer = Layer(features, cotangent, lengths[0], jnp.zeros((SEG,), jnp.int32), smaller[0].shape[0])
     layer.set_small(lines)
     layer.front_forward(front)
-    middle = chunk(g_in, g_out, h_in, h_out)
-    layer.heads_forward(middle)
-    layer.gated_forward(middle)
-    layer.merge_forward(rear)
-    rear = layer.rear_both()
-    merge = layer.merge_backward()
-    left = layer.gated_linear()
-    heads = layer.heads_backward()
-    layer.gated_conv()
+    layer.branches_forward(chunk(g_in, g_out, h_in, h_out))
+    rear = layer.merge_rear(rear)
+    rear, merge = rear[:2], rear[2:]
+    wide = layer.branches_backward()
     right = layer.gated_gate()
     front_down_halves = layer.front_hidden()
     front_up_halves = layer.front_input()
@@ -1482,11 +1464,12 @@
         return tuple(array[:, :, start:stop] for array in pair)
 
     gated_halves = tuple(
-        jnp.concatenate([one[:, :, :48], two], axis=2) for one, two in zip(left, right)
+        jnp.concatenate([one[:, :, :48], two], axis=2) for one, two in zip(wide, right)
     )
     ordered = (
-        part(front_up_halves, 0, 64), front_down_halves, part(heads, 0, 48), part(heads, 48, 64),
-        gated_halves, part(left, 48, 96), merge, part(rear, 0, 64), part(rear, 64, 128),
+        part(front_up_halves, 0, 64), front_down_halves, part(wide, 96, 144),
+        part(wide, 144, 160), gated_halves, part(wide, 48, 96), merge,
+        part(rear, 0, 64), part(rear, 64, 128),
     )
     front_gain = front_up_halves[1][0, 0, 64].astype(F32)
     small_grads = layer.small_grads()
@@ -1518,11 +1501,11 @@
     for element in smaller:
         outputs.append(flat[start : start + element.size].reshape(element.shape))
         start += element.size
-    front_stat, merge_stat, rear_stat = layer.stats()
+    front_stat, rear_stat = layer.stats()
     squares = jnp.stack(
         [
-            front_stat[0], front_stat[1], merge_stat[0], rear_stat[0], front_stat[2],
-            merge_stat[1], rear_stat[1],
+            front_stat[0], front_stat[1], rear_stat[0], rear_stat[2], front_stat[2], rear_stat[1],
+            rear_stat[3],
         ]
     )
     totals = lax.psum(

time: 393 us -> 368 us (0.936)
  Pallas kernels: 221 us -> 203 us
  starting transfers between devices: 66.8 us -> 62.2 us
    ppermute x12, waiting for transfers between devices: 25.7 us -> 3.99 us  [line_swap(): lax.ppermute(array, 'z', ring(4, d))]
    pallas_call x27 -> x21, Pallas kernels: 211 us -> 193 us  [call(): pl.pallas_call(body, grid_spec=pltpu.PrefetchScalarGridSpec(num_scalar_pr...]
    all_to_all x7, waiting for transfers between devices: 18.8 us -> 31.7 us  [plane_exchange(): return lax.all_to_all(array, ('x', 'y'), 0, 0, tiled=True)]
    ppermute x11 -> x10, waiting for transfers between devices: 5.87 us -> 13.9 us  [core_swap(): return lax.ppermute(array, 'k', ring(2, 1))]
    unnamed x72 -> x68, local copies, waits for them, and re-layouts: 16.3 us -> 16.8 us
  transfers between devices with their start and end apart: 39 -> 38, of which waited for: 16 -> 18; matrix products, arithmetic and copies ran while one was open for 1% -> 1% of each run, Pallas kernels for 43% -> 40%
where the time goes in v3:
time: 368 us; the launch traced here: 367 us
  Pallas kernels  203 us (55%)
  waiting for transfers between devices  77.5 us (21%)
  starting transfers between devices  62.2 us (17%)
  local copies, waits for them, and re-layouts  20.9 us (6%)
    pallas_call x21, Pallas kernels, call(): pl.pallas_call(body, grid_spec=pltpu.PrefetchScalarGridSpec(num_scalar_pr...  193 us
    all_to_all x7, waiting for transfers between devices, plane_exchange(): return lax.all_to_all(array, ('x', 'y'), 0, 0, tiled=True)  31.7 us
    all_to_all x7, starting transfers between devices, plane_exchange(): return lax.all_to_all(array, ('x', 'y'), 0, 0, tiled=True)  28.4 us
    ppermute x9, waiting for transfers between devices, line_sends(): return [lax.ppermute(array, 'z', ring(4, d)) for d in (1, 2, 3)]  27.9 us
    ppermute x12, starting transfers between devices, line_swap(): lax.ppermute(array, 'z', ring(4, d))  18.1 us
    unnamed x68, local copies, waits for them, and re-layouts  16.8 us
    ppermute x9, starting transfers between devices, line_sends(): return [lax.ppermute(array, 'z', ring(4, d)) for d in (1, 2, 3)]  14.3 us
    ppermute x10, waiting for transfers between devices, core_swap(): return lax.ppermute(array, 'k', ring(2, 1))  13.9 us
  transfers between devices with their start and end apart: 38, of which 18 were waited for; matrix products, arithmetic and copies ran while one was open for 1% of the time, Pallas kernels for 40%

profile of v3, /device:TPU:0, one launch (start us, length us, event | category | flops | bytes accessed | tf_op | source)
XLA Modules:
  0.0 366.7 jit_solution(18184937746689547068)
XLA Ops:
  3.9 5.0 %collective-permute-start.2 = (bf16[144,512]{1,0:T(8,128)(2,1)}, bf16[144,512]{1,0:T(8,128)(2,1)S(1)}, u32[]{:S(2)}, u32[]{:S(2)}) collective-permute-start(bf16[144,512]{1,0:T(8,128)(2,1)} %get-tuple-element.120.refs_0_), channel_id=1, source_target_pairs={{0,6},{2,0},{4,2},{6,4},{1,7},{3,1},{5,3},{7,5},{8,14},{10,8},{12,... | collective-permute-start | bytes 442376 | tf_op jit(solution)/shard_map/ppermute | solution.py:965
  13.5 8.1 %collective-permute-done.1.refs_2_ = bf16[144,512]{1,0:T(8,128)(2,1)S(1)} collective-permute-done((bf16[144,512]{1,0:T(8,128)(2,1)}, bf16[144,512]{1,0:T(8,128)(2,1)S(1)}, u32[]{:S(2)}, u32[]{:S(2)}) %collective-permute-start.1) | collective-permute-done | bytes 147488 | tf_op jit(solution)/shard_map/ppermute | solution.py:965
  26.3 4.6 %all-to-all-start = ((bf16[4,4,144,512]{3,2,1,0:T(8,128)(2,1)}), bf16[4,4,144,512]{3,2,1,0:T(8,128)(2,1)}, u32[]{:S(2)}, u32[]{:S(2)}) async-start(bf16[4,4,144,512]{3,2,1,0:T(8,128)(2,1)} %place_line_kernel.3), calls=%async_computation | async-start | bytes 4718592 | tf_op jit(solution)/shard_map/all_to_all | solution.py:969
  38.3 13.2 %collective-permute-done.4.refs_2_ = bf16[208,512]{1,0:T(8,128)(2,1)S(1)} collective-permute-done((bf16[208,512]{1,0:T(8,128)(2,1)S(1)}, bf16[208,512]{1,0:T(8,128)(2,1)S(1)}, u32[]{:S(2)}, u32[]{:S(2)}) %collective-permute-start.4) | collective-permute-done | bytes 213024 | tf_op jit(solution)/shard_map/ppermute | solution.py:965
  52.9 3.9 %place_line_kernel.4 = bf16[4,4,208,512]{3,2,1,0:T(8,128)(2,1)} custom-call(s32[16]{0:T(128)} %concatenate.4.info.info_ref, bf16[208,512]{1,0:T(8,128)(2,1)} %get-tuple-element.122.refs_0_, bf16[208,512]{1,0:T(8,128)(2,1)} %copy-done.22, bf16[208,512]{1,0:T(8,128)(2,1)} %copy-done.21, bf16[208,512]{1,0:T(8,128)(2,1)} %copy-done.20), custom_call_target="tpu_custom_call" | custom-call | bytes 6815744 | tf_op jit(solution)/shard_map/place_line_kernel/pallas_call | solution.py:947
  71.4 8.0 %front_forward_kernel.1 = (f32[384,512]{1,0:T(8,128)}, f32[384,2048]{1,0:T(8,128)}, f32[8,512]{1,0:T(8,128)}) custom-call(s32[16]{0:T(128)} %concatenate.4.info.info_ref, bf16[384,512]{1,0:T(8,128)(2,1)} %refs_6_.3, f32[1,512]{1,0:T(1,128)} %get-tuple-element.224.refs_1_.refs_7_, f32[384,1]{1,0:T(8,128)} %compare_convert_fusion.refs_2_.refs_8_, ...), custom_call_target="tpu_custom_call" | custom-call | flops 1610612736 | bytes 13782528 | tf_op jit(solution)/shard_map/front_forward_kernel/pallas_call | solution.py:610
  84.3 17.7 %all-to-all-done.1.refs_4_.refs_6_.refs_11_.refs_13_.refs_8_.refs_10_.refs_17_.refs_19_ = bf16[4,4,208,512]{3,2,1,0:T(8,128)(2,1)S(1)} async-done(((bf16[4,4,208,512]{3,2,1,0:T(8,128)(2,1)}), bf16[4,4,208,512]{3,2,1,0:T(8,128)(2,1)S(1)}, u32[]{:S(2)}, u32[]{:S(2)}) %all-to-all-start.1) | async-done | bytes 3407904 | tf_op jit(solution)/shard_map/all_to_all | solution.py:969
  103.9 4.8 %all-to-all-start.2 = ((bf16[4,4,160,512]{3,2,1,0:T(8,128)(2,1)}), bf16[4,4,160,512]{3,2,1,0:T(8,128)(2,1)}, u32[]{:S(2)}, u32[]{:S(2)}) async-start(bf16[4,4,160,512]{3,2,1,0:T(8,128)(2,1)} %place_line_kernel.5), calls=%async_computation.2 | async-start | bytes 5242880 | tf_op jit(solution)/shard_map/all_to_all | solution.py:969
  110.1 27.7 %branches_forward_kernel.1 = (f32[384,512]{1,0:T(8,128)}, bf16[384,1536]{1,0:T(8,128)(2,1)}, bf16[384,512]{1,0:T(8,128)(2,1)}, f32[384,512]{1,0:T(8,128)}, f32[3...) custom-call(s32[16]{0:T(128)} %concatenate.4.info.info_ref, ...), custom_call_target="tpu_custom_call" | custom-call | flops 10468982784 | bytes 30541312 | tf_op jit(solution)/shard_map/branches_forward_kernel/pallas_call | solution.py:610
  139.4 5.1 %collective-permute-done.11.refs_5_.refs_11_.refs_13_ = bf16[4,4,160,512]{3,2,1,0:T(8,128)(2,1)S(1)} collective-permute-done((bf16[4,4,160,512]{3,2,1,0:T(8,128)(2,1)}, bf16[4,4,160,512]{3,2,1,0:T(8,128)(2,1)S(1)}, u32[]{:S(2)}, u32[]{:S(2)}) %collective-permute-start.11) | collective-permute-done | bytes 2621472 | tf_op jit(solution)/shard_map/ppermute | solution.py:973
  146.0 38.9 %merge_rear_kernel.1 = (bf16[384,512]{1,0:T(8,128)(2,1)}, f32[384,512]{1,0:T(8,128)}, f32[1,512]{1,0:T(1,128)}, f32[1,512]{1,0:T(1,128)}, f32[8,512]{1,0:T(8,128...) custom-call(s32[16]{0:T(128)} %concatenate.4.info.info_ref, ...), custom_call_target="tpu_custom_call" | custom-call | flops 16106127360 | bytes 24924160 | tf_op jit(solution)/shard_map/merge_rear_kernel/pallas_call | solution.py:610
  185.1 4.2 %collective-permute-done.12.refs_1_ = bf16[2,8,128,512]{3,2,1,0:T(8,128)(2,1)S(1)} collective-permute-done((bf16[2,8,128,512]{3,2,1,0:T(8,128)(2,1)}, bf16[2,8,128,512]{3,2,1,0:T(8,128)(2,1)S(1)}, u32[]{:S(2)}, u32[]{:S(2)}) %collective-permute-start.12) | collective-permute-done | bytes 2097184 | tf_op jit(solution)/shard_map/ppermute | solution.py:973
  190.6 4.5 %tasks_kernel.12.refs_0_ = bf16[4,4,128,512]{3,2,1,0:T(8,128)(2,1)} custom-call(s32[16]{0:T(128)} %concatenate.4.info.info_ref, bf16[2,8,128,512]{3,2,1,0:T(8,128)(2,1)} %get-tuple-element.140.refs_0_, bf16[2,8,128,512]{3,2,1,0:T(8,128)(2,1)} %copy-done.6), custom_call_target="tpu_custom_call" | custom-call | bytes 6291456 | tf_op jit(solution)/shard_map/tasks_kernel/pallas_call | solution.py:610
  195.1 3.8 %all-to-all-start.3 = ((bf16[4,4,128,512]{3,2,1,0:T(8,128)(2,1)}), bf16[4,4,128,512]{3,2,1,0:T(8,128)(2,1)S(1)}, u32[]{:S(2)}, u32[]{:S(2)}) async-start(bf16[4,4,128,512]{3,2,1,0:T(8,128)(2,1)} %tasks_kernel.12.refs_0_), calls=%async_computation.3 | async-start | bytes 4194304 | tf_op jit(solution)/shard_map/all_to_all | solution.py:969
  198.9 23.9 %branches_backward_kernel.1 = (f32[384,512]{1,0:T(8,128)}, f32[1,512]{1,0:T(1,128)}, f32[384,1536]{1,0:T(8,128)}, f32[384,512]{1,0:T(8,128)}, bf16[2,8,160,512]{...) custom-call(s32[16]{0:T(128)} %concatenate.4.info.info_ref, bf16[4,4,128,512]{3,2,1,0:T(8,128)(2,1)} %tasks_kernel.12.refs_0_, ...), custom_call_target="tpu_custom_call" | custom-call | flops 8053063680 | bytes 25954304 | tf_op jit(solution)/shard_map/branches_backward_kernel/pallas_call | solution.py:610
  231.6 5.5 %tasks_kernel.14.refs_0_ = bf16[4,4,192,512]{3,2,1,0:T(8,128)(2,1)} custom-call(s32[16]{0:T(128)} %concatenate.4.info.info_ref, f32[128,512]{1,0:T(8,128)} %get-tuple-element.153.refs_0_.refs_1_, bf16[2,8,32,512]{3,2,1,0:T(8,128)(2,1)} %get-tuple-element.154.refs_1_, bf16[2,8,160,512]{3,2,1,0:T(8,128)(2,1)} %get-tuple-element.155.refs_2_, ...), custom_call_target="tpu_custom_call" | custom-call | bytes 9437184 | tf_op jit(solution)/shard_map/tasks_kernel/pallas_call | solution.py:610
  245.8 27.8 %gated_gate_kernel.1 = (f32[384,512]{1,0:T(8,128)}, f32[1,512]{1,0:T(1,128)}, f32[1,1536]{1,0:T(1,128)}, f32[32,1536]{1,0:T(8,128)}, bf16[2,8,48,512]{3,2,1,0:T(8,128)(2,1)}, /*index=5*/bf16[2,8,48,512]{3,2,1,0:T(8,128)(2,1)}) custom-call(s32[16]{0:T(128)} %concatenate.4.info.info_ref, bf16[4,4,192,512]{3,2,1,0:T(8,128)(2,1)} %tasks_kernel.14.refs_0_, ...), custom_call_target="tpu_custom_call" | custom-call | flops 9663676416 | bytes 19341312 | tf_op jit(solution)/shard_map/gated_gate_kernel/pallas_call | solution.py:610
  274.3 3.9 %tasks_kernel.15 = (bf16[2,8,16,512]{3,2,1,0:T(8,128)(2,1)}, bf16[2,8,16,512]{3,2,1,0:T(8,128)(2,1)}) custom-call(s32[16]{0:T(128)} %concatenate.4.info.info_ref, bf16[128,512]{1,0:T(8,128)(2,1)} %copy-done.14, bf16[128,512]{1,0:T(8,128)(2,1)} %copy-done.15, bf16[128,512]{1,0:T(8,128)(2,1)} %copy-done.16, f32[32,1536]{1,0:T(8,128)} %get-tuple-element.162.refs_3_, ...), custom_call_target="tpu_custom_call" | custom-call | bytes 899072 | tf_op jit(solution)/shard_map/tasks_kernel/pallas_call | solution.py:610
  278.2 9.0 %front_hidden_kernel.1 = (f32[384,512]{1,0:T(8,128)}, bf16[384,2048]{1,0:T(8,128)(2,1)}, bf16[2,8,64,512]{3,2,1,0:T(8,128)(2,1)}, bf16[2,8,64,512]{3,2,1,0:T(8,128)(2,1)}) custom-call(s32[16]{0:T(128)} %concatenate.4.info.info_ref, bf16[2,8,16,512]{3,2,1,0:T(8,128)(2,1)} %get-tuple-element.170.refs_0_, f32[384,512]{1,0:T(8,128)} %get-tuple-element.171.refs_1_, ...), custom_call_target="tpu_custom_call" | custom-call | flops 2415919104 | bytes 14680064 | tf_op jit(solution)/shard_map/front_hidden_kernel/pallas_call | solution.py:610
  288.9 3.7 %tasks_kernel.16 = (f32[192,512]{1,0:T(8,128)}, bf16[192,512]{1,0:T(8,128)(2,1)}, bf16[192,512]{1,0:T(8,128)(2,1)}, bf16[192,512]{1,0:T(8,128)(2,1)}) custom-call(s32[16]{0:T(128)} %concatenate.4.info.info_ref, f32[384,512]{1,0:T(8,128)} %get-tuple-element.175.refs_0_.refs_4_, bf16[4,4,192,512]{3,2,1,0:T(8,128)(2,1)} %copy-done.1), custom_call_target="tpu_custom_call" | custom-call | bytes 4128768 | tf_op jit(solution)/shard_map/tasks_kernel/pallas_call | solution.py:610
  297.8 4.7 %tasks_kernel.17.refs_0_ = bf16[4,4,128,512]{3,2,1,0:T(8,128)(2,1)} custom-call(s32[16]{0:T(128)} %concatenate.4.info.info_ref, f32[192,512]{1,0:T(8,128)} %get-tuple-element.177.refs_0_.refs_5_, bf16[2,8,48,512]{3,2,1,0:T(8,128)(2,1)} %get-tuple-element.178.refs_1_, bf16[2,8,64,512]{3,2,1,0:T(8,128)(2,1)} %get-tuple-element.179.refs_2_, ...), custom_call_target="tpu_custom_call" | custom-call | bytes 6291456 | tf_op jit(solution)/shard_map/tasks_kernel/pallas_call | solution.py:610
  302.5 4.1 %all-to-all-start.5 = ((bf16[4,4,128,512]{3,2,1,0:T(8,128)(2,1)}), bf16[4,4,128,512]{3,2,1,0:T(8,128)(2,1)S(1)}, u32[]{:S(2)}, u32[]{:S(2)}) async-start(bf16[4,4,128,512]{3,2,1,0:T(8,128)(2,1)} %tasks_kernel.17.refs_0_), calls=%async_computation.5 | async-start | bytes 4194304 | tf_op jit(solution)/shard_map/all_to_all | solution.py:969
  310.3 8.8 %front_input_kernel.1 = (bf16[384,512]{1,0:T(8,128)(2,1)}, bf16[2,8,80,512]{3,2,1,0:T(8,128)(2,1)}, bf16[2,8,80,512]{3,2,1,0:T(8,128)(2,1)}) custom-call(s32[16]{0:T(128)} %concatenate.4.info.info_ref, bf16[4,4,128,512]{3,2,1,0:T(8,128)(2,1)} %tasks_kernel.17.refs_0_, bf16[192,512]{1,0:T(8,128)(2,1)} %copy-done.10, bf16[192,512]{1,0:T(8,128)(2,1)} %copy-done.11, ...), custom_call_target="tpu_custom_call" | custom-call | flops 2415919104 | bytes 10487808 | tf_op jit(solution)/shard_map/front_input_kernel/pallas_call | solution.py:610
  344.9 5.8 %all-to-all-done.6.refs_2_ = bf16[4,4,80,512]{3,2,1,0:T(8,128)(2,1)S(1)} async-done(((bf16[4,4,80,512]{3,2,1,0:T(8,128)(2,1)}), bf16[4,4,80,512]{3,2,1,0:T(8,128)(2,1)S(1)}, u32[]{:S(2)}, u32[]{:S(2)}) %all-to-all-start.6) | async-done | bytes 1310752 | tf_op jit(solution)/shard_map/all_to_all | solution.py:969
  (152 shorter events, 118.8 us)
Async XLA Ops:
  3.9 9.7 %collective-permute-start.2 = (bf16[144,512]{1,0:T(8,128)(2,1)}, bf16[144,512]{1,0:T(8,128)(2,1)S(1)}, u32[]{:S(2)}, u32[]{:S(2)}) collective-permute-start(bf16[144,512]{1,0:T(8,128)(2,1)} %get-tuple-element.120.refs_0_), channel_id=1, source_target_pairs={{0,6},{2,0},{4,2},{6,4},{1,7},{3,1},{5,3},{7,5},{8,14},{10,8},{12,... | collective-permute-start | bytes 442376 | tf_op jit(solution)/shard_map/ppermute | solution.py:965
  8.9 12.7 %collective-permute-start.1 = (bf16[144,512]{1,0:T(8,128)(2,1)}, bf16[144,512]{1,0:T(8,128)(2,1)S(1)}, u32[]{:S(2)}, u32[]{:S(2)}) collective-permute-start(bf16[144,512]{1,0:T(8,128)(2,1)} %get-tuple-element.120.refs_0_), channel_id=1, source_target_pairs={{0,4},{2,6},{4,0},{6,2},{1,5},{3,7},{5,1},{7,3},{8,12},{10,14},{12... | collective-permute-start | bytes 442376 | tf_op jit(solution)/shard_map/ppermute | solution.py:965
  8.9 12.7 %collective-permute-start = (bf16[144,512]{1,0:T(8,128)(2,1)}, bf16[144,512]{1,0:T(8,128)(2,1)S(1)}, u32[]{:S(2)}, u32[]{:S(2)}) collective-permute-start(bf16[144,512]{1,0:T(8,128)(2,1)} %get-tuple-element.120.refs_0_), channel_id=1, source_target_pairs={{0,2},{2,4},{4,6},{6,0},{1,3},{3,5},{5,7},{7,1},{8,10},{10,12},{12... | collective-permute-start | bytes 442376 | tf_op jit(solution)/shard_map/ppermute | solution.py:965
  26.3 32.2 %all-to-all-start = ((bf16[4,4,144,512]{3,2,1,0:T(8,128)(2,1)}), bf16[4,4,144,512]{3,2,1,0:T(8,128)(2,1)}, u32[]{:S(2)}, u32[]{:S(2)}) async-start(bf16[4,4,144,512]{3,2,1,0:T(8,128)(2,1)} %place_line_kernel.3), calls=%async_computation | async-start | bytes 4718592 | tf_op jit(solution)/shard_map/all_to_all | solution.py:969
  32.4 19.1 %collective-permute-start.4 = (bf16[208,512]{1,0:T(8,128)(2,1)S(1)}, bf16[208,512]{1,0:T(8,128)(2,1)S(1)}, u32[]{:S(2)}, u32[]{:S(2)}) collective-permute-start(bf16[208,512]{1,0:T(8,128)(2,1)S(1)} %copy-done.19), channel_id=1, source_target_pairs={{0,4},{2,6},{4,0},{6,2},{1,5},{3,7},{5,1},{7,3},{8,12},{10,14},{12... | collective-permute-start | bytes 638984 | tf_op jit(solution)/shard_map/ppermute | solution.py:965
  33.2 18.3 %collective-permute-start.3 = (bf16[208,512]{1,0:T(8,128)(2,1)S(1)}, bf16[208,512]{1,0:T(8,128)(2,1)S(1)}, u32[]{:S(2)}, u32[]{:S(2)}) collective-permute-start(bf16[208,512]{1,0:T(8,128)(2,1)S(1)} %copy-done.19), channel_id=1, source_target_pairs={{0,2},{2,4},{4,6},{6,0},{1,3},{3,5},{5,7},{7,1},{8,10},{10,12},{12... | collective-permute-start | bytes 638984 | tf_op jit(solution)/shard_map/ppermute | solution.py:965
  58.5 43.6 %all-to-all-start.1 = ((bf16[4,4,208,512]{3,2,1,0:T(8,128)(2,1)}), bf16[4,4,208,512]{3,2,1,0:T(8,128)(2,1)S(1)}, u32[]{:S(2)}, u32[]{:S(2)}) async-start(bf16[4,4,208,512]{3,2,1,0:T(8,128)(2,1)} %place_line_kernel.4), calls=%async_computation.1 | async-start | bytes 6815744 | tf_op jit(solution)/shard_map/all_to_all | solution.py:969
  63.2 16.3 %collective-permute-start.9 = (bf16[160,512]{1,0:T(8,128)(2,1)}, bf16[160,512]{1,0:T(8,128)(2,1)}, u32[]{:S(2)}, u32[]{:S(2)}) collective-permute-start(bf16[160,512]{1,0:T(8,128)(2,1)} %get-tuple-element.129.refs_1_), channel_id=1, source_target_pairs={{0,6},{2,0},{4,2},{6,4},{1,7},{3,1},{5,3},{7,5},{8,14},{10,8},{12,... | collective-permute-start | bytes 491528 | tf_op jit(solution)/shard_map/ppermute | solution.py:965
  63.5 17.3 %collective-permute-start.8 = (bf16[160,512]{1,0:T(8,128)(2,1)}, bf16[160,512]{1,0:T(8,128)(2,1)}, u32[]{:S(2)}, u32[]{:S(2)}) collective-permute-start(bf16[160,512]{1,0:T(8,128)(2,1)} %get-tuple-element.129.refs_1_), channel_id=1, source_target_pairs={{0,4},{2,6},{4,0},{6,2},{1,5},{3,7},{5,1},{7,3},{8,12},{10,14},{12... | collective-permute-start | bytes 491528 | tf_op jit(solution)/shard_map/ppermute | solution.py:965
  65.2 15.7 %collective-permute-start.7 = (bf16[160,512]{1,0:T(8,128)(2,1)}, bf16[160,512]{1,0:T(8,128)(2,1)}, u32[]{:S(2)}, u32[]{:S(2)}) collective-permute-start(bf16[160,512]{1,0:T(8,128)(2,1)} %get-tuple-element.129.refs_1_), channel_id=1, source_target_pairs={{0,2},{2,4},{4,6},{6,0},{1,3},{3,5},{5,7},{7,1},{8,10},{10,12},{12... | collective-permute-start | bytes 491528 | tf_op jit(solution)/shard_map/ppermute | solution.py:965
  103.9 35.5 %all-to-all-start.2 = ((bf16[4,4,160,512]{3,2,1,0:T(8,128)(2,1)}), bf16[4,4,160,512]{3,2,1,0:T(8,128)(2,1)}, u32[]{:S(2)}, u32[]{:S(2)}) async-start(bf16[4,4,160,512]{3,2,1,0:T(8,128)(2,1)} %place_line_kernel.5), calls=%async_computation.2 | async-start | bytes 5242880 | tf_op jit(solution)/shard_map/all_to_all | solution.py:969
  195.1 29.1 %all-to-all-start.3 = ((bf16[4,4,128,512]{3,2,1,0:T(8,128)(2,1)}), bf16[4,4,128,512]{3,2,1,0:T(8,128)(2,1)S(1)}, u32[]{:S(2)}, u32[]{:S(2)}) async-start(bf16[4,4,128,512]{3,2,1,0:T(8,128)(2,1)} %tasks_kernel.12.refs_0_), calls=%async_computation.3 | async-start | bytes 4194304 | tf_op jit(solution)/shard_map/all_to_all | solution.py:969
  237.1 50.1 %all-to-all-start.4 = ((bf16[4,4,192,512]{3,2,1,0:T(8,128)(2,1)}), bf16[4,4,192,512]{3,2,1,0:T(8,128)(2,1)S(1)}, u32[]{:S(2)}, u32[]{:S(2)}) async-start(bf16[4,4,192,512]{3,2,1,0:T(8,128)(2,1)} %tasks_kernel.14.refs_0_), calls=%async_computation.4 | async-start | bytes 6291456 | tf_op jit(solution)/shard_map/all_to_all | solution.py:969
  240.8 32.8 %collective-permute-start.13 = (bf16[128,512]{1,0:T(8,128)(2,1)}, bf16[128,512]{1,0:T(8,128)(2,1)S(1)}, u32[]{:S(2)}, u32[]{:S(2)}) collective-permute-start(bf16[128,512]{1,0:T(8,128)(2,1)} %get-tuple-element.150), channel_id=1, source_target_pairs={{0,2},{2,4},{4,6},{6,0},{1,3},{3,5},{5,7},{7,1},{8,10},{10,12},{12... | collective-permute-start | bytes 393224 | tf_op jit(solution)/shard_map/ppermute | solution.py:1221
  241.0 32.6 %collective-permute-start.14 = (bf16[128,512]{1,0:T(8,128)(2,1)}, bf16[128,512]{1,0:T(8,128)(2,1)S(1)}, u32[]{:S(2)}, u32[]{:S(2)}) collective-permute-start(bf16[128,512]{1,0:T(8,128)(2,1)} %get-tuple-element.151), channel_id=1, source_target_pairs={{0,4},{2,6},{4,0},{6,2},{1,5},{3,7},{5,1},{7,3},{8,12},{10,14},{12... | collective-permute-start | bytes 393224 | tf_op jit(solution)/shard_map/ppermute | solution.py:1221
  242.9 30.7 %collective-permute-start.15 = (bf16[128,512]{1,0:T(8,128)(2,1)}, bf16[128,512]{1,0:T(8,128)(2,1)S(1)}, u32[]{:S(2)}, u32[]{:S(2)}) collective-permute-start(bf16[128,512]{1,0:T(8,128)(2,1)} %get-tuple-element.152), channel_id=1, source_target_pairs={{0,6},{2,0},{4,2},{6,4},{1,7},{3,1},{5,3},{7,5},{8,14},{10,8},{12,... | collective-permute-start | bytes 393224 | tf_op jit(solution)/shard_map/ppermute | solution.py:1221
  292.7 14.0 %collective-permute-start.21 = (bf16[192,512]{1,0:T(8,128)(2,1)}, bf16[192,512]{1,0:T(8,128)(2,1)S(1)}, u32[]{:S(2)}, u32[]{:S(2)}) collective-permute-start(bf16[192,512]{1,0:T(8,128)(2,1)} %get-tuple-element.184), channel_id=1, source_target_pairs={{0,2},{2,4},{4,6},{6,0},{1,3},{3,5},{5,7},{7,1},{8,10},{10,12},{12... | collective-permute-start | bytes 589832 | tf_op jit(solution)/shard_map/ppermute | solution.py:1221
  292.7 16.8 %collective-permute-start.22 = (bf16[192,512]{1,0:T(8,128)(2,1)}, bf16[192,512]{1,0:T(8,128)(2,1)S(1)}, u32[]{:S(2)}, u32[]{:S(2)}) collective-permute-start(bf16[192,512]{1,0:T(8,128)(2,1)} %get-tuple-element.185), channel_id=1, source_target_pairs={{0,4},{2,6},{4,0},{6,2},{1,5},{3,7},{5,1},{7,3},{8,12},{10,14},{12... | collective-permute-start | bytes 589832 | tf_op jit(solution)/shard_map/ppermute | solution.py:1221
  293.6 15.9 %collective-permute-start.23 = (bf16[192,512]{1,0:T(8,128)(2,1)}, bf16[192,512]{1,0:T(8,128)(2,1)S(1)}, u32[]{:S(2)}, u32[]{:S(2)}) collective-permute-start(bf16[192,512]{1,0:T(8,128)(2,1)} %get-tuple-element.186), channel_id=1, source_target_pairs={{0,6},{2,0},{4,2},{6,4},{1,7},{3,1},{5,3},{7,5},{8,14},{10,8},{12,... | collective-permute-start | bytes 589832 | tf_op jit(solution)/shard_map/ppermute | solution.py:1221
  302.5 28.0 %all-to-all-start.5 = ((bf16[4,4,128,512]{3,2,1,0:T(8,128)(2,1)}), bf16[4,4,128,512]{3,2,1,0:T(8,128)(2,1)S(1)}, u32[]{:S(2)}, u32[]{:S(2)}) async-start(bf16[4,4,128,512]{3,2,1,0:T(8,128)(2,1)} %tasks_kernel.17.refs_0_), calls=%async_computation.5 | async-start | bytes 4194304 | tf_op jit(solution)/shard_map/all_to_all | solution.py:969
  330.5 20.1 %all-to-all-start.6 = ((bf16[4,4,80,512]{3,2,1,0:T(8,128)(2,1)}), bf16[4,4,80,512]{3,2,1,0:T(8,128)(2,1)S(1)}, u32[]{:S(2)}, u32[]{:S(2)}) async-start(bf16[4,4,80,512]{3,2,1,0:T(8,128)(2,1)} %tasks_kernel.18.refs_0_), calls=%async_computation.6 | async-start | bytes 2621440 | tf_op jit(solution)/shard_map/all_to_all | solution.py:969
  337.3 19.0 %collective-permute-start.25 = (bf16[128,512]{1,0:T(8,128)(2,1)}, bf16[128,512]{1,0:T(8,128)(2,1)S(1)}, u32[]{:S(2)}, u32[]{:S(2)}) collective-permute-start(bf16[128,512]{1,0:T(8,128)(2,1)} %get-tuple-element.196), channel_id=1, source_target_pairs={{0,2},{2,4},{4,6},{6,0},{1,3},{3,5},{5,7},{7,1},{8,10},{10,12},{12... | collective-permute-start | bytes 393224 | tf_op jit(solution)/shard_map/ppermute | solution.py:1221
  338.0 21.2 %collective-permute-start.26 = (bf16[128,512]{1,0:T(8,128)(2,1)}, bf16[128,512]{1,0:T(8,128)(2,1)S(1)}, u32[]{:S(2)}, u32[]{:S(2)}) collective-permute-start(bf16[128,512]{1,0:T(8,128)(2,1)} %get-tuple-element.197), channel_id=1, source_target_pairs={{0,4},{2,6},{4,0},{6,2},{1,5},{3,7},{5,1},{7,3},{8,12},{10,14},{12... | collective-permute-start | bytes 393224 | tf_op jit(solution)/shard_map/ppermute | solution.py:1221
  339.0 20.1 %collective-permute-start.27 = (bf16[128,512]{1,0:T(8,128)(2,1)}, bf16[128,512]{1,0:T(8,128)(2,1)S(1)}, u32[]{:S(2)}, u32[]{:S(2)}) collective-permute-start(bf16[128,512]{1,0:T(8,128)(2,1)} %get-tuple-element.198), channel_id=1, source_target_pairs={{0,6},{2,0},{4,2},{6,4},{1,7},{3,1},{5,3},{7,5},{8,14},{10,8},{12,... | collective-permute-start | bytes 393224 | tf_op jit(solution)/shard_map/ppermute | solution.py:1221
  (48 other events, 193.1 us)

commit v4 on v3

--- a/solution.py
+++ b/solution.py
@@ -140,43 +140,71 @@
     visits(info, segments, body)
 
 
-def conv_rows(padded, kernel, out, blocks, row_block, taps, flip):
+def conv_rows(padded, kernel, out, steps_ref, sums, blocks, taps, flip):
     half = (taps - 1) // 2
-    steps = (padded.shape[1] - 2 * GAP) // row_block
+    rows = padded.shape[1]
+    pairs = (rows - 2 * GAP) // (4 * GAP)
+    order = [taps - 1 - j if flip else j for j in range(taps)]
+    for c in range(blocks):
+        steps_ref[c, 0 : rows - GAP, :] = padded[c, 0 : rows - GAP, :] - padded[c, GAP:rows, :]
+    for j in range(GAP):
+        total = kernel[order[j] : order[j] + 1, :]
+        if j + GAP < taps:
+            total = total + kernel[order[j + GAP] : order[j + GAP] + 1, :]
+        sums[j : j + 1, :] = total
 
     def body(step, _):
-        c = step // steps
-        base = (step % steps) * row_block + GAP
+        c = step // 2
+        base = GAP + lax.rem(step, 2) * (pairs * 2 * GAP)
         lanes = pl.ds(pl.multiple_of(c * CHAN, CHAN), CHAN)
-        total = jnp.zeros((row_block, CHAN), F32)
-        for j in range(taps):
-            shift = half - j if flip else j - half
-            total += kernel[pl.ds(j, 1), lanes] * padded[c, pl.ds(base + shift, row_block), :]
-        out[c, pl.ds(pl.multiple_of(base, TILE), row_block), :] = total
+        for w in range(pairs):
+            start = base + 2 * GAP * w
+            first_part = second = third = jnp.zeros((GAP, CHAN), F32)
+            for j in range(GAP):
+                row = start + j - half
+                first_part += kernel[pl.ds(order[j], 1), lanes] * steps_ref[c, pl.ds(row, GAP), :]
+                second += sums[pl.ds(j, 1), lanes] * padded[c, pl.ds(row + GAP, GAP), :]
+                if j + GAP < taps:
+                    third += (
+                        kernel[pl.ds(order[j + GAP], 1), lanes]
+                        * steps_ref[c, pl.ds(row + GAP, GAP), :]
+                    )
+            start = pl.multiple_of(start, TILE)
+            out[c, pl.ds(start, GAP), :] = first_part + second
+            out[c, pl.ds(start + GAP, GAP), :] = second - third
         return 0
 
-    lax.fori_loop(0, blocks * steps, body, 0)
-
-
-def conv_taps(padded_grad, padded, out, blocks, row_block, taps):
+    lax.fori_loop(0, blocks * 2, body, 0)
+
+
+def conv_taps(padded_grad, padded, steps_ref, out, blocks, taps):
     half = (taps - 1) // 2
-    steps = (padded.shape[1] - 2 * GAP) // row_block
-    tiles = row_block // TILE
+    rows = padded.shape[1]
+    pairs = (rows - 2 * GAP) // (2 * GAP)
+
+    def fold(value):
+        return value[:TILE] + value[TILE:]
 
     def block(c, _):
         lanes = pl.ds(pl.multiple_of(c * CHAN, CHAN), CHAN)
+        zero = jnp.zeros((TILE, CHAN), F32)
 
         def body(step, sums):
-            base = pl.multiple_of(step * row_block + GAP, TILE)
-            grad = padded_grad[c, pl.ds(base, row_block), :]
-            new = []
-            for j in range(taps):
-                term = grad * padded[c, pl.ds(base + j - half, row_block), :]
-                new.append(sums[j] + jnp.sum(term.reshape(tiles, TILE, CHAN), axis=0))
+            start = pl.multiple_of(step * 2 * GAP + GAP, TILE)
+            lower = padded_grad[c, pl.ds(start, GAP), :]
+            upper = padded_grad[c, pl.ds(start + GAP, GAP), :]
+            both = lower + upper
+            new = list(sums)
+            for j in range(GAP):
+                row = start + j - half
+                shared = fold(both * padded[c, pl.ds(row + GAP, GAP), :])
+                new[j] = new[j] + (fold(lower * steps_ref[c, pl.ds(row, GAP), :]) + shared)
+                if j + GAP < taps:
+                    rest = fold(upper * steps_ref[c, pl.ds(row + GAP, GAP), :])
+                    new[j + GAP] = new[j + GAP] + (shared - rest)
             return tuple(new)
 
-        zero = jnp.zeros((TILE, CHAN), F32)
-        sums = lax.fori_loop(0, steps, body, (zero,) * taps)
+        sums = lax.fori_loop(0, pairs, body, (zero,) * taps)
         for j in range(taps):
             out[pl.ds(j, 1), lanes] = row_sum(sums[j])
         return 0
@@ -303,7 +331,7 @@
     info, x_ref, heads_gain, segs_col, segs_row, w_heads, w_heads_two, w_mix, w_mix_two,
     gain, gate_gain, taps_ref, w_in, w_in_two, w_out, w_out_two, attended, packed, mixed,
     gated, before_out, normal_out, inverse_out, part_out, product,
-    low, act, padded, conv, *, segments, row_block, taps,
+    low, act, padded, conv, steps_ref, sums, *, segments, taps,
 ):
     j = pl.program_id(0)
     thirds = WIDTH * 3
@@ -333,7 +361,7 @@
         act[...] = normal * gate_gain[...]
         blocks = thirds // CHAN
         spread(act, padded, info, segments, blocks)
-        conv_rows(padded, taps_ref, conv, blocks, row_block, taps, False)
+        conv_rows(padded, taps_ref, conv, steps_ref, sums, blocks, taps, False)
         unspread(conv, part_out, info, segments, blocks)
 
     @pl.when(j >= 3)
@@ -383,14 +411,17 @@
 
 def gated_conv(
     info, part_grad, normal_ref, inverse_ref, gate_gain, taps_ref,
-    gate_gain_grad, taps_grad, padded, padded_grad, conv, work, segments, row_block, taps,
+    gate_gain_grad, taps_grad, padded, padded_grad, conv, work, steps_ref, sums, segments, taps,
 ):
     blocks = 3 * WIDTH // CHAN
     spread(part_grad, padded_grad, info, segments, blocks)
     work[...] = normal_ref[...] * gate_gain[...]
     spread(work, padded, info, segments, blocks)
-    conv_taps(padded_grad, padded, taps_grad, blocks, row_block, taps)
-    conv_rows(padded_grad, taps_ref, conv, blocks, row_block, taps, True)
+    rows = padded.shape[1]
+    for c in range(blocks):
+        steps_ref[c, 0 : rows - GAP, :] = padded[c, 0 : rows - GAP, :] - padded[c, GAP:rows, :]
+    conv_taps(padded_grad, padded, steps_ref, taps_grad, blocks, taps)
+    conv_rows(padded_grad, taps_ref, conv, steps_ref, sums, blocks, taps, True)
     unspread(conv, work, info, segments, blocks)
     upstream = work[...]
     normal = normal_ref[...]
@@ -402,7 +433,7 @@
     info, part_grad, normal_ref, inverse_ref, gate_gain, taps_ref, x_ref, gain, before, total_in,
     w_in, w_in_two,
     stream, gain_grad, gate_gain_grad, taps_grad, send, keep,
-    low, total, padded, padded_grad, conv, work, *, segments, row_block, taps,
+    low, total, padded, padded_grad, conv, work, steps_ref, sums, *, segments, taps,
 ):
     j = pl.program_id(0)
     mine = info[0]
@@ -411,7 +442,7 @@
     def _():
         gated_conv(
             info, part_grad, normal_ref, inverse_ref, gate_gain, taps_ref, gate_gain_grad,
-            taps_grad, padded, padded_grad, conv, work, segments, row_block, taps,
+            taps_grad, padded, padded_grad, conv, work, steps_ref, sums, segments, taps,
         )
         normal, _ = normalize(x_ref[...])
         low[...] = (normal * gain[...]).astype(LOW)
@@ -431,8 +462,8 @@
         stream[...] = normalize_back(total[...], gain[...], normal, inverse)
 
 
-def conv_add(padded, conv, taps_ref, blocks, row_block, taps, flip):
-    conv_rows(padded, taps_ref, conv, blocks, row_block, taps, flip)
+def conv_add(padded, conv, taps_ref, steps_ref, sums, blocks, taps, flip):
+    conv_rows(padded, taps_ref, conv, steps_ref, sums, blocks, taps, flip)
     for c in range(blocks):
         conv[c] += padded[c]
 
@@ -461,7 +492,7 @@
     encoded, stream, gain_grad, final_gain_grad, stat, attended_grad, gated_grad, taps_grad,
     send, keep, merge_send, merge_keep,
     low, before, part_grad, stream_grad, total, middle, joined, joined_low, padded, padded_grad,
-    conv, *, segments, row_block, taps,
+    conv, steps_ref, sums, *, segments, taps,
 ):
     step = pl.program_id(0)
     h = jnp.where(step < 4, step, 7 - step)
@@ -474,7 +505,7 @@
         joined[:, :WIDTH] = attended[...]
         joined[:, WIDTH:] = gated[...]
         spread(joined, padded, info, segments, blocks)
-        conv_add(padded, conv, taps_ref, blocks, row_block, taps, False)
+        conv_add(padded, conv, taps_ref, steps_ref, sums, blocks, taps, False)
         unspread(conv, joined, info, segments, blocks)
         joined_low[...] = joined[...].astype(LOW)
         part = dot(joined_low[...], join_rows(weight[...], weight_two[...], info[0]))
@@ -530,8 +561,8 @@
         store_halves(dot_tn(joined_low[...], grad_low), merge_send, merge_keep, info[0], 32, 0)
         joined[...] = dot_nt(grad_low, join_rows(weight[...], weight_two[...], info[0]))
         spread(joined, padded_grad, info, segments, blocks)
-        conv_taps(padded_grad, padded, taps_grad, blocks, row_block, taps)
-        conv_add(padded_grad, conv, taps_ref, blocks, row_block, taps, True)
+        conv_taps(padded_grad, padded, steps_ref, taps_grad, blocks, taps)
+        conv_add(padded_grad, conv, taps_ref, steps_ref, sums, blocks, taps, True)
         unspread(conv, joined, info, segments, blocks)
         attended_grad[...] = joined[:, :WIDTH]
         gated_grad[...] = joined[:, WIDTH:]
@@ -588,7 +619,7 @@
     return pl.BlockSpec(shape, lambda *_: (0,) * len(shape))
 
 
-def call(kernel, grid, inputs, outputs, scratch, info, flops=0, after=()):
+def call(kernel, grid, inputs, outputs, scratch, info, flops=0, after=(), room=56):
     in_specs = [
         whole(array.shape) if block is None else pl.BlockSpec(block, index)
         for array, block, index in inputs
@@ -618,7 +649,7 @@
         ),
         out_shape=shapes,
         name=name,
-        compiler_params=pltpu.CompilerParams(vmem_limit_bytes=56 * 1024 * 1024),
+        compiler_params=pltpu.CompilerParams(vmem_limit_bytes=room * 1024 * 1024),
         cost_estimate=pl.CostEstimate(flops=flops, bytes_accessed=moved, transcendentals=0),
     )(info, *after, *arrays)
 
@@ -674,10 +705,9 @@
         self.stream = ((self.tokens, WIDTH), F32)
         self.low = pltpu.VMEM((self.tokens, WIDTH), LOW)
         self.wide = pltpu.VMEM((self.tokens, WIDTH), F32)
-        self.spread_rows = self.tokens + GAP * (self.segments + 1)
-        self.conv = dict(
-            segments=self.segments, row_block=(self.spread_rows - 2 * GAP) // 4, taps=taps
-        )
+        rows = self.tokens + GAP * (self.segments - 1)
+        self.spread_rows = -(-rows // (4 * GAP)) * 4 * GAP + 2 * GAP
+        self.conv = dict(segments=self.segments, taps=taps)
         self.stat = ((8, WIDTH), F32)
         self.vector = ((1, WIDTH), F32)
         self.flop = 2 * self.tokens * WIDTH * WIDTH
@@ -734,7 +764,9 @@
             + plain(
                 self.tall(3 * WIDTH), self.tall(1), self.tall(3 * WIDTH), self.tall(3 * WIDTH, LOW)
             ),
-            [self.low, pltpu.VMEM((self.tokens, 3 * WIDTH), F32)] + [self.padded(3 * WIDTH)] * 2,
+            [self.low, pltpu.VMEM((self.tokens, 3 * WIDTH), F32)]
+            + [self.padded(3 * WIDTH)] * 3
+            + [pltpu.VMEM((GAP, 3 * WIDTH), F32)],
             self.info,
             52 * self.flop,
             after,
@@ -766,7 +798,8 @@
             [
                 self.low, pltpu.VMEM((4, self.tokens, WIDTH), F32), self.low, self.wide, self.wide,
                 self.wide, pltpu.VMEM((self.tokens, 2 * WIDTH), F32),
-                pltpu.VMEM((self.tokens, 2 * WIDTH), LOW), padded, padded, padded,
+                pltpu.VMEM((self.tokens, 2 * WIDTH), LOW), padded, padded, padded, padded,
+                pltpu.VMEM((GAP, 2 * WIDTH), F32),
             ],
             self.info,
             80 * self.flop,
@@ -825,7 +858,8 @@
             + halves(48),
             [
                 self.low, self.wide, padded, padded, padded,
-                pltpu.VMEM((self.tokens, 3 * WIDTH), F32),
+                pltpu.VMEM((self.tokens, 3 * WIDTH), F32), padded,
+                pltpu.VMEM((GAP, 3 * WIDTH), F32),
             ],
             self.info,
             48 * self.flop,
@@ -937,11 +971,11 @@
     )
 
 
-def place(kernel, pieces, rows, spots, after=()):
+def place(kernel, pieces, rows, info, after=()):
     skipped = len(after)
 
-    def body(info, *refs):
-        kernel(info, *refs[skipped:])
+    def body(info_ref, *refs):
+        kernel(info_ref, *refs[skipped:])
 
     anywhere = pl.BlockSpec(memory_space=pl.ANY)
     return pl.pallas_call(
@@ -949,16 +983,17 @@
         grid_spec=pltpu.PrefetchScalarGridSpec(
             num_scalar_prefetch=1,
             grid=(1,),
-            in_specs=[anywhere] * skipped + [whole(piece.shape) for piece in pieces],
+            in_specs=[anywhere] * skipped + [pl.BlockSpec(memory_space=pltpu.VMEM)] * 4,
             out_specs=anywhere,
             scratch_shapes=[pltpu.SemaphoreType.DMA((4, 4))],
         ),
         out_shape=jax.ShapeDtypeStruct((4, 4, rows, WIDTH), LOW),
         name=kernel.__name__,
+        compiler_params=pltpu.CompilerParams(vmem_limit_bytes=16 * 1024 * 1024),
         cost_estimate=pl.CostEstimate(
             flops=0, bytes_accessed=32 * rows * WIDTH * 2, transcendentals=0
         ),
-    )(spots, *after, *pieces)
+    )(info, *after, *pieces)
 
 
 def line_sends(array):
@@ -1181,6 +1216,7 @@
         [],
         info,
         after=after,
+        room=24,
     )
     grouped = []
     for _, given in counts:

time: 368 us -> 352 us (0.957)
  Pallas kernels: 203 us -> 171 us
  waiting for transfers between devices: 77.5 us -> 88.7 us
    pallas_call x21, Pallas kernels: 193 us -> 164 us  [call(): pl.pallas_call(body, grid_spec=pltpu.PrefetchScalarGridSpec(num_scalar_pr...]
    ppermute x12, waiting for transfers between devices: 3.99 us -> 9.52 us  [line_swap(): lax.ppermute(array, 'z', ring(4, d))]
    all_to_all x7, waiting for transfers between devices: 31.7 us -> 36.3 us  [plane_exchange(): return lax.all_to_all(array, ('x', 'y'), 0, 0, tiled=True)]
    unnamed x68 -> x108, local copies, waits for them, and re-layouts: 16.8 us -> 21 us
    pallas_call x3, Pallas kernels: 10.7 us -> 6.77 us  [place(): pl.pallas_call(body, grid_spec=pltpu.PrefetchScalarGridSpec(num_scalar_pr...]
  transfers between devices with their start and end apart: 38 -> 38, of which waited for: 18 -> 20; matrix products, arithmetic and copies ran while one was open for 1% -> 1% of each run, Pallas kernels for 40% -> 35%
where the time goes in v4:
time: 352 us; the launch traced here: 350 us
  Pallas kernels  171 us (49%)
  waiting for transfers between devices  88.7 us (25%)
  starting transfers between devices  63.4 us (18%)
  local copies, waits for them, and re-layouts  24.5 us (7%)
    pallas_call x21, Pallas kernels, call(): pl.pallas_call(body, grid_spec=pltpu.PrefetchScalarGridSpec(num_scalar_pr...  164 us
    all_to_all x7, waiting for transfers between devices, plane_exchange(): return lax.all_to_all(array, ('x', 'y'), 0, 0, tiled=True)  36.3 us
    all_to_all x7, starting transfers between devices, plane_exchange(): return lax.all_to_all(array, ('x', 'y'), 0, 0, tiled=True)  28.3 us
    ppermute x9, waiting for transfers between devices, line_sends(): return [lax.ppermute(array, 'z', ring(4, d)) for d in (1, 2, 3)]  27.1 us
    unnamed x108, local copies, waits for them, and re-layouts  21 us
    ppermute x12, starting transfers between devices, line_swap(): lax.ppermute(array, 'z', ring(4, d))  18.3 us
    ppermute x10, waiting for transfers between devices, core_swap(): return lax.ppermute(array, 'k', ring(2, 1))  15.8 us
    ppermute x9, starting transfers between devices, line_sends(): return [lax.ppermute(array, 'z', ring(4, d)) for d in (1, 2, 3)]  15.5 us
  transfers between devices with their start and end apart: 38, of which 20 were waited for; matrix products, arithmetic and copies ran while one was open for 1% of the time, Pallas kernels for 35%

profile of v4, /device:TPU:0, one launch (start us, length us, event | category | flops | bytes accessed | tf_op | source)
XLA Modules:
  0.0 350.4 jit_solution(11920994764573177462)
XLA Ops:
  3.9 5.0 %collective-permute-start.2 = (bf16[144,512]{1,0:T(8,128)(2,1)}, bf16[144,512]{1,0:T(8,128)(2,1)S(1)}, u32[]{:S(2)}, u32[]{:S(2)}) collective-permute-start(bf16[144,512]{1,0:T(8,128)(2,1)} %get-tuple-element.120.refs_0_), channel_id=1, source_target_pairs={{0,6},{2,0},{4,2},{6,4},{1,7},{3,1},{5,3},{7,5},{8,14},{10,8},{12,... | collective-permute-start | bytes 442376 | tf_op jit(solution)/shard_map/ppermute | solution.py:1000
  13.5 8.1 %collective-permute-done.1.refs_2_ = bf16[144,512]{1,0:T(8,128)(2,1)S(1)} collective-permute-done((bf16[144,512]{1,0:T(8,128)(2,1)}, bf16[144,512]{1,0:T(8,128)(2,1)S(1)}, u32[]{:S(2)}, u32[]{:S(2)}) %collective-permute-start.1) | collective-permute-done | bytes 147488 | tf_op jit(solution)/shard_map/ppermute | solution.py:1000
  24.7 3.9 %all-to-all-start = ((bf16[4,4,144,512]{3,2,1,0:T(8,128)(2,1)}), bf16[4,4,144,512]{3,2,1,0:T(8,128)(2,1)S(1)}, u32[]{:S(2)}, u32[]{:S(2)}) async-start(bf16[4,4,144,512]{3,2,1,0:T(8,128)(2,1)} %place_line_kernel.3), calls=%async_computation | async-start | bytes 4718592 | tf_op jit(solution)/shard_map/all_to_all | solution.py:1004
  35.6 14.0 %collective-permute-done.4.refs_2_ = bf16[208,512]{1,0:T(8,128)(2,1)S(1)} collective-permute-done((bf16[208,512]{1,0:T(8,128)(2,1)S(1)}, bf16[208,512]{1,0:T(8,128)(2,1)S(1)}, u32[]{:S(2)}, u32[]{:S(2)}) %collective-permute-start.4) | collective-permute-done | bytes 213024 | tf_op jit(solution)/shard_map/ppermute | solution.py:1000
  52.1 3.9 %all-to-all-done.refs_0_.refs_3_.refs_5_.refs_8_ = bf16[4,4,144,512]{3,2,1,0:T(8,128)(2,1)S(1)} async-done(((bf16[4,4,144,512]{3,2,1,0:T(8,128)(2,1)}), bf16[4,4,144,512]{3,2,1,0:T(8,128)(2,1)S(1)}, u32[]{:S(2)}, u32[]{:S(2)}) %all-to-all-start) | async-done | bytes 2359328 | tf_op jit(solution)/shard_map/all_to_all | solution.py:1004
  57.4 4.7 %all-to-all-start.1 = ((bf16[4,4,208,512]{3,2,1,0:T(8,128)(2,1)}), bf16[4,4,208,512]{3,2,1,0:T(8,128)(2,1)}, u32[]{:S(2)}, u32[]{:S(2)}) async-start(bf16[4,4,208,512]{3,2,1,0:T(8,128)(2,1)} %place_line_kernel.4), calls=%async_computation.1 | async-start | bytes 6815744 | tf_op jit(solution)/shard_map/all_to_all | solution.py:1004
  71.9 8.1 %front_forward_kernel.1 = (f32[384,512]{1,0:T(8,128)}, f32[384,2048]{1,0:T(8,128)}, f32[8,512]{1,0:T(8,128)}) custom-call(s32[16]{0:T(128)} %copy-done.27, bf16[384,512]{1,0:T(8,128)(2,1)} %refs_6_.3, f32[1,512]{1,0:T(1,128)} %get-tuple-element.224.refs_1_.refs_7_, f32[384,1]{1,0:T(8,128)} %compare_convert_fusion.refs_2_.refs_8_, ...), custom_call_target="tpu_custom_call" | custom-call | flops 1610612736 | bytes 13782528 | tf_op jit(solution)/shard_map/front_forward_kernel/pallas_call | solution.py:641
  83.0 18.3 %all-to-all-done.1.refs_4_.refs_6_.refs_11_.refs_13_.refs_8_.refs_10_.refs_17_.refs_19_ = bf16[4,4,208,512]{3,2,1,0:T(8,128)(2,1)} async-done(((bf16[4,4,208,512]{3,2,1,0:T(8,128)(2,1)}), bf16[4,4,208,512]{3,2,1,0:T(8,128)(2,1)}, u32[]{:S(2)}, u32[]{:S(2)}) %all-to-all-start.1) | async-done | bytes 3407904 | tf_op jit(solution)/shard_map/all_to_all | solution.py:1004
  101.3 4.7 %all-to-all-start.2 = ((bf16[4,4,160,512]{3,2,1,0:T(8,128)(2,1)}), bf16[4,4,160,512]{3,2,1,0:T(8,128)(2,1)}, u32[]{:S(2)}, u32[]{:S(2)}) async-start(bf16[4,4,160,512]{3,2,1,0:T(8,128)(2,1)} %place_line_kernel.5), calls=%async_computation.2 | async-start | bytes 5242880 | tf_op jit(solution)/shard_map/all_to_all | solution.py:1004
  109.3 26.2 %branches_forward_kernel.1 = (f32[384,512]{1,0:T(8,128)}, bf16[384,1536]{1,0:T(8,128)(2,1)}, bf16[384,512]{1,0:T(8,128)(2,1)}, f32[384,512]{1,0:T(8,128)}, f32[3...) custom-call(s32[16]{0:T(128)} %copy-done.27, ...), custom_call_target="tpu_custom_call" | custom-call | flops 10468982784 | bytes 30541312 | tf_op jit(solution)/shard_map/branches_forward_kernel/pallas_call | solution.py:641
  137.4 5.1 %collective-permute-done.11.refs_5_.refs_11_.refs_13_ = bf16[4,4,160,512]{3,2,1,0:T(8,128)(2,1)S(1)} collective-permute-done((bf16[4,4,160,512]{3,2,1,0:T(8,128)(2,1)}, bf16[4,4,160,512]{3,2,1,0:T(8,128)(2,1)S(1)}, u32[]{:S(2)}, u32[]{:S(2)}) %collective-permute-start.11) | collective-permute-done | bytes 2621472 | tf_op jit(solution)/shard_map/ppermute | solution.py:1008
  144.0 36.5 %merge_rear_kernel.1 = (bf16[384,512]{1,0:T(8,128)(2,1)}, f32[384,512]{1,0:T(8,128)}, f32[1,512]{1,0:T(1,128)}, f32[1,512]{1,0:T(1,128)}, f32[8,512]{1,0:T(8,128...) custom-call(s32[16]{0:T(128)} %copy-done.27, ...), custom_call_target="tpu_custom_call" | custom-call | flops 16106127360 | bytes 24924160 | tf_op jit(solution)/shard_map/merge_rear_kernel/pallas_call | solution.py:641
  180.7 4.2 %collective-permute-done.12.refs_1_ = bf16[2,8,128,512]{3,2,1,0:T(8,128)(2,1)S(1)} collective-permute-done((bf16[2,8,128,512]{3,2,1,0:T(8,128)(2,1)}, bf16[2,8,128,512]{3,2,1,0:T(8,128)(2,1)S(1)}, u32[]{:S(2)}, u32[]{:S(2)}) %collective-permute-start.12) | collective-permute-done | bytes 2097184 | tf_op jit(solution)/shard_map/ppermute | solution.py:1008
  188.6 3.6 %all-to-all-start.3 = ((bf16[4,4,128,512]{3,2,1,0:T(8,128)(2,1)}), bf16[4,4,128,512]{3,2,1,0:T(8,128)(2,1)S(1)}, u32[]{:S(2)}, u32[]{:S(2)}) async-start(bf16[4,4,128,512]{3,2,1,0:T(8,128)(2,1)} %tasks_kernel.12.refs_0_), calls=%async_computation.3 | async-start | bytes 4194304 | tf_op jit(solution)/shard_map/all_to_all | solution.py:1004
  192.2 23.9 %branches_backward_kernel.1 = (f32[384,512]{1,0:T(8,128)}, f32[1,512]{1,0:T(1,128)}, f32[384,1536]{1,0:T(8,128)}, f32[384,512]{1,0:T(8,128)}, bf16[2,8,160,512]{...) custom-call(s32[16]{0:T(128)} %copy-done.27, bf16[4,4,128,512]{3,2,1,0:T(8,128)(2,1)} %tasks_kernel.12.refs_0_, ...), custom_call_target="tpu_custom_call" | custom-call | flops 8053063680 | bytes 25954304 | tf_op jit(solution)/shard_map/branches_backward_kernel/pallas_call | solution.py:641
  226.7 3.7 %all-to-all-start.4 = ((bf16[4,4,192,512]{3,2,1,0:T(8,128)(2,1)}), bf16[4,4,192,512]{3,2,1,0:T(8,128)(2,1)S(1)}, u32[]{:S(2)}, u32[]{:S(2)}) async-start(bf16[4,4,192,512]{3,2,1,0:T(8,128)(2,1)} %tasks_kernel.14.refs_0_), calls=%async_computation.4 | async-start | bytes 6291456 | tf_op jit(solution)/shard_map/all_to_all | solution.py:1004
  236.0 26.1 %gated_gate_kernel.1 = (f32[384,512]{1,0:T(8,128)}, f32[1,512]{1,0:T(1,128)}, f32[1,1536]{1,0:T(1,128)}, f32[32,1536]{1,0:T(8,128)}, bf16[2,8,48,512]{3,2,1,0:T(8,128)(2,1)}, /*index=5*/bf16[2,8,48,512]{3,2,1,0:T(8,128)(2,1)}) custom-call(s32[16]{0:T(128)} %copy-done.27, bf16[4,4,192,512]{3,2,1,0:T(8,128)(2,1)} %tasks_kernel.14.refs_0_, ...), custom_call_target="tpu_custom_call" | custom-call | flops 9663676416 | bytes 19341312 | tf_op jit(solution)/shard_map/gated_gate_kernel/pallas_call | solution.py:641
  267.9 9.0 %front_hidden_kernel.1 = (f32[384,512]{1,0:T(8,128)}, bf16[384,2048]{1,0:T(8,128)(2,1)}, bf16[2,8,64,512]{3,2,1,0:T(8,128)(2,1)}, bf16[2,8,64,512]{3,2,1,0:T(8,128)(2,1)}) custom-call(s32[16]{0:T(128)} %copy-done.27, bf16[2,8,16,512]{3,2,1,0:T(8,128)(2,1)} %copy-done.26, f32[384,512]{1,0:T(8,128)} %get-tuple-element.171.refs_1_, ...), custom_call_target="tpu_custom_call" | custom-call | flops 2415919104 | bytes 14680064 | tf_op jit(solution)/shard_map/front_hidden_kernel/pallas_call | solution.py:641
  287.3 4.1 %all-to-all-start.5 = ((bf16[4,4,128,512]{3,2,1,0:T(8,128)(2,1)}), bf16[4,4,128,512]{3,2,1,0:T(8,128)(2,1)S(1)}, u32[]{:S(2)}, u32[]{:S(2)}) async-start(bf16[4,4,128,512]{3,2,1,0:T(8,128)(2,1)} %tasks_kernel.17.refs_0_), calls=%async_computation.5 | async-start | bytes 4194304 | tf_op jit(solution)/shard_map/all_to_all | solution.py:1004
  291.4 6.2 %collective-permute-done.22.refs_2_.refs_7_ = bf16[192,512]{1,0:T(8,128)(2,1)S(1)} collective-permute-done((bf16[192,512]{1,0:T(8,128)(2,1)}, bf16[192,512]{1,0:T(8,128)(2,1)S(1)}, u32[]{:S(2)}, u32[]{:S(2)}) %collective-permute-start.22) | collective-permute-done | bytes 196640 | tf_op jit(solution)/shard_map/ppermute | solution.py:1257
  298.4 9.0 %front_input_kernel.1 = (bf16[384,512]{1,0:T(8,128)(2,1)}, bf16[2,8,80,512]{3,2,1,0:T(8,128)(2,1)}, bf16[2,8,80,512]{3,2,1,0:T(8,128)(2,1)}) custom-call(s32[16]{0:T(128)} %copy-done.27, bf16[4,4,128,512]{3,2,1,0:T(8,128)(2,1)} %tasks_kernel.17.refs_0_, bf16[192,512]{1,0:T(8,128)(2,1)} %copy-done.13, bf16[192,512]{1,0:T(8,128)(2,1)} %copy-done.15, ...), custom_call_target="tpu_custom_call" | custom-call | flops 2415919104 | bytes 10487808 | tf_op jit(solution)/shard_map/front_input_kernel/pallas_call | solution.py:641
  307.3 3.2 collective-permute-done.24.refs_1_
  316.3 3.5 %all-to-all-start.6 = ((bf16[4,4,80,512]{3,2,1,0:T(8,128)(2,1)}), bf16[4,4,80,512]{3,2,1,0:T(8,128)(2,1)S(1)}, u32[]{:S(2)}, u32[]{:S(2)}) async-start(bf16[4,4,80,512]{3,2,1,0:T(8,128)(2,1)} %tasks_kernel.18.refs_0_), calls=%async_computation.6 | async-start | bytes 2621440 | tf_op jit(solution)/shard_map/all_to_all | solution.py:1004
  328.3 8.1 %all-to-all-done.6.refs_2_ = bf16[4,4,80,512]{3,2,1,0:T(8,128)(2,1)S(1)} async-done(((bf16[4,4,80,512]{3,2,1,0:T(8,128)(2,1)}), bf16[4,4,80,512]{3,2,1,0:T(8,128)(2,1)S(1)}, u32[]{:S(2)}, u32[]{:S(2)}) %all-to-all-start.6) | async-done | bytes 1310752 | tf_op jit(solution)/shard_map/all_to_all | solution.py:1004
  (192 shorter events, 106.0 us)
Async XLA Ops:
  8.9 12.7 %collective-permute-start.1 = (bf16[144,512]{1,0:T(8,128)(2,1)}, bf16[144,512]{1,0:T(8,128)(2,1)S(1)}, u32[]{:S(2)}, u32[]{:S(2)}) collective-permute-start(bf16[144,512]{1,0:T(8,128)(2,1)} %get-tuple-element.120.refs_0_), channel_id=1, source_target_pairs={{0,4},{2,6},{4,0},{6,2},{1,5},{3,7},{5,1},{7,3},{8,12},{10,14},{12... | collective-permute-start | bytes 442376 | tf_op jit(solution)/shard_map/ppermute | solution.py:1000
  8.9 12.7 %collective-permute-start = (bf16[144,512]{1,0:T(8,128)(2,1)}, bf16[144,512]{1,0:T(8,128)(2,1)S(1)}, u32[]{:S(2)}, u32[]{:S(2)}) collective-permute-start(bf16[144,512]{1,0:T(8,128)(2,1)} %get-tuple-element.120.refs_0_), channel_id=1, source_target_pairs={{0,2},{2,4},{4,6},{6,0},{1,3},{3,5},{5,7},{7,1},{8,10},{10,12},{12... | collective-permute-start | bytes 442376 | tf_op jit(solution)/shard_map/ppermute | solution.py:1000
  24.7 31.3 %all-to-all-start = ((bf16[4,4,144,512]{3,2,1,0:T(8,128)(2,1)}), bf16[4,4,144,512]{3,2,1,0:T(8,128)(2,1)S(1)}, u32[]{:S(2)}, u32[]{:S(2)}) async-start(bf16[4,4,144,512]{3,2,1,0:T(8,128)(2,1)} %place_line_kernel.3), calls=%async_computation | async-start | bytes 4718592 | tf_op jit(solution)/shard_map/all_to_all | solution.py:1004
  29.9 19.7 %collective-permute-start.4 = (bf16[208,512]{1,0:T(8,128)(2,1)S(1)}, bf16[208,512]{1,0:T(8,128)(2,1)S(1)}, u32[]{:S(2)}, u32[]{:S(2)}) collective-permute-start(bf16[208,512]{1,0:T(8,128)(2,1)S(1)} %copy-done.34), channel_id=1, source_target_pairs={{0,4},{2,6},{4,0},{6,2},{1,5},{3,7},{5,1},{7,3},{8,12},{10,14},{12... | collective-permute-start | bytes 638984 | tf_op jit(solution)/shard_map/ppermute | solution.py:1000
  31.4 18.3 %collective-permute-start.3 = (bf16[208,512]{1,0:T(8,128)(2,1)S(1)}, bf16[208,512]{1,0:T(8,128)(2,1)S(1)}, u32[]{:S(2)}, u32[]{:S(2)}) collective-permute-start(bf16[208,512]{1,0:T(8,128)(2,1)S(1)} %copy-done.34), channel_id=1, source_target_pairs={{0,2},{2,4},{4,6},{6,0},{1,3},{3,5},{5,7},{7,1},{8,10},{10,12},{12... | collective-permute-start | bytes 638984 | tf_op jit(solution)/shard_map/ppermute | solution.py:1000
  56.0 11.7 %collective-permute-start.6 = (bf16[4,4,144,512]{3,2,1,0:T(8,128)(2,1)S(1)}, bf16[4,4,144,512]{3,2,1,0:T(8,128)(2,1)}, u32[]{:S(2)}, u32[]{:S(2)}) collective-permute-start(bf16[4,4,144,512]{3,2,1,0:T(8,128)(2,1)S(1)} %all-to-all-done.refs_0_.refs_3_.refs_5_.refs_8_), channel_id=1, source_target_pairs={{0,8},{8,0},{1,9},{9,1},{2,10},{10,2},{3,11},{11,3},{4,12},{12,4},... | collective-permute-start | bytes 7077896 | tf_op jit(solution)/shard_map/ppermute | solution.py:1008
  57.4 43.9 %all-to-all-start.1 = ((bf16[4,4,208,512]{3,2,1,0:T(8,128)(2,1)}), bf16[4,4,208,512]{3,2,1,0:T(8,128)(2,1)}, u32[]{:S(2)}, u32[]{:S(2)}) async-start(bf16[4,4,208,512]{3,2,1,0:T(8,128)(2,1)} %place_line_kernel.4), calls=%async_computation.1 | async-start | bytes 6815744 | tf_op jit(solution)/shard_map/all_to_all | solution.py:1004
  63.0 17.0 %collective-permute-start.9 = (bf16[160,512]{1,0:T(8,128)(2,1)S(1)}, bf16[160,512]{1,0:T(8,128)(2,1)S(1)}, u32[]{:S(2)}, u32[]{:S(2)}) collective-permute-start(bf16[160,512]{1,0:T(8,128)(2,1)S(1)} %copy-done.36), channel_id=1, source_target_pairs={{0,6},{2,0},{4,2},{6,4},{1,7},{3,1},{5,3},{7,5},{8,14},{10,8},{12,... | collective-permute-start | bytes 491528 | tf_op jit(solution)/shard_map/ppermute | solution.py:1000
  63.4 16.7 %collective-permute-start.8 = (bf16[160,512]{1,0:T(8,128)(2,1)S(1)}, bf16[160,512]{1,0:T(8,128)(2,1)S(1)}, u32[]{:S(2)}, u32[]{:S(2)}) collective-permute-start(bf16[160,512]{1,0:T(8,128)(2,1)S(1)} %copy-done.36), channel_id=1, source_target_pairs={{0,4},{2,6},{4,0},{6,2},{1,5},{3,7},{5,1},{7,3},{8,12},{10,14},{12... | collective-permute-start | bytes 491528 | tf_op jit(solution)/shard_map/ppermute | solution.py:1000
  65.6 14.4 %collective-permute-start.7 = (bf16[160,512]{1,0:T(8,128)(2,1)S(1)}, bf16[160,512]{1,0:T(8,128)(2,1)S(1)}, u32[]{:S(2)}, u32[]{:S(2)}) collective-permute-start(bf16[160,512]{1,0:T(8,128)(2,1)S(1)} %copy-done.36), channel_id=1, source_target_pairs={{0,2},{2,4},{4,6},{6,0},{1,3},{3,5},{5,7},{7,1},{8,10},{10,12},{12... | collective-permute-start | bytes 491528 | tf_op jit(solution)/shard_map/ppermute | solution.py:1000
  101.3 36.1 %all-to-all-start.2 = ((bf16[4,4,160,512]{3,2,1,0:T(8,128)(2,1)}), bf16[4,4,160,512]{3,2,1,0:T(8,128)(2,1)}, u32[]{:S(2)}, u32[]{:S(2)}) async-start(bf16[4,4,160,512]{3,2,1,0:T(8,128)(2,1)} %place_line_kernel.5), calls=%async_computation.2 | async-start | bytes 5242880 | tf_op jit(solution)/shard_map/all_to_all | solution.py:1004
  188.6 29.0 %all-to-all-start.3 = ((bf16[4,4,128,512]{3,2,1,0:T(8,128)(2,1)}), bf16[4,4,128,512]{3,2,1,0:T(8,128)(2,1)S(1)}, u32[]{:S(2)}, u32[]{:S(2)}) async-start(bf16[4,4,128,512]{3,2,1,0:T(8,128)(2,1)} %tasks_kernel.12.refs_0_), calls=%async_computation.3 | async-start | bytes 4194304 | tf_op jit(solution)/shard_map/all_to_all | solution.py:1004
  226.7 50.2 %all-to-all-start.4 = ((bf16[4,4,192,512]{3,2,1,0:T(8,128)(2,1)}), bf16[4,4,192,512]{3,2,1,0:T(8,128)(2,1)S(1)}, u32[]{:S(2)}, u32[]{:S(2)}) async-start(bf16[4,4,192,512]{3,2,1,0:T(8,128)(2,1)} %tasks_kernel.14.refs_0_), calls=%async_computation.4 | async-start | bytes 6291456 | tf_op jit(solution)/shard_map/all_to_all | solution.py:1004
  230.4 31.7 %collective-permute-start.13 = (bf16[128,512]{1,0:T(8,128)(2,1)}, bf16[128,512]{1,0:T(8,128)(2,1)S(1)}, u32[]{:S(2)}, u32[]{:S(2)}) collective-permute-start(bf16[128,512]{1,0:T(8,128)(2,1)} %get-tuple-element.150), channel_id=1, source_target_pairs={{0,2},{2,4},{4,6},{6,0},{1,3},{3,5},{5,7},{7,1},{8,10},{10,12},{12... | collective-permute-start | bytes 393224 | tf_op jit(solution)/shard_map/ppermute | solution.py:1257
  231.4 30.7 %collective-permute-start.14 = (bf16[128,512]{1,0:T(8,128)(2,1)}, bf16[128,512]{1,0:T(8,128)(2,1)S(1)}, u32[]{:S(2)}, u32[]{:S(2)}) collective-permute-start(bf16[128,512]{1,0:T(8,128)(2,1)} %get-tuple-element.151), channel_id=1, source_target_pairs={{0,4},{2,6},{4,0},{6,2},{1,5},{3,7},{5,1},{7,3},{8,12},{10,14},{12... | collective-permute-start | bytes 393224 | tf_op jit(solution)/shard_map/ppermute | solution.py:1257
  233.1 29.0 %collective-permute-start.15 = (bf16[128,512]{1,0:T(8,128)(2,1)}, bf16[128,512]{1,0:T(8,128)(2,1)S(1)}, u32[]{:S(2)}, u32[]{:S(2)}) collective-permute-start(bf16[128,512]{1,0:T(8,128)(2,1)} %copy-done.49), channel_id=1, source_target_pairs={{0,6},{2,0},{4,2},{6,4},{1,7},{3,1},{5,3},{7,5},{8,14},{10,8},{12,... | collective-permute-start | bytes 393224 | tf_op jit(solution)/shard_map/ppermute | solution.py:1257
  280.3 11.1 %collective-permute-start.21 = (bf16[192,512]{1,0:T(8,128)(2,1)}, bf16[192,512]{1,0:T(8,128)(2,1)S(1)}, u32[]{:S(2)}, u32[]{:S(2)}) collective-permute-start(bf16[192,512]{1,0:T(8,128)(2,1)} %get-tuple-element.184), channel_id=1, source_target_pairs={{0,2},{2,4},{4,6},{6,0},{1,3},{3,5},{5,7},{7,1},{8,10},{10,12},{12... | collective-permute-start | bytes 589832 | tf_op jit(solution)/shard_map/ppermute | solution.py:1257
  280.3 17.3 %collective-permute-start.22 = (bf16[192,512]{1,0:T(8,128)(2,1)}, bf16[192,512]{1,0:T(8,128)(2,1)S(1)}, u32[]{:S(2)}, u32[]{:S(2)}) collective-permute-start(bf16[192,512]{1,0:T(8,128)(2,1)} %get-tuple-element.185), channel_id=1, source_target_pairs={{0,4},{2,6},{4,0},{6,2},{1,5},{3,7},{5,1},{7,3},{8,12},{10,14},{12... | collective-permute-start | bytes 589832 | tf_op jit(solution)/shard_map/ppermute | solution.py:1257
  281.4 16.2 %collective-permute-start.23 = (bf16[192,512]{1,0:T(8,128)(2,1)S(1)}, bf16[192,512]{1,0:T(8,128)(2,1)S(1)}, u32[]{:S(2)}, u32[]{:S(2)}) collective-permute-start(bf16[192,512]{1,0:T(8,128)(2,1)S(1)} %get-tuple-element.186), channel_id=1, source_target_pairs={{0,6},{2,0},{4,2},{6,4},{1,7},{3,1},{5,3},{7,5},{8,14},{10,8},{12,... | collective-permute-start | bytes 589832 | tf_op jit(solution)/shard_map/ppermute | solution.py:1257
  287.3 29.0 %all-to-all-start.5 = ((bf16[4,4,128,512]{3,2,1,0:T(8,128)(2,1)}), bf16[4,4,128,512]{3,2,1,0:T(8,128)(2,1)S(1)}, u32[]{:S(2)}, u32[]{:S(2)}) async-start(bf16[4,4,128,512]{3,2,1,0:T(8,128)(2,1)} %tasks_kernel.17.refs_0_), calls=%async_computation.5 | async-start | bytes 4194304 | tf_op jit(solution)/shard_map/all_to_all | solution.py:1004
  316.3 20.1 %all-to-all-start.6 = ((bf16[4,4,80,512]{3,2,1,0:T(8,128)(2,1)}), bf16[4,4,80,512]{3,2,1,0:T(8,128)(2,1)S(1)}, u32[]{:S(2)}, u32[]{:S(2)}) async-start(bf16[4,4,80,512]{3,2,1,0:T(8,128)(2,1)} %tasks_kernel.18.refs_0_), calls=%async_computation.6 | async-start | bytes 2621440 | tf_op jit(solution)/shard_map/all_to_all | solution.py:1004
  321.5 20.2 %collective-permute-start.25 = (bf16[128,512]{1,0:T(8,128)(2,1)}, bf16[128,512]{1,0:T(8,128)(2,1)S(1)}, u32[]{:S(2)}, u32[]{:S(2)}) collective-permute-start(bf16[128,512]{1,0:T(8,128)(2,1)} %get-tuple-element.196), channel_id=1, source_target_pairs={{0,2},{2,4},{4,6},{6,0},{1,3},{3,5},{5,7},{7,1},{8,10},{10,12},{12... | collective-permute-start | bytes 393224 | tf_op jit(solution)/shard_map/ppermute | solution.py:1257
  323.6 20.2 %collective-permute-start.26 = (bf16[128,512]{1,0:T(8,128)(2,1)}, bf16[128,512]{1,0:T(8,128)(2,1)S(1)}, u32[]{:S(2)}, u32[]{:S(2)}) collective-permute-start(bf16[128,512]{1,0:T(8,128)(2,1)} %get-tuple-element.197), channel_id=1, source_target_pairs={{0,4},{2,6},{4,0},{6,2},{1,5},{3,7},{5,1},{7,3},{8,12},{10,14},{12... | collective-permute-start | bytes 393224 | tf_op jit(solution)/shard_map/ppermute | solution.py:1257
  323.9 19.8 %collective-permute-start.27 = (bf16[128,512]{1,0:T(8,128)(2,1)}, bf16[128,512]{1,0:T(8,128)(2,1)S(1)}, u32[]{:S(2)}, u32[]{:S(2)}) collective-permute-start(bf16[128,512]{1,0:T(8,128)(2,1)} %get-tuple-element.198), channel_id=1, source_target_pairs={{0,6},{2,0},{4,2},{6,4},{1,7},{3,1},{5,3},{7,5},{8,14},{10,8},{12,... | collective-permute-start | bytes 393224 | tf_op jit(solution)/shard_map/ppermute | solution.py:1257
  (68 other events, 605.5 us)
